TPU v7x, 32 devices: a whole 2x2x4 slice. The times are simulated.
32 devices in a mesh: ctx: 4 (over x, core), fsdp: 8 (over z, y).
Axes of the slice: x: 2, y: 2, z: 4, core: 2. Of those that a mesh axis runs over, the one named last changes fastest.
Arguments:
- hidden: bfloat16 [16, 1024, 3, 1024], P('fsdp', 'ctx'), may hold values from -6 to 6
- encoded: bfloat16 [16, 512, 1024], P('fsdp', 'ctx'), may hold values from -6 to 6
- assign: int32 [32], replicated, may hold values from 0 to 31, as said below
- bucket_table: int32 [1055], replicated, may hold values from 0 to 31
- w_query: bfloat16 [1024, 1024], P('fsdp'), may hold values from -0.1875 to 0.1875
- w_key: bfloat16 [1024, 1024], P('fsdp'), may hold values from -0.1875 to 0.1875
- w_value: bfloat16 [1024, 1024], P('fsdp'), may hold values from -0.1875 to 0.1875
- w_rel: bfloat16 [1024, 512], P('fsdp'), may hold values from -0.1875 to 0.1875
- w_out: bfloat16 [1024, 1024], P('fsdp'), may hold values from -0.75 to 0.75
- gain_one: bfloat16 [1024], P('fsdp'), may hold values from 0.25 to 1.75
- shift_one: bfloat16 [1024], P('fsdp'), may hold values from -3 to 3
- c_query: bfloat16 [1024, 1024], P('fsdp'), may hold values from -0.1875 to 0.1875
- c_key: bfloat16 [1024, 1024], P('fsdp'), may hold values from -0.1875 to 0.1875
- c_value: bfloat16 [1024, 1024], P('fsdp'), may hold values from -0.1875 to 0.1875
- c_out: bfloat16 [1024, 1024], P('fsdp'), may hold values from -3 to 3
- gain_two: bfloat16 [1024], P('fsdp'), may hold values from 0.25 to 1.75
- shift_two: bfloat16 [1024], P('fsdp'), may hold values from -3 to 3
- w_inner: bfloat16 [1024, 4096], P('fsdp'), may hold values from -0.1875 to 0.1875
- w_outer: bfloat16 [4096, 1024], P('fsdp'), may hold values from -0.09375 to 0.09375
- gain_three: bfloat16 [1024], P('fsdp'), may hold values from 0.25 to 1.75
- shift_three: bfloat16 [1024], P('fsdp'), may hold values from -3 to 3
- cotangent: bfloat16 [16, 1024, 3, 1024], P('fsdp', 'ctx'), may hold values from -6 to 6
Outputs:
- output: bfloat16 [16, 1024, 3, 1024], P('fsdp', 'ctx')
- grad_hidden: float32 [16, 1024, 3, 1024], P('fsdp', 'ctx')
- grad_encoded: float32 [16, 512, 1024], P('fsdp', 'ctx')
- grad_w_query: float32 [1024, 1024], P('fsdp')
- grad_w_key: float32 [1024, 1024], P('fsdp')
- grad_w_value: float32 [1024, 1024], P('fsdp')
- grad_w_rel: float32 [1024, 512], P('fsdp')
- grad_w_out: float32 [1024, 1024], P('fsdp')
- grad_gain_one: float32 [1024], P('fsdp')
- grad_shift_one: float32 [1024], P('fsdp')
- grad_c_query: float32 [1024, 1024], P('fsdp')
- grad_c_key: float32 [1024, 1024], P('fsdp')
- grad_c_value: float32 [1024, 1024], P('fsdp')
- grad_c_out: float32 [1024, 1024], P('fsdp')
- grad_gain_two: float32 [1024], P('fsdp')
- grad_shift_two: float32 [1024], P('fsdp')
- grad_w_inner: float32 [1024, 4096], P('fsdp')
- grad_w_outer: float32 [4096, 1024], P('fsdp')
- grad_gain_three: float32 [1024], P('fsdp')
- grad_shift_three: float32 [1024], P('fsdp')
Inputs may be any that keep to these rules, and one draw needn't show every extreme that they name: assign holds each of the 32 block numbers once; slots 2 i and 2 i + 1 hold blocks b and 31 - b, in either order.
All inputs are finite; a program needn't handle non-finite values.
Results may differ from a plain program's by a relative error of at most 0.03.
Values may be sent and summed in bfloat16 or wider, within the bound.
No kernel may reach another device: no remote copies, remote signals or barrier semaphores. Data moves between devices by JAX's collectives and lax.ppermute only.
A program may use at most 640 MiB of HBM per device.

v0:
```python
import jax
import jax.numpy as jnp
from jax import lax
from jax.sharding import PartitionSpec as P

HEADS = 16
HEAD_DIM = 64
BUCKETS = 32
BLK = 32


EPSILON = 1e-05
FILLER = -1e30


def layer_norm(values, gain, shift):
    average = jnp.mean(values, axis=-1, keepdims=True)
    centred = values - average
    variance = jnp.mean(centred * centred, axis=-1, keepdims=True)
    return centred * lax.rsqrt(variance + EPSILON) * gain + shift


def exact_gelu(values):
    return jax.nn.gelu(values, approximate=False)


def matmul(left, right):
    return jnp.dot(left, right, preferred_element_type=jnp.float32)


def left_transposed(left, right):
    return lax.dot_general(
        left, right, (((0,), (0,)), ((), ())), preferred_element_type=jnp.float32
    )


def right_transposed(left, right):
    return lax.dot_general(
        left, right, (((1,), (1,)), ((), ())), preferred_element_type=jnp.float32
    )


def fetch_weights(
    w_query,
    w_key,
    w_value,
    w_rel,
    w_out,
    gain_one,
    shift_one,
    c_query,
    c_key,
    c_value,
    c_out,
    gain_two,
    shift_two,
    w_inner,
    w_outer,
    gain_three,
    shift_three,
):
    return (
        lax.all_gather(w_query, "fsdp", axis=0, tiled=True),
        lax.all_gather(w_key, "fsdp", axis=0, tiled=True),
        lax.all_gather(w_value, "fsdp", axis=0, tiled=True),
        lax.all_gather(w_rel, "fsdp", axis=0, tiled=True),
        lax.all_gather(w_out, "fsdp", axis=0, tiled=True),
        lax.all_gather(gain_one, "fsdp", axis=0, tiled=True),
        lax.all_gather(shift_one, "fsdp", axis=0, tiled=True),
        lax.all_gather(c_query, "fsdp", axis=0, tiled=True),
        lax.all_gather(c_key, "fsdp", axis=0, tiled=True),
        lax.all_gather(c_value, "fsdp", axis=0, tiled=True),
        lax.all_gather(c_out, "fsdp", axis=0, tiled=True),
        lax.all_gather(gain_two, "fsdp", axis=0, tiled=True),
        lax.all_gather(shift_two, "fsdp", axis=0, tiled=True),
        lax.all_gather(w_inner, "fsdp", axis=0, tiled=True),
        lax.all_gather(w_outer, "fsdp", axis=0, tiled=True),
        lax.all_gather(gain_three, "fsdp", axis=0, tiled=True),
        lax.all_gather(shift_three, "fsdp", axis=0, tiled=True),
    )


def reduce_grads(grads):
    return (
        lax.psum_scatter(
            grads[0].astype(jnp.bfloat16), "fsdp", scatter_dimension=0, tiled=True
        ).astype(jnp.float32),
        lax.psum_scatter(
            grads[1].astype(jnp.bfloat16), "fsdp", scatter_dimension=0, tiled=True
        ).astype(jnp.float32),
        lax.psum_scatter(
            grads[2].astype(jnp.bfloat16), "fsdp", scatter_dimension=0, tiled=True
        ).astype(jnp.float32),
        lax.psum_scatter(
            grads[3].astype(jnp.bfloat16), "fsdp", scatter_dimension=0, tiled=True
        ).astype(jnp.float32),
        lax.psum_scatter(
            grads[4].astype(jnp.bfloat16), "fsdp", scatter_dimension=0, tiled=True
        ).astype(jnp.float32),
        lax.psum_scatter(
            grads[5].astype(jnp.bfloat16), "fsdp", scatter_dimension=0, tiled=True
        ).astype(jnp.float32),
        lax.psum_scatter(
            grads[6].astype(jnp.bfloat16), "fsdp", scatter_dimension=0, tiled=True
        ).astype(jnp.float32),
        lax.psum_scatter(
            grads[7].astype(jnp.bfloat16), "fsdp", scatter_dimension=0, tiled=True
        ).astype(jnp.float32),
        lax.psum_scatter(
            grads[8].astype(jnp.bfloat16), "fsdp", scatter_dimension=0, tiled=True
        ).astype(jnp.float32),
        lax.psum_scatter(
            grads[9].astype(jnp.bfloat16), "fsdp", scatter_dimension=0, tiled=True
        ).astype(jnp.float32),
        lax.psum_scatter(
            grads[10].astype(jnp.bfloat16), "fsdp", scatter_dimension=0, tiled=True
        ).astype(jnp.float32),
        lax.psum_scatter(
            grads[11].astype(jnp.bfloat16), "fsdp", scatter_dimension=0, tiled=True
        ).astype(jnp.float32),
        lax.psum_scatter(
            grads[12].astype(jnp.bfloat16), "fsdp", scatter_dimension=0, tiled=True
        ).astype(jnp.float32),
        lax.psum_scatter(
            grads[13].astype(jnp.bfloat16), "fsdp", scatter_dimension=0, tiled=True
        ).astype(jnp.float32),
        lax.psum_scatter(
            grads[14].astype(jnp.bfloat16), "fsdp", scatter_dimension=0, tiled=True
        ).astype(jnp.float32),
        lax.psum_scatter(
            grads[15].astype(jnp.bfloat16), "fsdp", scatter_dimension=0, tiled=True
        ).astype(jnp.float32),
        lax.psum_scatter(
            grads[16].astype(jnp.bfloat16), "fsdp", scatter_dimension=0, tiled=True
        ).astype(jnp.float32),
    )


def self_scores(query, rel, keys_main, onehot, allowed, scale):
    raw = jnp.einsum("rhd,khd->hrk", query, keys_main, preferred_element_type=jnp.float32)
    bias = jnp.einsum("rbh,rbk->hrk", rel, onehot, preferred_element_type=jnp.float32)
    return jnp.where(allowed[None], raw * scale + bias, FILLER)


def own_scores(query, rel, own_key, own_bucket, scale):
    raw = jnp.sum(query.astype(jnp.float32) * own_key.astype(jnp.float32), axis=-1)
    return jnp.transpose(raw * scale + rel[:, own_bucket, :].astype(jnp.float32))


def self_forward(
    query, rel, own_key, own_value, keys_main, values_main, onehot, allowed, own_bucket, scale
):
    scores = self_scores(query, rel, keys_main, onehot, allowed, scale)
    top = jnp.max(scores, axis=-1)
    if own_key is not None:
        own = own_scores(query, rel, own_key, own_bucket, scale)
        top = jnp.maximum(top, own)
    weights = jnp.exp(scores - top[..., None])
    total = jnp.sum(weights, axis=-1)
    if own_key is not None:
        own_weight = jnp.exp(own - top)
        total = total + own_weight
    probs = (weights / total[..., None]).astype(jnp.bfloat16)
    mixed = jnp.einsum("hrk,khd->rhd", probs, values_main, preferred_element_type=jnp.float32)
    if own_key is not None:
        own_prob = (own_weight / total).astype(jnp.bfloat16)
        mixed = mixed + jnp.transpose(own_prob).astype(jnp.float32)[..., None] * own_value.astype(
            jnp.float32
        )
    return (mixed.astype(jnp.bfloat16), top, total)


def self_backward(
    grad_out,
    query,
    rel,
    own_key,
    own_value,
    keys_main,
    values_main,
    onehot,
    allowed,
    own_bucket,
    scale,
    top,
    total,
):
    scores = self_scores(query, rel, keys_main, onehot, allowed, scale)
    probs_full = jnp.exp(scores - top[..., None]) / total[..., None]
    probs = probs_full.astype(jnp.bfloat16)
    grad_probs = jnp.einsum(
        "rhd,khd->hrk", grad_out, values_main, preferred_element_type=jnp.float32
    )
    delta = jnp.sum(probs_full * grad_probs, axis=-1)
    if own_key is not None:
        own = own_scores(query, rel, own_key, own_bucket, scale)
        own_full = jnp.exp(own - top) / total
        grad_own = jnp.transpose(
            jnp.sum(grad_out.astype(jnp.float32) * own_value.astype(jnp.float32), axis=-1)
        )
        delta = delta + own_full * grad_own
    grad_scores = (probs_full * (grad_probs - delta[..., None])).astype(jnp.bfloat16)
    grad_query = scale * jnp.einsum(
        "hrk,khd->rhd", grad_scores, keys_main, preferred_element_type=jnp.float32
    )
    grad_keys = scale * jnp.einsum(
        "hrk,rhd->khd", grad_scores, query, preferred_element_type=jnp.float32
    )
    grad_values = jnp.einsum("hrk,rhd->khd", probs, grad_out, preferred_element_type=jnp.float32)
    grad_rel = jnp.einsum("hrk,rbk->rbh", grad_scores, onehot, preferred_element_type=jnp.float32)
    grad_own_key = None
    grad_own_value = None
    if own_key is not None:
        grad_own_score = (own_full * (grad_own - delta)).astype(jnp.bfloat16)
        own_column = jnp.transpose(grad_own_score).astype(jnp.float32)
        grad_query = grad_query + scale * own_column[..., None] * own_key.astype(jnp.float32)
        grad_own_key = scale * own_column[..., None] * query.astype(jnp.float32)
        own_prob = jnp.transpose(own_full.astype(jnp.bfloat16)).astype(jnp.float32)
        grad_own_value = own_prob[..., None] * grad_out.astype(jnp.float32)
        grad_rel = grad_rel.at[:, own_bucket, :].add(own_column)
    return (grad_query, grad_keys, grad_values, grad_rel, grad_own_key, grad_own_value)


def cross_scores(cross_query, enc_keys, scale):
    return (
        jnp.einsum("nhd,khd->hnk", cross_query, enc_keys, preferred_element_type=jnp.float32)
        * scale
    )


def micro_step(full, hidden_rows, encoded_rows, cotangent_rows, onehot, allowed, own_bucket):
    (
        w_query,
        w_key,
        w_value,
        w_rel,
        w_out,
        gain_one,
        shift_one,
        c_query,
        c_key,
        c_value,
        c_out,
        gain_two,
        shift_two,
        w_inner,
        w_outer,
        gain_three,
        shift_three,
    ) = full
    gain_one = gain_one.astype(jnp.float32)
    shift_one = shift_one.astype(jnp.float32)
    gain_two = gain_two.astype(jnp.float32)
    shift_two = shift_two.astype(jnp.float32)
    gain_three = gain_three.astype(jnp.float32)
    shift_three = shift_three.astype(jnp.float32)
    rows, streams, width = hidden_rows.shape
    total_rows = rows * streams
    scale = HEAD_DIM ** (-0.5)
    flat = hidden_rows.reshape(total_rows, width)
    query = matmul(flat, w_query).astype(jnp.bfloat16).reshape(rows, streams, HEADS, HEAD_DIM)
    keys = matmul(flat, w_key).astype(jnp.bfloat16).reshape(rows, streams, width)
    values = matmul(flat, w_value).astype(jnp.bfloat16).reshape(rows, streams, width)
    rel = matmul(flat, w_rel).astype(jnp.bfloat16).reshape(rows, streams, BUCKETS, HEADS)
    keys_main, values_main = (
        lax.all_gather(keys[:, 0, :], "ctx", axis=0, tiled=True),
        lax.all_gather(values[:, 0, :], "ctx", axis=0, tiled=True),
    )
    seq_rows = keys_main.shape[0]
    keys_main = keys_main.reshape(seq_rows, HEADS, HEAD_DIM)
    values_main = values_main.reshape(seq_rows, HEADS, HEAD_DIM)
    keys_heads = keys.reshape(rows, streams, HEADS, HEAD_DIM)
    values_heads = values.reshape(rows, streams, HEADS, HEAD_DIM)
    mixed_parts, tops, totals = ([], [], [])
    for stream in range(streams):
        own_key = None if stream == 0 else keys_heads[:, stream]
        own_value = None if stream == 0 else values_heads[:, stream]
        mixed_part, top, total = self_forward(
            query[:, stream],
            rel[:, stream],
            own_key,
            own_value,
            keys_main,
            values_main,
            onehot,
            allowed,
            own_bucket,
            scale,
        )
        mixed_parts.append(mixed_part)
        tops.append(top)
        totals.append(total)
    mixed = jnp.stack(mixed_parts, axis=1).reshape(total_rows, width)
    z_one = flat.astype(jnp.float32) + matmul(mixed, w_out)
    h_one = layer_norm(z_one, gain_one, shift_one)
    h_one_low = h_one.astype(jnp.bfloat16)
    cross_query = (
        matmul(h_one_low, c_query).astype(jnp.bfloat16).reshape(total_rows, HEADS, HEAD_DIM)
    )
    enc_keys_local = matmul(encoded_rows, c_key).astype(jnp.bfloat16)
    enc_values_local = matmul(encoded_rows, c_value).astype(jnp.bfloat16)
    enc_keys, enc_values = (
        lax.all_gather(enc_keys_local, "ctx", axis=0, tiled=True),
        lax.all_gather(enc_values_local, "ctx", axis=0, tiled=True),
    )
    enc_rows = enc_keys.shape[0]
    enc_keys = enc_keys.reshape(enc_rows, HEADS, HEAD_DIM)
    enc_values = enc_values.reshape(enc_rows, HEADS, HEAD_DIM)
    cross_raw = cross_scores(cross_query, enc_keys, scale)
    cross_top = jnp.max(cross_raw, axis=-1)
    cross_weights = jnp.exp(cross_raw - cross_top[..., None])
    cross_total = jnp.sum(cross_weights, axis=-1)
    cross_probs = (cross_weights / cross_total[..., None]).astype(jnp.bfloat16)
    cross_mixed = (
        jnp.einsum("hnk,khd->nhd", cross_probs, enc_values, preferred_element_type=jnp.float32)
        .astype(jnp.bfloat16)
        .reshape(total_rows, width)
    )
    z_two = h_one + matmul(cross_mixed, c_out)
    h_two = layer_norm(z_two, gain_two, shift_two)
    h_two_low = h_two.astype(jnp.bfloat16)
    inner = matmul(h_two_low, w_inner)
    active = exact_gelu(inner).astype(jnp.bfloat16)
    z_three = h_two + matmul(active, w_outer)
    result = layer_norm(z_three, gain_three, shift_three)
    output = result.astype(jnp.bfloat16).reshape(rows, streams, width)
    grad_result = cotangent_rows.reshape(total_rows, width).astype(jnp.float32)
    unused, norm_three_back = jax.vjp(layer_norm, z_three, gain_three, shift_three)
    grad_z_three, grad_gain_three, grad_shift_three = norm_three_back(grad_result)
    grad_ffn = grad_z_three.astype(jnp.bfloat16)
    grad_w_outer = left_transposed(active, grad_ffn)
    grad_active = right_transposed(grad_ffn, w_outer)
    unused, gelu_back = jax.vjp(exact_gelu, inner)
    grad_inner = gelu_back(grad_active)[0].astype(jnp.bfloat16)
    grad_w_inner = left_transposed(h_two_low, grad_inner)
    grad_h_two = grad_z_three + right_transposed(grad_inner, w_inner)
    unused, norm_two_back = jax.vjp(layer_norm, z_two, gain_two, shift_two)
    grad_z_two, grad_gain_two, grad_shift_two = norm_two_back(grad_h_two)
    grad_cross_out = grad_z_two.astype(jnp.bfloat16)
    grad_c_out = left_transposed(cross_mixed, grad_cross_out)
    grad_cross_mixed = (
        right_transposed(grad_cross_out, c_out)
        .astype(jnp.bfloat16)
        .reshape(total_rows, HEADS, HEAD_DIM)
    )
    cross_full = (
        jnp.exp(cross_scores(cross_query, enc_keys, scale) - cross_top[..., None])
        / cross_total[..., None]
    )
    cross_probs = cross_full.astype(jnp.bfloat16)
    grad_cross_probs = jnp.einsum(
        "nhd,khd->hnk", grad_cross_mixed, enc_values, preferred_element_type=jnp.float32
    )
    cross_delta = jnp.sum(cross_full * grad_cross_probs, axis=-1)
    grad_cross_scores = (cross_full * (grad_cross_probs - cross_delta[..., None])).astype(
        jnp.bfloat16
    )
    grad_cross_query = (
        scale
        * jnp.einsum(
            "hnk,khd->nhd", grad_cross_scores, enc_keys, preferred_element_type=jnp.float32
        )
    ).astype(jnp.bfloat16)
    grad_enc_keys = scale * jnp.einsum(
        "hnk,nhd->khd", grad_cross_scores, cross_query, preferred_element_type=jnp.float32
    )
    grad_enc_values = jnp.einsum(
        "hnk,nhd->khd", cross_probs, grad_cross_mixed, preferred_element_type=jnp.float32
    )
    grad_enc_keys, grad_enc_values = (
        lax.psum_scatter(
            grad_enc_keys.reshape(enc_rows, width).astype(jnp.bfloat16),
            "ctx",
            scatter_dimension=0,
            tiled=True,
        ).astype(jnp.float32),
        lax.psum_scatter(
            grad_enc_values.reshape(enc_rows, width).astype(jnp.bfloat16),
            "ctx",
            scatter_dimension=0,
            tiled=True,
        ).astype(jnp.float32),
    )
    grad_enc_keys = grad_enc_keys.astype(jnp.bfloat16)
    grad_enc_values = grad_enc_values.astype(jnp.bfloat16)
    grad_c_key = left_transposed(encoded_rows, grad_enc_keys)
    grad_c_value = left_transposed(encoded_rows, grad_enc_values)
    grad_encoded = right_transposed(grad_enc_keys, c_key) + right_transposed(
        grad_enc_values, c_value
    )
    grad_cross_query = grad_cross_query.reshape(total_rows, width)
    grad_c_query = left_transposed(h_one_low, grad_cross_query)
    grad_h_one = grad_z_two + right_transposed(grad_cross_query, c_query)
    unused, norm_one_back = jax.vjp(layer_norm, z_one, gain_one, shift_one)
    grad_z_one, grad_gain_one, grad_shift_one = norm_one_back(grad_h_one)
    grad_attn = grad_z_one.astype(jnp.bfloat16)
    grad_w_out = left_transposed(mixed, grad_attn)
    grad_mixed = (
        right_transposed(grad_attn, w_out)
        .astype(jnp.bfloat16)
        .reshape(rows, streams, HEADS, HEAD_DIM)
    )
    keys_total = jnp.zeros((seq_rows, HEADS, HEAD_DIM), jnp.float32)
    values_total = jnp.zeros((seq_rows, HEADS, HEAD_DIM), jnp.float32)
    query_grads, rel_grads, own_key_grads, own_value_grads = ([], [], [], [])
    for stream in range(streams):
        own_key = None if stream == 0 else keys_heads[:, stream]
        own_value = None if stream == 0 else values_heads[:, stream]
        parts = self_backward(
            grad_mixed[:, stream],
            query[:, stream],
            rel[:, stream],
            own_key,
            own_value,
            keys_main,
            values_main,
            onehot,
            allowed,
            own_bucket,
            scale,
            tops[stream],
            totals[stream],
        )
        query_grads.append(parts[0])
        keys_total = keys_total + parts[1]
        values_total = values_total + parts[2]
        rel_grads.append(parts[3])
        if stream > 0:
            own_key_grads.append(parts[4].reshape(rows, width))
            own_value_grads.append(parts[5].reshape(rows, width))
    main_key_grad, main_value_grad = (
        lax.psum_scatter(
            keys_total.reshape(seq_rows, width).astype(jnp.bfloat16),
            "ctx",
            scatter_dimension=0,
            tiled=True,
        ).astype(jnp.float32),
        lax.psum_scatter(
            values_total.reshape(seq_rows, width).astype(jnp.bfloat16),
            "ctx",
            scatter_dimension=0,
            tiled=True,
        ).astype(jnp.float32),
    )
    grad_query = jnp.stack(query_grads, axis=1).astype(jnp.bfloat16).reshape(total_rows, width)
    grad_keys = (
        jnp.stack([main_key_grad] + own_key_grads, axis=1)
        .astype(jnp.bfloat16)
        .reshape(total_rows, width)
    )
    grad_values = (
        jnp.stack([main_value_grad] + own_value_grads, axis=1)
        .astype(jnp.bfloat16)
        .reshape(total_rows, width)
    )
    grad_rel = (
        jnp.stack(rel_grads, axis=1).astype(jnp.bfloat16).reshape(total_rows, BUCKETS * HEADS)
    )
    grad_w_query = left_transposed(flat, grad_query)
    grad_w_key = left_transposed(flat, grad_keys)
    grad_w_value = left_transposed(flat, grad_values)
    grad_w_rel = left_transposed(flat, grad_rel)
    grad_hidden = (
        grad_z_one
        + right_transposed(grad_query, w_query)
        + right_transposed(grad_keys, w_key)
        + right_transposed(grad_values, w_value)
        + right_transposed(grad_rel, w_rel)
    )
    grads = (
        grad_w_query,
        grad_w_key,
        grad_w_value,
        grad_w_rel,
        grad_w_out,
        grad_gain_one,
        grad_shift_one,
        grad_c_query,
        grad_c_key,
        grad_c_value,
        grad_c_out,
        grad_gain_two,
        grad_shift_two,
        grad_w_inner,
        grad_w_outer,
        grad_gain_three,
        grad_shift_three,
    )
    return (output, grad_hidden.reshape(rows, streams, width), grad_encoded, grads)


def body(
    hidden,
    encoded,
    assign,
    bucket_table,
    w_query,
    w_key,
    w_value,
    w_rel,
    w_out,
    gain_one,
    shift_one,
    c_query,
    c_key,
    c_value,
    c_out,
    gain_two,
    shift_two,
    w_inner,
    w_outer,
    gain_three,
    shift_three,
    cotangent,
):
    rows = hidden.shape[1]
    rank = lax.axis_index("ctx")
    blocks_all = jnp.broadcast_to(assign[:, None], (assign.shape[0], BLK)).reshape(-1)
    places_all = blocks_all * BLK + jnp.arange(blocks_all.shape[0], dtype=jnp.int32) % BLK
    own_blocks = lax.dynamic_slice_in_dim(blocks_all, rank * rows, rows)
    own_places = lax.dynamic_slice_in_dim(places_all, rank * rows, rows)
    span = bucket_table.shape[0]
    distance = jnp.clip(own_places[:, None] - places_all[None, :] + BLK - 1, 0, span - 1)
    buckets = jnp.take(bucket_table, distance)
    onehot = (buckets[:, None, :] == jnp.arange(BUCKETS, dtype=jnp.int32)[None, :, None]).astype(
        jnp.bfloat16
    )
    allowed = own_blocks[:, None] >= blocks_all[None, :]
    own_bucket = bucket_table[BLK - 1]
    micro = hidden.shape[0]
    outputs, hidden_grads, encoded_grads = ([], [], [])
    shards = None
    for index in range(micro):
        full = fetch_weights(
            w_query,
            w_key,
            w_value,
            w_rel,
            w_out,
            gain_one,
            shift_one,
            c_query,
            c_key,
            c_value,
            c_out,
            gain_two,
            shift_two,
            w_inner,
            w_outer,
            gain_three,
            shift_three,
        )
        output, grad_rows, grad_enc, grads = micro_step(
            full, hidden[index], encoded[index], cotangent[index], onehot, allowed, own_bucket
        )
        outputs.append(output)
        hidden_grads.append(grad_rows)
        encoded_grads.append(grad_enc)
        reduced = reduce_grads(grads)
        shards = reduced if shards is None else jax.tree.map(jnp.add, shards, reduced)
    totals = (
        lax.psum(shards[0].astype(jnp.bfloat16), "ctx").astype(jnp.float32),
        lax.psum(shards[1].astype(jnp.bfloat16), "ctx").astype(jnp.float32),
        lax.psum(shards[2].astype(jnp.bfloat16), "ctx").astype(jnp.float32),
        lax.psum(shards[3].astype(jnp.bfloat16), "ctx").astype(jnp.float32),
        lax.psum(shards[4].astype(jnp.bfloat16), "ctx").astype(jnp.float32),
        lax.psum(shards[5].astype(jnp.bfloat16), "ctx").astype(jnp.float32),
        lax.psum(shards[6].astype(jnp.bfloat16), "ctx").astype(jnp.float32),
        lax.psum(shards[7].astype(jnp.bfloat16), "ctx").astype(jnp.float32),
        lax.psum(shards[8].astype(jnp.bfloat16), "ctx").astype(jnp.float32),
        lax.psum(shards[9].astype(jnp.bfloat16), "ctx").astype(jnp.float32),
        lax.psum(shards[10].astype(jnp.bfloat16), "ctx").astype(jnp.float32),
        lax.psum(shards[11].astype(jnp.bfloat16), "ctx").astype(jnp.float32),
        lax.psum(shards[12].astype(jnp.bfloat16), "ctx").astype(jnp.float32),
        lax.psum(shards[13].astype(jnp.bfloat16), "ctx").astype(jnp.float32),
        lax.psum(shards[14].astype(jnp.bfloat16), "ctx").astype(jnp.float32),
        lax.psum(shards[15].astype(jnp.bfloat16), "ctx").astype(jnp.float32),
        lax.psum(shards[16].astype(jnp.bfloat16), "ctx").astype(jnp.float32),
    )
    return (
        jnp.stack(outputs, axis=0),
        jnp.stack(hidden_grads, axis=0),
        jnp.stack(encoded_grads, axis=0),
        totals[0],
        totals[1],
        totals[2],
        totals[3],
        totals[4],
        totals[5],
        totals[6],
        totals[7],
        totals[8],
        totals[9],
        totals[10],
        totals[11],
        totals[12],
        totals[13],
        totals[14],
        totals[15],
        totals[16],
    )


def solution(mesh):
    in_specs = (
        P("fsdp", "ctx", None, None),
        P("fsdp", "ctx", None),
        P(),
        P(),
        P("fsdp", None),
        P("fsdp", None),
        P("fsdp", None),
        P("fsdp", None),
        P("fsdp", None),
        P("fsdp"),
        P("fsdp"),
        P("fsdp", None),
        P("fsdp", None),
        P("fsdp", None),
        P("fsdp", None),
        P("fsdp"),
        P("fsdp"),
        P("fsdp", None),
        P("fsdp", None),
        P("fsdp"),
        P("fsdp"),
        P("fsdp", "ctx", None, None),
    )
    out_specs = (
        P("fsdp", "ctx", None, None),
        P("fsdp", "ctx", None, None),
        P("fsdp", "ctx", None),
        P("fsdp", None),
        P("fsdp", None),
        P("fsdp", None),
        P("fsdp", None),
        P("fsdp", None),
        P("fsdp"),
        P("fsdp"),
        P("fsdp", None),
        P("fsdp", None),
        P("fsdp", None),
        P("fsdp", None),
        P("fsdp"),
        P("fsdp"),
        P("fsdp", None),
        P("fsdp", None),
        P("fsdp"),
        P("fsdp"),
    )
    return jax.shard_map(body, mesh=mesh, in_specs=in_specs, out_specs=out_specs, check_vma=False)
```

profile of v0, /device:TPU:1, one launch (start us, length us, event | category | flops | bytes accessed | tf_op | source)
XLA Modules:
  0.0 5253.3 jit_solution(1780666454313451250)
XLA Ops:
  11.2 48.2 all-gather.46.cloned.1.call-done
  62.5 46.7 all-gather.40.cloned.1.call-done
  123.4 35.6 all-gather.34.cloned.1.call-done
  184.0 24.6 all-gather.30.cloned.1.call-done
  232.7 1449.2 %gather_fusion = s32[262144]{0:T(1024)S(1)} fusion(s32[1055]{0:T(1024)S(1)} %copy-done, s32[262144]{0:T(1024)S(1)} %broadcast_clamp_fusion), kind=kCustom, calls=%fused_computation | custom fusion | bytes 3145728 | tf_op jit(solution)/shard_map/jit(_take)/gather | solution.py:524
  1684.3 15.7 all-gather.4
  1700.6 12.8 all-gather.5
  1714.0 14.2 all-gather.6
  1769.4 14.2 all-gather.8
  1801.7 14.7 reshape.967
  1998.3 22.1 fusion.386
  2028.9 21.6 fusion.385
  2062.8 22.1 fusion.379
  2094.1 21.8 fusion.378
  2125.0 21.6 fusion.20
  2146.6 18.0 fusion.387
  2168.5 15.4 fusion.196
  2224.5 13.5 fusion.389
  2256.7 21.5 fusion.23
  2278.3 17.9 fusion.380
  2299.1 18.7 fusion.199
  2354.9 13.5 fusion.382
  2384.6 38.8 multiply_convert_fusion.8
  2436.7 37.4 multiply_convert_fusion.9
  2493.0 19.7 add_convert_fusion
  2524.8 20.6 add_convert_fusion.1
  2545.4 16.6 multiply_reduce_fusion.13
  2572.9 19.3 multiply_reduce_fusion.1
  2592.2 13.7 fusion.128
  2612.4 16.3 multiply_reduce_fusion
  2640.2 16.6 multiply_convert_fusion
  2666.4 16.8 multiply_convert_fusion.1
  2735.0 13.1 multiply_reduce_fusion.7
  2820.6 13.3 multiply_reduce_fusion.4
  2869.9 15.3 multiply_convert_fusion.5
  2885.3 19.6 add_convert_fusion.3
  2935.5 16.2 multiply_convert_fusion.3
  2951.8 15.0 multiply_reduce_fusion.6
  2973.0 19.8 add_convert_fusion.2
  3004.2 16.0 multiply_convert_fusion.4
  3045.4 16.2 multiply_convert_fusion.2
  3111.0 22.2 scatter-add.14
  3139.5 22.1 scatter-add.15
  3226.0 22.5 scatter-add.16
  3261.2 22.1 scatter-add.19
  3579.7 27.6 all-reduce.12
  3607.8 37.3 all-reduce.13
  3691.7 69.2 %reduce-scatter.75.cloned.1.call-done = bf16[128,1024]{1,0:T(8,128)(2,1)} async-done(((bf16[1024,1024]{1,0:T(8,128)(2,1)}), bf16[128,1024]{1,0:T(8,128)(2,1)}) %reduce-scatter.75.cloned.1.call-update) | async-done | bytes 262160 | tf_op jit(solution)/shard_map/reduce_scatter | solution.py:106
  3760.9 71.1 %reduce-scatter.77.cloned.1.call-done = bf16[128,1024]{1,0:T(8,128)(2,1)} async-done(((bf16[1024,1024]{1,0:T(8,128)(2,1)}), bf16[128,1024]{1,0:T(8,128)(2,1)}) %reduce-scatter.77.cloned.1.call-update) | async-done | bytes 262160 | tf_op jit(solution)/shard_map/reduce_scatter | solution.py:106
  3833.8 69.1 %reduce-scatter.71.cloned.1.call-done = bf16[128,1024]{1,0:T(8,128)(2,1)} async-done(((bf16[1024,1024]{1,0:T(8,128)(2,1)}), bf16[128,1024]{1,0:T(8,128)(2,1)}) %reduce-scatter.71.cloned.1.call-update) | async-done | bytes 262160 | tf_op jit(solution)/shard_map/reduce_scatter | solution.py:97
  3902.9 70.9 %reduce-scatter.73.cloned.1.call-done = bf16[128,1024]{1,0:T(8,128)(2,1)} async-done(((bf16[1024,1024]{1,0:T(8,128)(2,1)}), bf16[128,1024]{1,0:T(8,128)(2,1)}) %reduce-scatter.73.cloned.1.call-update) | async-done | bytes 262160 | tf_op jit(solution)/shard_map/reduce_scatter | solution.py:97
  3984.6 60.3 %reduce-scatter.119.cloned.1.call-done = bf16[128,1024]{1,0:T(8,128)(2,1)} async-done(((bf16[1024,1024]{1,0:T(8,128)(2,1)}), bf16[128,1024]{1,0:T(8,128)(2,1)}) %reduce-scatter.119.cloned.1.call-update) | async-done | bytes 262160
  4046.0 69.8 %reduce-scatter.121.cloned.1.call-done = bf16[128,1024]{1,0:T(8,128)(2,1)} async-done(((bf16[1024,1024]{1,0:T(8,128)(2,1)}), bf16[128,1024]{1,0:T(8,128)(2,1)}) %reduce-scatter.121.cloned.1.call-update) | async-done | bytes 262160
  4116.9 69.7 %reduce-scatter.117.cloned.1.call-done = bf16[128,1024]{1,0:T(8,128)(2,1)} async-done(((bf16[1024,1024]{1,0:T(8,128)(2,1)}), bf16[128,1024]{1,0:T(8,128)(2,1)}) %reduce-scatter.117.cloned.1.call-update) | async-done | bytes 262160
  4187.7 69.8 %reduce-scatter.115.cloned.1.call-done = bf16[128,1024]{1,0:T(8,128)(2,1)} async-done(((bf16[1024,1024]{1,0:T(8,128)(2,1)}), bf16[128,1024]{1,0:T(8,128)(2,1)}) %reduce-scatter.115.cloned.1.call-update) | async-done | bytes 262160
  4260.2 68.2 %reduce-scatter.107.cloned.1.call-done = bf16[128,1024]{1,0:T(8,128)(2,1)} async-done(((bf16[1024,1024]{1,0:T(8,128)(2,1)}), bf16[128,1024]{1,0:T(8,128)(2,1)}) %reduce-scatter.107.cloned.1.call-update) | async-done | bytes 262160
  4329.5 69.7 %reduce-scatter.109.cloned.1.call-done = bf16[128,1024]{1,0:T(8,128)(2,1)} async-done(((bf16[1024,1024]{1,0:T(8,128)(2,1)}), bf16[128,1024]{1,0:T(8,128)(2,1)}) %reduce-scatter.109.cloned.1.call-update) | async-done | bytes 262160
  4400.3 69.9 %reduce-scatter.103.cloned.1.call-done = bf16[128,1024]{1,0:T(8,128)(2,1)} async-done(((bf16[1024,1024]{1,0:T(8,128)(2,1)}), bf16[128,1024]{1,0:T(8,128)(2,1)}) %reduce-scatter.103.cloned.1.call-update) | async-done | bytes 262160
  4471.3 69.6 %reduce-scatter.105.cloned.1.call-done = bf16[128,1024]{1,0:T(8,128)(2,1)} async-done(((bf16[1024,1024]{1,0:T(8,128)(2,1)}), bf16[128,1024]{1,0:T(8,128)(2,1)}) %reduce-scatter.105.cloned.1.call-update) | async-done | bytes 262160
  4543.7 148.5 %reduce-scatter.87.cloned.1.call-done = bf16[512,1024]{1,0:T(8,128)(2,1)} async-done(((bf16[4096,1024]{1,0:T(8,128)(2,1)}), bf16[512,1024]{1,0:T(8,128)(2,1)}) %reduce-scatter.87.cloned.1.call-update) | async-done | bytes 1048592 | tf_op jit(solution)/shard_map/reduce_scatter | solution.py:127
  4692.2 150.1 %reduce-scatter.89.cloned.1.call-done = bf16[512,1024]{1,0:T(8,128)(2,1)} async-done(((bf16[4096,1024]{1,0:T(8,128)(2,1)}), bf16[512,1024]{1,0:T(8,128)(2,1)}) %reduce-scatter.89.cloned.1.call-update) | async-done | bytes 1048592 | tf_op jit(solution)/shard_map/reduce_scatter | solution.py:127
  4845.2 147.2 %reduce-scatter.83.cloned.1.call-done = bf16[128,4096]{1,0:T(8,128)(2,1)} async-done(((bf16[1024,4096]{1,0:T(8,128)(2,1)}), bf16[128,4096]{1,0:T(8,128)(2,1)}) %reduce-scatter.83.cloned.1.call-update) | async-done | bytes 1048592 | tf_op jit(solution)/shard_map/reduce_scatter | solution.py:124
  4992.4 150.1 %reduce-scatter.85.cloned.1.call-done = bf16[128,4096]{1,0:T(8,128)(2,1)} async-done(((bf16[1024,4096]{1,0:T(8,128)(2,1)}), bf16[128,4096]{1,0:T(8,128)(2,1)}) %reduce-scatter.85.cloned.1.call-update) | async-done | bytes 1048592 | tf_op jit(solution)/shard_map/reduce_scatter | solution.py:124
  5185.6 48.4 all-reduce.17.cloned.1.call-done
  (1266 shorter events, 1342.1 us)
Async XLA Ops:
  7.2 52.2 all-gather.46.cloned.1.call-start
  7.9 101.2 %all-gather.40.cloned.1.call-start = ((), (), s32[]{:S(2)}) async-start(), calls=%async_computation.35 | async-start | bytes 2359296 | tf_op jit(solution)/shard_map/all_gather | solution.py:72
  8.7 150.3 %all-gather.34.cloned.1.call-start = ((), (), s32[]{:S(2)}) async-start(), calls=%async_computation.32 | async-start | bytes 2359296 | tf_op jit(solution)/shard_map/all_gather | solution.py:64
  9.4 199.2 %all-gather.30.cloned.1.call-start = ((), (), s32[]{:S(2)}) async-start(), calls=%async_computation.30 | async-start | bytes 2359296 | tf_op jit(solution)/shard_map/all_gather | solution.py:65
  10.0 1789.0 %all-gather.36.cloned.1.call-start = ((), (), s32[]{:S(2)}) async-start(), calls=%async_computation.33 | async-start | bytes 1179648 | tf_op jit(solution)/shard_map/all_gather | solution.py:66
  10.6 1901.8 %all-gather.32.cloned.1.call-start = ((), (), s32[]{:S(2)}) async-start(), calls=%async_computation.31 | async-start | bytes 2359296 | tf_op jit(solution)/shard_map/all_gather | solution.py:63
  11.2 1975.1 %all-gather.58.cloned.1.call-start = ((), (), s32[]{:S(2)}) async-start(), calls=%async_computation.44 | async-start | bytes 1310720 | tf_op jit(solution)/shard_map/all_gather | solution.py:303
  62.4 1926.2 %all-gather.56.cloned.1.call-start = ((), (), s32[]{:S(2)}) async-start(), calls=%async_computation.43 | async-start | bytes 1310720 | tf_op jit(solution)/shard_map/all_gather | solution.py:304
  111.9 1878.9 %all-gather.48.cloned.1.call-start = ((), (), s32[]{:S(2)}) async-start(), calls=%async_computation.39 | async-start | bytes 1310720 | tf_op jit(solution)/shard_map/all_gather | solution.py:303
  113.2 1880.0 %all-gather.42.cloned.1.call-start = ((), (), s32[]{:S(2)}) async-start(), calls=%async_computation.36 | async-start | bytes 1310720 | tf_op jit(solution)/shard_map/all_gather | solution.py:304
  116.0 1879.4 %all-gather.66.cloned.1.call-start = ((), (), s32[]{:S(2)}) async-start(), calls=%async_computation.62 | async-start | bytes 2621440 | tf_op jit(solution)/shard_map/all_gather | solution.py:266
  168.8 1890.1 %all-gather.62.cloned.1.call-start = ((), (), s32[]{:S(2)}) async-start(), calls=%async_computation.60 | async-start | bytes 2621440 | tf_op jit(solution)/shard_map/all_gather | solution.py:266
  183.7 1980.9 %all-gather.64.cloned.1.call-start = ((), (), s32[]{:S(2)}) async-start(), calls=%async_computation.61 | async-start | bytes 2621440 | tf_op jit(solution)/shard_map/all_gather | solution.py:267
  218.0 1991.6 %all-gather.38.cloned.1.call-start = ((), (), s32[]{:S(2)}) async-start(), calls=%async_computation.34 | async-start | bytes 2359296 | tf_op jit(solution)/shard_map/all_gather | solution.py:67
  218.6 1997.7 %all-gather.44.cloned.1.call-start = ((), (), s32[]{:S(2)}) async-start(), calls=%async_computation.37 | async-start | bytes 2359296 | tf_op jit(solution)/shard_map/all_gather | solution.py:70
  219.2 2030.5 %all-gather.50.cloned.1.call-start = ((), (), s32[]{:S(2)}) async-start(), calls=%async_computation.40 | async-start | bytes 2359296 | tf_op jit(solution)/shard_map/all_gather | solution.py:73
  219.7 2076.5 %all-gather.60.cloned.1.call-start = ((), (), s32[]{:S(2)}) async-start(), calls=%async_computation.59 | async-start | bytes 2621440 | tf_op jit(solution)/shard_map/all_gather | solution.py:267
  229.0 2155.6 %all-gather.52.cloned.1.call-start = ((), (), s32[]{:S(2)}) async-start(), calls=%async_computation.41 | async-start | bytes 9437184 | tf_op jit(solution)/shard_map/all_gather | solution.py:76
  229.6 2193.8 %all-gather.54.cloned.1.call-start = ((), (), s32[]{:S(2)}) async-start(), calls=%async_computation.42 | async-start | bytes 9437184 | tf_op jit(solution)/shard_map/all_gather | solution.py:77
  230.4 3183.2 %reduce-scatter.93.cloned.1.call-start = ((), (), s32[]{:S(2)}) async-start(), calls=%async_computation.64 | async-start | bytes 1310720
  232.7 1449.5 %copy-start.231 = (s32[1024]{0:T(1024)S(1)}, s32[1024]{0:T(1024)}, u32[]{:S(2)}) copy-start(s32[1024]{0:T(1024)} %copy-done.230) | copy-start | bytes 12292
  232.7 1449.5 %copy-start.281 = (s32[256]{0:T(256)S(1)}, s32[256]{0:T(256)}, u32[]{:S(2)}) copy-start(s32[256]{0:T(256)} %copy-done.280) | copy-start | bytes 3076
  1682.7 197.6 %copy-start.6 = (s32[256,1024]{1,0:T(8,128)}, s32[256,1024]{1,0:T(8,128)S(1)}, u32[]{:S(2)}) copy-start(s32[256,1024]{1,0:T(8,128)S(1)} %fusion.228) | copy-start | bytes 3145732
  1891.2 167.0 %copy-start.166 = (bf16[256,1,1,16]{0,3,2,1:T(8,128)(2,1)}, bf16[256,1,1,16]{0,3,2,1:T(8,128)(2,1)S(1)}, u32[]{:S(2)}) copy-start(bf16[256,1,1,16]{0,3,2,1:T(8,128)(2,1)S(1)} %copy.1894) | copy-start | bytes 24580
  1892.8 200.6 %copy-start.172 = (bf16[256,1,1,16]{0,3,2,1:T(8,128)(2,1)}, bf16[256,1,1,16]{0,3,2,1:T(8,128)(2,1)S(1)}, u32[]{:S(2)}) copy-start(bf16[256,1,1,16]{0,3,2,1:T(8,128)(2,1)S(1)} %copy.1891) | copy-start | bytes 24580
  1892.9 231.4 %copy-start.170 = (bf16[256,1,1,16]{0,3,2,1:T(8,128)(2,1)}, bf16[256,1,1,16]{0,3,2,1:T(8,128)(2,1)S(1)}, u32[]{:S(2)}) copy-start(bf16[256,1,1,16]{0,3,2,1:T(8,128)(2,1)S(1)} %copy.1892) | copy-start | bytes 24580
  2020.4 163.6 %copy-start.183 = (f32[16,256]{1,0:T(8,128)}, f32[16,256]{1,0:T(8,128)S(1)}, u32[]{:S(2)}) copy-start(f32[16,256]{1,0:T(8,128)S(1)} %bitcast_maximum_fusion.1) | copy-start | bytes 49156
  2028.2 155.7 %copy-start.208 = (f32[16,256]{1,0:T(8,128)}, f32[16,256]{1,0:T(8,128)S(1)}, u32[]{:S(2)}) copy-start(f32[16,256]{1,0:T(8,128)S(1)} %fusion.305) | copy-start | bytes 49156
  2028.9 155.1 %copy-start.197 = (f32[256,16]{0,1:T(8,128)}, f32[256,16]{0,1:T(8,128)S(1)}, u32[]{:S(2)}) copy-start(f32[256,16]{0,1:T(8,128)S(1)} %get-tuple-element.423) | copy-start | bytes 49156
  2256.7 166.7 %copy-start.243 = (f32[768]{0:T(1024)}, f32[768]{0:T(1024)S(1)}, u32[]{:S(2)}) copy-start(f32[768]{0:T(1024)S(1)} %broadcast_multiply_fusion.1) | copy-start | bytes 9220
  2382.0 180.1 %copy-start.246 = (f32[768]{0:T(1024)}, f32[768]{0:T(1024)S(1)}, u32[]{:S(2)}) copy-start(f32[768]{0:T(1024)S(1)} %broadcast_multiply_fusion.4) | copy-start | bytes 9220
  2384.6 177.5 %copy-start.272 = (f32[768]{0:T(1024)}, f32[768]{0:T(1024)S(1)}, u32[]{:S(2)}) copy-start(f32[768]{0:T(1024)S(1)} %fusion.312) | copy-start | bytes 9220
  2786.1 631.9 %reduce-scatter.97.cloned.1.call-start = ((), (), s32[]{:S(2)}) async-start(), calls=%async_computation.66 | async-start | bytes 1310720
  2869.8 552.8 %reduce-scatter.95.cloned.1.call-start = ((), (), s32[]{:S(2)}) async-start(), calls=%async_computation.65 | async-start | bytes 1310720
  2926.5 500.4 %reduce-scatter.91.cloned.1.call-start = ((), (), s32[]{:S(2)}) async-start(), calls=%async_computation.63 | async-start | bytes 1310720
  2935.4 507.9 %reduce-scatter.65.cloned.1.call-start = ((), (), s32[]{:S(2)}) async-start(), calls=%async_computation.46 | async-start | bytes 2621440 | tf_op jit(solution)/shard_map/reduce_scatter | solution.py:438
  2972.9 494.0 %reduce-scatter.69.cloned.1.call-start = ((), (), s32[]{:S(2)}) async-start(), calls=%async_computation.48 | async-start | bytes 2621440 | tf_op jit(solution)/shard_map/reduce_scatter | solution.py:438
  3020.2 467.6 %reduce-scatter.63.cloned.1.call-start = ((), (), s32[]{:S(2)}) async-start(), calls=%async_computation.45 | async-start | bytes 2621440 | tf_op jit(solution)/shard_map/reduce_scatter | solution.py:432
  3061.6 447.2 %reduce-scatter.67.cloned.1.call-start = ((), (), s32[]{:S(2)}) async-start(), calls=%async_computation.47 | async-start | bytes 2621440 | tf_op jit(solution)/shard_map/reduce_scatter | solution.py:432
  3096.9 575.6 %reduce-scatter.111.cloned.1.call-start = ((), (), s32[]{:S(2)}) async-start(), calls=%async_computation.73 | async-start | bytes 1179648
  3216.9 456.6 %reduce-scatter.113.cloned.1.call-start = ((), (), s32[]{:S(2)}) async-start(), calls=%async_computation.74 | async-start | bytes 1179648
  3320.1 360.4 %reduce-scatter.99.cloned.1.call-start = ((), (), s32[]{:S(2)}) async-start(), calls=%async_computation.67 | async-start | bytes 2359296
  3350.0 331.6 %reduce-scatter.101.cloned.1.call-start = ((), (), s32[]{:S(2)}) async-start(), calls=%async_computation.68 | async-start | bytes 2359296
  3380.6 303.0 %reduce-scatter.79.cloned.1.call-start = ((), (), s32[]{:S(2)}) async-start(), calls=%async_computation.53 | async-start | bytes 2359296 | tf_op jit(solution)/shard_map/reduce_scatter | solution.py:115
  3386.4 303.5 %reduce-scatter.81.cloned.1.call-start = ((), (), s32[]{:S(2)}) async-start(), calls=%async_computation.54 | async-start | bytes 2359296 | tf_op jit(solution)/shard_map/reduce_scatter | solution.py:115
  3391.6 369.3 %reduce-scatter.75.cloned.1.call-start = ((), (), s32[]{:S(2)}) async-start(), calls=%async_computation.51 | async-start | bytes 2359296 | tf_op jit(solution)/shard_map/reduce_scatter | solution.py:106
  3397.8 434.2 %reduce-scatter.77.cloned.1.call-start = ((), (), s32[]{:S(2)}) async-start(), calls=%async_computation.52 | async-start | bytes 2359296 | tf_op jit(solution)/shard_map/reduce_scatter | solution.py:106
  3402.8 500.1 %reduce-scatter.71.cloned.1.call-start = ((), (), s32[]{:S(2)}) async-start(), calls=%async_computation.49 | async-start | bytes 2359296 | tf_op jit(solution)/shard_map/reduce_scatter | solution.py:97
  3408.7 565.1 %reduce-scatter.73.cloned.1.call-start = ((), (), s32[]{:S(2)}) async-start(), calls=%async_computation.50 | async-start | bytes 2359296 | tf_op jit(solution)/shard_map/reduce_scatter | solution.py:97
  3413.5 631.4 %reduce-scatter.119.cloned.1.call-start = ((), (), s32[]{:S(2)}) async-start(), calls=%async_computation.77 | async-start | bytes 2359296
  3417.9 697.9 %reduce-scatter.121.cloned.1.call-start = ((), (), s32[]{:S(2)}) async-start(), calls=%async_computation.78 | async-start | bytes 2359296
  3422.3 764.3 %reduce-scatter.117.cloned.1.call-start = ((), (), s32[]{:S(2)}) async-start(), calls=%async_computation.76 | async-start | bytes 2359296
  3426.9 830.6 %reduce-scatter.115.cloned.1.call-start = ((), (), s32[]{:S(2)}) async-start(), calls=%async_computation.75 | async-start | bytes 2359296
  3431.3 897.1 %reduce-scatter.107.cloned.1.call-start = ((), (), s32[]{:S(2)}) async-start(), calls=%async_computation.71 | async-start | bytes 2359296
  3454.9 944.3 %reduce-scatter.109.cloned.1.call-start = ((), (), s32[]{:S(2)}) async-start(), calls=%async_computation.72 | async-start | bytes 2359296
  3478.6 991.6 %reduce-scatter.103.cloned.1.call-start = ((), (), s32[]{:S(2)}) async-start(), calls=%async_computation.69 | async-start | bytes 2359296
  3499.5 1041.5 %reduce-scatter.105.cloned.1.call-start = ((), (), s32[]{:S(2)}) async-start(), calls=%async_computation.70 | async-start | bytes 2359296
  3523.4 1168.8 %reduce-scatter.87.cloned.1.call-start = ((), (), s32[]{:S(2)}) async-start(), calls=%async_computation.57 | async-start | bytes 9437184 | tf_op jit(solution)/shard_map/reduce_scatter | solution.py:127
  3535.7 1306.5 %reduce-scatter.89.cloned.1.call-start = ((), (), s32[]{:S(2)}) async-start(), calls=%async_computation.58 | async-start | bytes 9437184 | tf_op jit(solution)/shard_map/reduce_scatter | solution.py:127
  3549.6 1442.7 %reduce-scatter.83.cloned.1.call-start = ((), (), s32[]{:S(2)}) async-start(), calls=%async_computation.55 | async-start | bytes 9437184 | tf_op jit(solution)/shard_map/reduce_scatter | solution.py:124
  3563.6 1578.8 %reduce-scatter.85.cloned.1.call-start = ((), (), s32[]{:S(2)}) async-start(), calls=%async_computation.56 | async-start | bytes 9437184 | tf_op jit(solution)/shard_map/reduce_scatter | solution.py:124
  3577.8 1656.2 %all-reduce.17.cloned.1.call-start = ((), (), s32[]{:S(2)}) async-start(), calls=%async_computation.79 | async-start | bytes 8650752 | tf_op jit(solution)/shard_map/psum | solution.py:562
  3678.7 296.9 %copy-start.121 = (bf16[768,1024]{1,0:T(8,128)(2,1)S(1)}, bf16[768,1024]{1,0:T(8,128)(2,1)}, u32[]{:S(2)}) copy-start(bf16[768,1024]{1,0:T(8,128)(2,1)} %convert_element_type.1185) | copy-start | bytes 4718596
  4845.2 300.0 %copy-start.259 = (f32[768]{0:T(1024)S(1)}, f32[768]{0:T(1024)}, u32[]{:S(2)}) copy-start(f32[768]{0:T(1024)} %copy-done.257) | copy-start | bytes 9220
  (330 other events, 4733.7 us)
Sparse Core Ops, SparseCore 0:
  10.1 49.2 all-gather.45
  61.5 47.6 all-gather.39
  111.3 47.6 all-gather.33
  160.9 47.6 all-gather.29
  210.6 39.0 all-gather.35
  251.6 47.6 all-gather.31
  300.8 17.5 all-gather.57
  320.0 16.6 all-gather.55
  338.3 16.6 all-gather.47
  357.0 16.6 all-gather.41
  375.3 22.5 all-gather.65
  399.9 22.5 all-gather.61
  424.1 22.5 all-gather.63
  448.6 46.7 all-gather.37
  497.5 47.6 all-gather.43
  547.1 47.6 all-gather.49
  596.8 23.3 all-gather.59
  622.2 123.3 all-gather.51
  747.7 122.6 all-gather.53
  2786.2 46.1 reduce-scatter.92
  2869.9 46.0 reduce-scatter.96
  2926.6 46.3 reduce-scatter.94
  2975.5 24.8 reduce-scatter.90
  3002.8 31.1 reduce-scatter.64
  3036.5 35.8 reduce-scatter.68
  3074.8 39.0 reduce-scatter.62
  3116.3 33.8 reduce-scatter.66
  3217.1 85.1 reduce-scatter.110
  3320.2 84.5 reduce-scatter.112
  3408.2 67.7 reduce-scatter.98
  3480.1 67.4 reduce-scatter.100
  3551.1 67.4 reduce-scatter.78
  3621.9 67.9 reduce-scatter.80
  3693.5 67.4 reduce-scatter.74
  3764.5 67.5 reduce-scatter.76
  3835.4 67.4 reduce-scatter.70
  3906.3 67.4 reduce-scatter.72
  3977.4 67.4 reduce-scatter.118
  4048.3 67.4 reduce-scatter.120
  4119.3 67.2 reduce-scatter.116
  4190.1 67.3 reduce-scatter.114
  4261.1 67.3 reduce-scatter.106
  4331.8 67.3 reduce-scatter.108
  4402.7 67.4 reduce-scatter.102
  4473.6 67.3 reduce-scatter.104
  4544.5 147.6 reduce-scatter.86
  4695.7 146.5 reduce-scatter.88
  4845.8 146.5 reduce-scatter.82
  4995.8 146.5 reduce-scatter.84
  5147.3 86.5 all-reduce.16
where the time goes:
time: 5260 us; the launch traced here: 5250 us
  local copies, waits for them, and re-layouts  2060 us (39%)
  waiting for transfers between devices  1640 us (31%)
  matrix products  1070 us (20%)
  other arithmetic  303 us (6%)
  blocking collectives  147 us (3%)
    gather x2, local copies, waits for them, and re-layouts, body(): buckets = jnp.take(bucket_table, distance)  1450 us
    unnamed x66, waiting for transfers between devices  554 us
    reduce_scatter x2, waiting for transfers between devices, reduce_grads(): lax.psum_scatter(grads[14].astype(jnp.bfloat16), 'fsdp', scatter_dimensio...  299 us
    reduce_scatter x2, waiting for transfers between devices, reduce_grads(): lax.psum_scatter(grads[13].astype(jnp.bfloat16), 'fsdp', scatter_dimensio...  297 us
    dot_general x22, matrix products, matmul(): return jnp.dot(left, right, preferred_element_type=jnp.float32)  161 us
    unnamed x750, local copies, waits for them, and re-layouts  151 us
    reduce_scatter x2, waiting for transfers between devices, reduce_grads(): lax.psum_scatter(grads[7].astype(jnp.bfloat16), 'fsdp', scatter_dimension...  140 us
    reduce_scatter x2, waiting for transfers between devices, reduce_grads(): lax.psum_scatter(grads[4].astype(jnp.bfloat16), 'fsdp', scatter_dimension...  140 us
  transfers between devices with their start and end apart: 50, of which 22 were waited for; matrix products, arithmetic and copies ran while one was open for 58% of the time, Pallas kernels for 0%

commit v1 on v0

v1 whole, which is shorter than its diff:
```python
import functools
import jax
import jax.numpy as jnp
from jax import lax
from jax.sharding import PartitionSpec as P
from jax.experimental import pallas as pl
from jax.experimental.pallas import tpu as pltpu

HEAD_DIM = 64
BUCKETS = 32
BLK = 32
CHUNK = 256
FILLER = -1e30
SCALE = HEAD_DIM ** (-0.5)
LIMIT = 60 * 1024 * 1024
F32 = jnp.float32
BF16 = jnp.bfloat16


def dot_nt(left, right):
    return lax.dot_general(left, right, (((1,), (1,)), ((), ())), preferred_element_type=F32)


def dot_tn(left, right):
    return lax.dot_general(left, right, (((0,), (0,)), ((), ())), preferred_element_type=F32)


def dot_nn(left, right):
    return jnp.dot(left, right, preferred_element_type=F32)


def low_lanes(rows):
    return lax.broadcasted_iota(jnp.int32, (rows, 128), 1) < HEAD_DIM


def pair_rows(value, low):
    zero = jnp.zeros_like(value)
    return jnp.concatenate([jnp.where(low, value, zero), jnp.where(low, zero, value)], axis=0)


def self_parts(place, query_ref, own_key_ref, own_value_ref):
    slot, pair = place // 2, place % 2
    rows = pl.ds(pl.multiple_of(slot * BLK, BLK), BLK)
    lanes = pl.ds(pl.multiple_of(pair * 128, 128), 128)
    total = query_ref.shape[0] * BLK
    low = low_lanes(total)
    query = query_ref[:, 0, rows, lanes].reshape(total, 128)
    pairs = pair_rows(query, low) * jnp.asarray(SCALE, BF16)
    zero = jnp.zeros((BLK, 128), F32)
    own_key = own_key_ref[:, 0, rows, lanes].reshape(total - BLK, 128).astype(F32)
    own_key = jnp.concatenate([zero, own_key], axis=0)
    own_value = own_value_ref[:, 0, rows, lanes].reshape(total - BLK, 128).astype(F32)
    own_value = jnp.concatenate([zero, own_value], axis=0)
    return slot, pair, rows, lanes, low, pairs, own_key, own_value


def self_forward_kernel(
    blocks,
    own_ref,
    query_ref,
    rel_ref,
    own_key_ref,
    own_value_ref,
    key_ref,
    value_ref,
    index_ref,
    out_ref,
    prob_ref,
    own_prob_ref,
):
    seq = key_ref.shape[1]
    streams = query_ref.shape[0]
    total = streams * BLK

    def step(place, carry):
        slot, pair, rows, lanes, low, pairs, own_key, own_value = self_parts(
            place, query_ref, own_key_ref, own_value_ref
        )
        block = blocks[slot]
        rel = rel_ref[:, 0, rows, :].reshape(total, 128).astype(F32)
        table = jnp.concatenate(
            [pltpu.roll(rel, pair * 64, 1), pltpu.roll(rel, pair * 64 + 96, 1)], axis=0
        )
        lane = lax.broadcasted_iota(jnp.int32, (2 * total, 128), 1)
        own = jnp.where(lane == own_ref[0], table, 0.0)
        own = own + pairs.astype(F32) * jnp.concatenate([own_key, own_key], axis=0)
        own = jnp.sum(own, axis=1, keepdims=True)
        row = lax.broadcasted_iota(jnp.int32, (2 * total, 1), 0)
        main = jnp.logical_or(row < BLK, jnp.logical_and(row >= total, row < total + BLK))
        own = jnp.where(main, FILLER, own)
        count = (block * BLK) // CHUNK + 1
        for parts in range(1, seq // CHUNK + 1):
            width = parts * CHUNK

            @pl.when(count == parts)
            def _():
                span = slice(seq - width, seq)
                index = index_ref[rows, span]
                bias = [
                    jnp.take_along_axis(
                        table,
                        jnp.concatenate([index[:, start : start + 128]] * (2 * streams), axis=0),
                        axis=1,
                    )
                    for start in range(0, width, 128)
                ]
                scores = dot_nt(pairs, key_ref[0, span, lanes]) + jnp.concatenate(bias, axis=1)
                column = lax.broadcasted_iota(jnp.int32, (2 * total, CHUNK), 1)
                seen = column >= width - BLK * (block + 1)
                first = jnp.where(seen, scores[:, :CHUNK], FILLER)
                scores = (
                    jnp.concatenate([first, scores[:, CHUNK:]], axis=1) if parts > 1 else first
                )
                top = jnp.maximum(jnp.max(scores, axis=1, keepdims=True), own)
                weights = jnp.exp(scores - top)
                own_weight = jnp.exp(own - top)
                inverse = 1.0 / (jnp.sum(weights, axis=1, keepdims=True) + own_weight)
                probs = (weights * inverse).astype(BF16)
                prob_ref[0, pair, slot, :, span] = probs
                own_prob = own_weight * inverse
                own_prob_ref[0, pair, slot] = jnp.broadcast_to(own_prob, (2 * total, 128)).astype(
                    BF16
                )
                mixed = dot_nn(probs, value_ref[0, span, lanes])
                result = jnp.where(
                    low,
                    mixed[:total] + own_prob[:total] * own_value,
                    mixed[total:] + own_prob[total:] * own_value,
                )
                out_ref[:, 0, rows, lanes] = result.astype(BF16).reshape(streams, BLK, 128)

        return carry

    lax.fori_loop(0, 2 * blocks.shape[0], step, 0)


def self_backward_kernel(
    blocks,
    own_ref,
    query_ref,
    own_key_ref,
    own_value_ref,
    key_ref,
    value_ref,
    hot_ref,
    out_ref,
    grad_ref,
    prob_ref,
    own_prob_ref,
    grad_query_ref,
    grad_rel_ref,
    grad_own_key_ref,
    grad_own_value_ref,
    grad_key_ref,
    grad_value_ref,
    key_total,
    value_total,
):
    seq = key_ref.shape[1]
    streams = query_ref.shape[0]
    total = streams * BLK
    key_total[...] = jnp.zeros_like(key_total)
    value_total[...] = jnp.zeros_like(value_total)

    def step(place, carry):
        slot, pair, rows, lanes, low, pairs, own_key, own_value = self_parts(
            place, query_ref, own_key_ref, own_value_ref
        )
        block = blocks[slot]
        grads = pair_rows(grad_ref[:, 0, rows, lanes].reshape(total, 128), low)
        wide = grads.astype(F32)
        mixed = out_ref[:, 0, rows, lanes].reshape(total, 128).astype(F32)
        delta = jnp.sum(wide * jnp.concatenate([mixed, mixed], axis=0), axis=1, keepdims=True)
        grad_own = jnp.sum(
            wide * jnp.concatenate([own_value, own_value], axis=0), axis=1, keepdims=True
        )
        own_prob = own_prob_ref[0, pair, slot].astype(F32)
        grad_own = own_prob * (grad_own - delta)
        part = grad_own * pairs.astype(F32)
        part = (part[:total] + part[total:])[BLK:]
        grad_own_key_ref[:, 0, rows, lanes] = part.astype(BF16).reshape(streams - 1, BLK, 128)
        part = own_prob * wide
        part = (part[:total] + part[total:])[BLK:]
        grad_own_value_ref[:, 0, rows, lanes] = part.astype(BF16).reshape(streams - 1, BLK, 128)
        count = (block * BLK) // CHUNK + 1
        for parts in range(1, seq // CHUNK + 1):
            width = parts * CHUNK

            @pl.when(count == parts)
            def _():
                span = slice(seq - width, seq)
                probs = prob_ref[0, pair, slot, :, span]
                grad_probs = dot_nt(grads, value_ref[0, span, lanes])
                grad_scores = probs.astype(F32) * (grad_probs - delta)
                low_scores = grad_scores.astype(BF16)
                value_total[span, lanes] += dot_tn(probs, grads)
                key_total[span, lanes] += dot_tn(low_scores, pairs)
                moved = dot_nn(low_scores, key_ref[0, span, lanes])
                moved = jnp.where(
                    low,
                    moved[:total] + grad_own[:total] * own_key,
                    moved[total:] + grad_own[total:] * own_key,
                )
                grad_query_ref[:, 0, rows, lanes] = (
                    (moved * SCALE).astype(BF16).reshape(streams, BLK, 128)
                )
                pad = jnp.zeros((BLK, 128), F32)
                skewed = []
                for start in range(0, 2 * total, BLK):
                    piece = jnp.concatenate([grad_scores[start : start + BLK], pad], axis=1)
                    skewed.append(pltpu.roll(piece, 0, 1, stride=1, stride_axis=0).astype(BF16))
                begin = pl.multiple_of(BLK * (block + 1) - width + CHUNK, BLK)
                hots = hot_ref[pl.ds(begin, width + 128), :]
                sums = dot_nn(jnp.concatenate(skewed, axis=0), hots)
                lane = lax.broadcasted_iota(jnp.int32, (2 * total, 128), 1)
                sums = sums + jnp.where(lane == own_ref[0], grad_own, 0.0)
                sums = pltpu.roll(sums[:total], pair * 64, 1) + pltpu.roll(
                    sums[total:], pair * 64 + BUCKETS, 1
                )
                lane = lax.broadcasted_iota(jnp.int32, (total, 128), 1)
                mine = jnp.logical_and(lane >= 64 * pair, lane < 64 * pair + 64)
                before = grad_rel_ref[:, 0, rows, :].reshape(total, 128)
                sums = jnp.where(mine, sums.astype(BF16), before)
                grad_rel_ref[:, 0, rows, :] = sums.reshape(streams, BLK, 128)

        return carry

    lax.fori_loop(0, 2 * blocks.shape[0], step, 0)
    grad_key_ref[0] = key_total[...].astype(BF16)
    grad_value_ref[0] = value_total[...].astype(BF16)


def group_spec(streams, rows, lanes):
    return pl.BlockSpec((streams, 1, rows, lanes), lambda n, g: (0, n, 0, g))


def full_spec(rows, lanes):
    return pl.BlockSpec((1, rows, lanes), lambda n, g: (n, 0, g))


def smem_spec():
    return pl.BlockSpec(memory_space=pltpu.SMEM)


def estimate(flops, moved):
    return pl.CostEstimate(flops=int(flops), bytes_accessed=int(moved), transcendentals=0)


def prob_spec(slots, total, width):
    return pl.BlockSpec((1, 2, slots, total, width), lambda n, g: (n, g, 0, 0, 0))


def whole_spec(value):
    return pl.BlockSpec(value.shape, lambda n, g: (0,) * value.ndim)


def self_forward(blocks, own, query, rel, own_key, own_value, keys, values, index):
    streams, seqs, rows, width = query.shape
    seq = keys.shape[1]
    slots = rows // BLK
    total = 2 * streams * BLK
    return pl.pallas_call(
        self_forward_kernel,
        grid=(seqs, width // 256),
        in_specs=[
            smem_spec(),
            smem_spec(),
            group_spec(streams, rows, 256),
            group_spec(streams, rows, 128),
            group_spec(streams - 1, rows, 256),
            group_spec(streams - 1, rows, 256),
            full_spec(seq, 256),
            full_spec(seq, 256),
            whole_spec(index),
        ],
        out_specs=[
            group_spec(streams, rows, 256),
            prob_spec(slots, total, seq),
            prob_spec(slots, total, 128),
        ],
        out_shape=[
            jax.ShapeDtypeStruct(query.shape, BF16),
            jax.ShapeDtypeStruct((seqs, width // 128, slots, total, seq), BF16),
            jax.ShapeDtypeStruct((seqs, width // 128, slots, total, 128), BF16),
        ],
        compiler_params=pltpu.CompilerParams(vmem_limit_bytes=LIMIT),
        cost_estimate=estimate(40e9, 80e6),
        name="self_forward",
    )(blocks, own, query, rel, own_key, own_value, keys, values, index)


def self_backward(
    blocks, own, query, own_key, own_value, keys, values, hot, mixed, grad, probs, own_probs
):
    streams, seqs, rows, width = query.shape
    seq = keys.shape[1]
    slots = rows // BLK
    total = 2 * streams * BLK
    return pl.pallas_call(
        self_backward_kernel,
        grid=(seqs, width // 256),
        in_specs=[
            smem_spec(),
            smem_spec(),
            group_spec(streams, rows, 256),
            group_spec(streams - 1, rows, 256),
            group_spec(streams - 1, rows, 256),
            full_spec(seq, 256),
            full_spec(seq, 256),
            whole_spec(hot),
            group_spec(streams, rows, 256),
            group_spec(streams, rows, 256),
            prob_spec(slots, total, seq),
            prob_spec(slots, total, 128),
        ],
        out_specs=[
            group_spec(streams, rows, 256),
            group_spec(streams, rows, 128),
            group_spec(streams - 1, rows, 256),
            group_spec(streams - 1, rows, 256),
            full_spec(seq, 256),
            full_spec(seq, 256),
        ],
        out_shape=[
            jax.ShapeDtypeStruct(query.shape, BF16),
            jax.ShapeDtypeStruct((streams, seqs, rows, width // 2), BF16),
            jax.ShapeDtypeStruct(own_key.shape, BF16),
            jax.ShapeDtypeStruct(own_key.shape, BF16),
            jax.ShapeDtypeStruct(keys.shape, BF16),
            jax.ShapeDtypeStruct(keys.shape, BF16),
        ],
        scratch_shapes=[pltpu.VMEM((seq, 256), F32), pltpu.VMEM((seq, 256), F32)],
        compiler_params=pltpu.CompilerParams(vmem_limit_bytes=LIMIT),
        cost_estimate=estimate(90e9, 100e6),
        name="self_backward",
    )(blocks, own, query, own_key, own_value, keys, values, hot, mixed, grad, probs, own_probs)


def cross_forward_kernel(query_ref, key_ref, value_ref, out_ref, prob_ref):
    rows = query_ref.shape[2]
    low = low_lanes(rows)
    for pair in range(2):
        lanes = slice(128 * pair, 128 * pair + 128)
        pairs = pair_rows(query_ref[0, 0, :, lanes], low) * jnp.asarray(SCALE, BF16)
        scores = dot_nt(pairs, key_ref[0, :, lanes])
        top = jnp.max(scores, axis=1, keepdims=True)
        weights = jnp.exp(scores - top)
        inverse = 1.0 / jnp.sum(weights, axis=1, keepdims=True)
        probs = (weights * inverse).astype(BF16)
        prob_ref[0, 0, pair] = probs
        mixed = dot_nn(probs, value_ref[0, :, lanes])
        out_ref[0, 0, :, lanes] = jnp.where(low, mixed[:rows], mixed[rows:]).astype(BF16)


def cross_backward_kernel(
    query_ref,
    key_ref,
    value_ref,
    out_ref,
    grad_ref,
    prob_ref,
    grad_query_ref,
    grad_key_ref,
    grad_value_ref,
    key_total,
    value_total,
):
    rows = query_ref.shape[2]
    low = low_lanes(rows)
    stream = pl.program_id(2)

    @pl.when(stream == 0)
    def _():
        key_total[...] = jnp.zeros_like(key_total)
        value_total[...] = jnp.zeros_like(value_total)

    for pair in range(2):
        lanes = slice(128 * pair, 128 * pair + 128)
        pairs = pair_rows(query_ref[0, 0, :, lanes], low) * jnp.asarray(SCALE, BF16)
        keys = key_ref[0, :, lanes]
        grads = pair_rows(grad_ref[0, 0, :, lanes], low)
        mixed = out_ref[0, 0, :, lanes].astype(F32)
        delta = jnp.sum(
            grads.astype(F32) * jnp.concatenate([mixed, mixed], axis=0), axis=1, keepdims=True
        )
        probs = prob_ref[0, 0, pair]
        grad_probs = dot_nt(grads, value_ref[0, :, lanes])
        grad_scores = (probs.astype(F32) * (grad_probs - delta)).astype(BF16)
        value_total[:, lanes] += dot_tn(probs, grads)
        key_total[:, lanes] += dot_tn(grad_scores, pairs)
        moved = dot_nn(grad_scores, keys) * SCALE
        grad_query_ref[0, 0, :, lanes] = jnp.where(low, moved[:rows], moved[rows:]).astype(BF16)

    @pl.when(stream == pl.num_programs(2) - 1)
    def _():
        grad_key_ref[0] = key_total[...].astype(BF16)
        grad_value_ref[0] = value_total[...].astype(BF16)


def stream_spec(rows):
    return pl.BlockSpec((1, 1, rows, 256), lambda n, g, s: (s, n, 0, g))


def memory_spec(rows):
    return pl.BlockSpec((1, rows, 256), lambda n, g, s: (n, 0, g))


def cross_prob_spec(rows, memory):
    return pl.BlockSpec((1, 1, 2, 2 * rows, memory), lambda n, g, s: (s, n, g, 0, 0))


def cross_forward(query, keys, values):
    streams, seqs, rows, width = query.shape
    memory = keys.shape[1]
    return pl.pallas_call(
        cross_forward_kernel,
        grid=(seqs, width // 256, streams),
        in_specs=[stream_spec(rows), memory_spec(memory), memory_spec(memory)],
        out_specs=[stream_spec(rows), cross_prob_spec(rows, memory)],
        out_shape=[
            jax.ShapeDtypeStruct(query.shape, BF16),
            jax.ShapeDtypeStruct((streams, seqs, width // 128, 2 * rows, memory), BF16),
        ],
        compiler_params=pltpu.CompilerParams(vmem_limit_bytes=LIMIT),
        cost_estimate=estimate(26e9, 20e6),
        name="cross_forward",
    )(query, keys, values)


def cross_backward(query, keys, values, mixed, grad, probs):
    streams, seqs, rows, width = query.shape
    memory = keys.shape[1]
    return pl.pallas_call(
        cross_backward_kernel,
        grid=(seqs, width // 256, streams),
        in_specs=[
            stream_spec(rows),
            memory_spec(memory),
            memory_spec(memory),
            stream_spec(rows),
            stream_spec(rows),
            cross_prob_spec(rows, memory),
        ],
        out_specs=[stream_spec(rows), memory_spec(memory), memory_spec(memory)],
        out_shape=[
            jax.ShapeDtypeStruct(query.shape, BF16),
            jax.ShapeDtypeStruct(keys.shape, BF16),
            jax.ShapeDtypeStruct(keys.shape, BF16),
        ],
        scratch_shapes=[pltpu.VMEM((memory, 256), F32), pltpu.VMEM((memory, 256), F32)],
        compiler_params=pltpu.CompilerParams(vmem_limit_bytes=LIMIT),
        cost_estimate=estimate(60e9, 30e6),
        name="cross_backward",
    )(query, keys, values, mixed, grad, probs)


def bucket_index(own_blocks, bucket_table, seq):
    span = bucket_table.shape[0]
    front = seq - BLK
    length = 2 * seq + BLK
    line = jnp.zeros((length,), jnp.int32).at[front : front + span].set(bucket_table)
    flat = jnp.tile(line, BLK + 1)[: BLK * (length + 1)]
    skew = flat.reshape(BLK, length + 1)
    parts = [
        lax.dynamic_slice_in_dim(skew, own_blocks[slot] * BLK, seq, axis=1)
        for slot in range(own_blocks.shape[0])
    ]
    return jnp.concatenate(parts, axis=0)


def bucket_hots(bucket_table, seq, front):
    span = bucket_table.shape[0]
    depth = CHUNK + seq + 128
    line = jnp.full((front + span + depth,), -1, jnp.int32)
    line = line.at[front : front + span].set(bucket_table)[:depth]
    lane = jnp.arange(128, dtype=jnp.int32)
    return (line[:, None] == lane[None, :]).astype(BF16)


EPSILON = 1e-05
FULL = ("fsdp", "ctx")


def gather(shard, ranks):
    rows = shard.shape[0] // ranks
    piece = lax.dynamic_slice_in_dim(shard, lax.axis_index("ctx") * rows, rows)
    return lax.all_gather(piece, FULL, axis=0, tiled=True)


def reduce_rows(grad):
    piece = lax.psum_scatter(grad.astype(BF16), FULL, scatter_dimension=0, tiled=True)
    return lax.all_gather(piece, "ctx", axis=0, tiled=True).astype(F32)


def flat(value):
    return value.reshape(-1, value.shape[-1])


def normalize(values):
    average = jnp.mean(values, axis=-1, keepdims=True)
    centred = values - average
    variance = jnp.mean(centred * centred, axis=-1, keepdims=True)
    rate = lax.rsqrt(variance + EPSILON)
    return centred * rate, rate


def norm_back(grad, normal, rate, gain):
    inner = grad * gain
    first = jnp.mean(inner, axis=-1, keepdims=True)
    second = jnp.mean(inner * normal, axis=-1, keepdims=True)
    back = (inner - first - normal * second) * rate
    return back, jnp.sum(grad * normal, axis=0), jnp.sum(grad, axis=0)


def gelu_parts(inner):
    share = 0.5 * (1.0 + lax.erf(inner * (0.5**0.5)))
    slope = share + inner * jnp.exp(-0.5 * inner * inner) * ((0.5 / jnp.pi) ** 0.5)
    return (inner * share).astype(BF16), slope.astype(BF16)


def head_major(weight):
    rows, width = weight.shape
    return weight.reshape(rows, BUCKETS, width // BUCKETS).transpose(0, 2, 1).reshape(rows, width)


def bucket_major(weight):
    rows, width = weight.shape
    return weight.reshape(rows, width // BUCKETS, BUCKETS).transpose(0, 2, 1).reshape(rows, width)


def body(
    ranks,
    hidden,
    encoded,
    assign,
    bucket_table,
    w_query,
    w_key,
    w_value,
    w_rel,
    w_out,
    gain_one,
    shift_one,
    c_query,
    c_key,
    c_value,
    c_out,
    gain_two,
    shift_two,
    w_inner,
    w_outer,
    gain_three,
    shift_three,
    cotangent,
):
    seqs, rows, streams, width = hidden.shape
    seq = rows * ranks
    rank = lax.axis_index("ctx")
    slots = rows // BLK
    own_blocks = lax.dynamic_slice_in_dim(assign, rank * slots, slots)
    own = bucket_table[BLK - 1 : BLK]
    index = bucket_index(own_blocks, bucket_table, seq)
    hot = bucket_hots(bucket_table, seq, CHUNK)
    places = (assign[:, None] * BLK + jnp.arange(BLK, dtype=jnp.int32)[None, :]).reshape(-1)
    order = (places[None, :] == (seq - 1 - jnp.arange(seq, dtype=jnp.int32))[:, None]).astype(BF16)

    full_main = gather(jnp.concatenate([w_query, head_major(w_rel), w_key, w_value], axis=1), ranks)
    cut = w_query.shape[1] + w_rel.shape[1]
    w_query, w_rel = full_main[:, :width], full_main[:, width:cut]
    w_key, w_value = full_main[:, cut : cut + width], full_main[:, cut + width :]
    norms = jnp.stack([gain_one, shift_one, gain_two, shift_two, gain_three, shift_three])
    norms = lax.all_gather(norms, "fsdp", axis=1, tiled=True).astype(F32)
    gain_one, shift_one, gain_two, shift_two, gain_three, shift_three = (
        norms[place : place + 1] for place in range(6)
    )
    main = lax.all_gather(hidden[:, :, 0, :], "ctx", axis=1, tiled=True)
    memory = lax.all_gather(encoded, "ctx", axis=1, tiled=True)
    w_out = gather(w_out, ranks)
    full_cross = gather(jnp.concatenate([c_key, c_value], axis=1), ranks)
    c_key, c_value = full_cross[:, :width], full_cross[:, width:]
    c_query = gather(c_query, ranks)
    c_out = gather(c_out, ranks)
    w_inner = gather(w_inner, ranks)
    w_outer = gather(w_outer, ranks)

    stacked = jnp.transpose(hidden, (2, 0, 1, 3))
    shape = stacked.shape
    lines = flat(stacked)
    own_shape = (streams - 1,) + shape[1:]
    own_lines = flat(stacked[1:])
    main = jnp.einsum("mu,nud->nmd", order, main, preferred_element_type=F32).astype(BF16)
    main_lines = flat(main)
    main_shape = main.shape
    query = dot_nn(lines, w_query).astype(BF16).reshape(shape)
    rel = dot_nn(lines, w_rel).astype(BF16).reshape(shape[:-1] + (-1,))
    own_keys = dot_nn(own_lines, w_key).astype(BF16).reshape(own_shape)
    own_values = dot_nn(own_lines, w_value).astype(BF16).reshape(own_shape)
    keys = dot_nn(main_lines, w_key).astype(BF16).reshape(main_shape)
    values = dot_nn(main_lines, w_value).astype(BF16).reshape(main_shape)
    mixed, probs, own_probs = self_forward(
        own_blocks, own, query, rel, own_keys, own_values, keys, values, index
    )
    normal_one, rate_one = normalize(lines.astype(F32) + dot_nn(flat(mixed), w_out))
    h_one = normal_one * gain_one + shift_one
    h_one_low = h_one.astype(BF16)
    cross_query = dot_nn(h_one_low, c_query).astype(BF16).reshape(shape)
    memory_lines = flat(memory)
    cross_keys = dot_nn(memory_lines, c_key).astype(BF16).reshape(memory.shape)
    cross_values = dot_nn(memory_lines, c_value).astype(BF16).reshape(memory.shape)
    cross_mixed, cross_probs = cross_forward(cross_query, cross_keys, cross_values)
    normal_two, rate_two = normalize(h_one + dot_nn(flat(cross_mixed), c_out))
    h_two = normal_two * gain_two + shift_two
    h_two_low = h_two.astype(BF16)
    active, slope = gelu_parts(dot_nn(h_two_low, w_inner))
    normal_three, rate_three = normalize(h_two + dot_nn(active, w_outer))
    output = (normal_three * gain_three + shift_three).astype(BF16)
    output = jnp.transpose(output.reshape(shape), (1, 2, 0, 3))

    grad = flat(jnp.transpose(cotangent, (2, 0, 1, 3))).astype(F32)
    grad_three, gain_three, shift_three = norm_back(grad, normal_three, rate_three, gain_three)
    grad_low = grad_three.astype(BF16)
    w_outer_grad = reduce_rows(dot_tn(active, grad_low))
    grad_inner = (dot_nt(grad_low, w_outer) * slope.astype(F32)).astype(BF16)
    w_inner_grad = reduce_rows(dot_tn(h_two_low, grad_inner))
    grad_h_two = grad_three + dot_nt(grad_inner, w_inner)
    grad_two, gain_two, shift_two = norm_back(grad_h_two, normal_two, rate_two, gain_two)
    grad_low = grad_two.astype(BF16)
    c_out_grad = reduce_rows(dot_tn(flat(cross_mixed), grad_low))
    grad_mixed = dot_nt(grad_low, c_out).astype(BF16).reshape(shape)
    cross_query_grad, key_grad, value_grad = cross_backward(
        cross_query, cross_keys, cross_values, cross_mixed, grad_mixed, cross_probs
    )
    cross_query_grad = flat(cross_query_grad)
    key_grad, value_grad = flat(key_grad), flat(value_grad)
    c_query_grad = reduce_rows(dot_tn(h_one_low, cross_query_grad))
    grad_h_one = grad_two + dot_nt(cross_query_grad, c_query)
    grad_one, gain_one, shift_one = norm_back(grad_h_one, normal_one, rate_one, gain_one)
    grad_low = grad_one.astype(BF16)
    w_out_grad = reduce_rows(dot_tn(flat(mixed), grad_low))
    grad_mixed = dot_nt(grad_low, w_out).astype(BF16).reshape(shape)
    cross_grad = reduce_rows(
        jnp.concatenate([dot_tn(memory_lines, key_grad), dot_tn(memory_lines, value_grad)], axis=1)
    )
    encoded_grad = (dot_nt(key_grad, c_key) + dot_nt(value_grad, c_value)).astype(BF16)
    encoded_grad = lax.psum_scatter(
        encoded_grad.reshape(memory.shape), "ctx", scatter_dimension=1, tiled=True
    ).astype(F32)
    query_grad, rel_grad, own_key_grad, own_value_grad, key_grad, value_grad = self_backward(
        own_blocks,
        own,
        query,
        own_keys,
        own_values,
        keys,
        values,
        hot,
        mixed,
        grad_mixed,
        probs,
        own_probs,
    )
    query_grad, rel_grad = flat(query_grad), flat(rel_grad)
    own_key_grad, own_value_grad = flat(own_key_grad), flat(own_value_grad)
    key_grad, value_grad = flat(key_grad), flat(value_grad)
    main_grad = (dot_nt(key_grad, w_key) + dot_nt(value_grad, w_value)).astype(BF16)
    main_grad = jnp.einsum(
        "mu,nmd->nud", order, main_grad.reshape(main_shape), preferred_element_type=F32
    ).astype(BF16)
    main_grad = lax.psum_scatter(main_grad, "ctx", scatter_dimension=1, tiled=True).astype(F32)
    full_grad = reduce_rows(
        jnp.concatenate(
            [
                dot_tn(lines, query_grad),
                dot_tn(lines, rel_grad),
                dot_tn(own_lines, own_key_grad) + dot_tn(main_lines, key_grad),
                dot_tn(own_lines, own_value_grad) + dot_tn(main_lines, value_grad),
            ],
            axis=1,
        )
    )
    own_grad = dot_nt(own_key_grad, w_key) + dot_nt(own_value_grad, w_value)
    grad_lines = grad_one + dot_nt(query_grad, w_query) + dot_nt(rel_grad, w_rel)
    grad_lines = grad_lines.reshape(shape) + jnp.concatenate(
        [main_grad[None], own_grad.reshape(own_shape)], axis=0
    )
    grad_hidden = jnp.transpose(grad_lines, (1, 2, 0, 3))
    norms = jnp.stack([gain_one, shift_one, gain_two, shift_two, gain_three, shift_three])
    norms = lax.psum_scatter(lax.psum(norms, "ctx"), "fsdp", scatter_dimension=1, tiled=True)
    gain_one, shift_one, gain_two, shift_two, gain_three, shift_three = (
        norms[place] for place in range(6)
    )
    return (
        output,
        grad_hidden,
        encoded_grad,
        full_grad[:, :width],
        full_grad[:, cut : cut + width],
        full_grad[:, cut + width :],
        bucket_major(full_grad[:, width:cut]),
        w_out_grad,
        gain_one,
        shift_one,
        c_query_grad,
        cross_grad[:, :width],
        cross_grad[:, width:],
        c_out_grad,
        gain_two,
        shift_two,
        w_inner_grad,
        w_outer_grad,
        gain_three,
        shift_three,
    )


def solution(mesh):
    matrix, vector = P("fsdp", None), P("fsdp")
    rows = P("fsdp", "ctx", None, None)
    weights = (matrix,) * 5 + (vector,) * 2 + (matrix,) * 4 + (vector,) * 2 + (matrix,) * 2
    weights = weights + (vector,) * 2
    in_specs = (rows, P("fsdp", "ctx", None), P(), P()) + weights + (rows,)
    out_specs = (rows, rows, P("fsdp", "ctx", None)) + weights
    return jax.shard_map(
        functools.partial(body, mesh.shape["ctx"]),
        mesh=mesh,
        in_specs=in_specs,
        out_specs=out_specs,
        check_vma=False,
    )
```

time: 5260 us -> 1780 us (0.34)
  local copies, waits for them, and re-layouts: 2060 us -> 77 us
  waiting for transfers between devices: 1640 us -> 851 us
  matrix products: 1070 us -> 340 us
  Pallas kernels: 0 us -> 341 us
  other arithmetic: 303 us -> 53.5 us
  blocking collectives: 147 us -> 85.8 us
    gather x2 -> x0, local copies, waits for them, and re-layouts: 1450 us -> none  [body(): buckets = jnp.take(bucket_table, distance)]
    dot_general x124 -> x41, matrix products: 1050 us -> 340 us  [the longest x13 119 us: dot_nt(): lax.dot_general(left, right, (((1,), (1,)), ((), ())), preferred_element_...]
    unnamed x66 -> x21, waiting for transfers between devices: 554 us -> 1.02 us
    pallas_call x0 -> x4, Pallas kernels: none -> 341 us  [the longest x1 137 us: self_forward(): pl.pallas_call(self_forward_kernel, grid=(seqs, width // 256), in_specs=[...]
    reduce_scatter x14 -> x10, waiting for transfers between devices: 883 us -> 644 us  [the longest x7 577 us: reduce_rows(): lax.psum_scatter(grad.astype(BF16), FULL, scatter_dimension=0, tiled=True)]
    convert_element_type x62 -> x8, other arithmetic: 165 us -> 13.8 us  [the longest x5 8.08 us: reduce_rows(): return lax.all_gather(piece, 'ctx', axis=0, tiled=True).astype(F32)]
    convert_element_type x36 -> x3, local copies, waits for them, and re-layouts: 126 us -> 10.8 us  [the longest x1 4.69 us: body(): query = dot_nn(lines, w_query).astype(BF16).reshape(shape)]
    unnamed x750 -> x183, local copies, waits for them, and re-layouts: 151 us -> 45.2 us
  transfers between devices with their start and end apart: 50 -> 21, of which waited for: 22 -> 13; matrix products, arithmetic and copies ran while one was open for 58% -> 23% of each run, Pallas kernels for 0% -> 19%
where the time goes in v1:
time: 1780 us; the launch traced here: 1770 us
  waiting for transfers between devices  851 us (48%)
  Pallas kernels  341 us (19%)
  matrix products  340 us (19%)
  blocking collectives  85.8 us (5%)
  local copies, waits for them, and re-layouts  77 us (4%)
  other arithmetic  53.5 us (3%)
  between operations  21.3 us (1%)
    reduce_scatter x7, waiting for transfers between devices, reduce_rows(): lax.psum_scatter(grad.astype(BF16), FULL, scatter_dimension=0, tiled=True)  577 us
    all_gather x7, waiting for transfers between devices, gather(): return lax.all_gather(piece, FULL, axis=0, tiled=True)  189 us
    pallas_call x1, Pallas kernels, self_forward(): pl.pallas_call(self_forward_kernel, grid=(seqs, width // 256), in_specs=[...  137 us
    pallas_call x1, Pallas kernels, self_backward(): pl.pallas_call(self_backward_kernel, grid=(seqs, width // 256), in_specs=...  128 us
    dot_general x13, matrix products, dot_nt(): lax.dot_general(left, right, (((1,), (1,)), ((), ())), preferred_element_...  119 us
    dot_general x13, matrix products, dot_nn(): return jnp.dot(left, right, preferred_element_type=F32)  114 us
    dot_general x13, matrix products, dot_tn(): lax.dot_general(left, right, (((0,), (0,)), ((), ())), preferred_element_...  91.5 us
    all_gather x5, blocking collectives, reduce_rows(): return lax.all_gather(piece, 'ctx', axis=0, tiled=True).astype(F32)  57 us
  transfers between devices with their start and end apart: 21, of which 13 were waited for; matrix products, arithmetic and copies ran while one was open for 23% of the time, Pallas kernels for 19%

profile of v1, /device:TPU:1, one launch (start us, length us, event | category | flops | bytes accessed | tf_op | source)
XLA Modules:
  0.0 1771.8 jit_solution(396378492316078148)
XLA Ops:
  31.8 22.9 %all_gather.54 = bf16[6,1024]{1,0:T(8,128)(2,1)S(1)} all-gather(bf16[6,128]{1,0:T(8,128)(2,1)S(1)} %stack.48), channel_id=1, replica_groups=mesh['ctx'=4,'fsdp'=8] {'fsdp'}, dimensions={1}, use_global_device_ids=true | all-gather | bytes 13824 | tf_op jit(solution)/shard_map/all_gather | solution.py:572
  69.9 9.0 fusion.29
  78.9 60.2 %all-gather.19.cloned.1.call-done = bf16[1024,2048]{1,0:T(8,128)(2,1)} async-done(((bf16[32,2048]{1,0:T(8,128)(2,1)}), bf16[1024,2048]{1,0:T(8,128)(2,1)}) %all-gather.19.cloned.1.call-update) | async-done | bytes 4194320 | tf_op jit(solution)/shard_map/all_gather | solution.py:487
  139.1 6.0 convolution_convert_fusion.10
  148.8 65.4 %all-gather.13.cloned.1.call-done = bf16[1024,3584]{1,0:T(8,128)(2,1)} async-done(((bf16[32,3584]{1,0:T(8,128)(2,1)}), bf16[1024,3584]{1,0:T(8,128)(2,1)}) %all-gather.13.cloned.1.call-update) | async-done | bytes 7340048 | tf_op jit(solution)/shard_map/all_gather | solution.py:487
  214.2 7.6 fusion.25
  221.8 4.7 copy.124
  226.5 5.2 fusion.26
  234.5 5.4 convolution_convert_fusion.12
  239.9 5.4 convolution_convert_fusion.11
  245.4 6.3 convolution_convert_fusion.7
  251.7 6.3 convolution_convert_fusion.6
  258.0 137.0 %self_forward.1 = (bf16[3,2,256,1024]{3,2,1,0:T(8,128)(2,1)}, bf16[2,8,8,192,1024]{4,3,2,1,0:T(8,128)(2,1)}, bf16[2,8,8,192,128]{4,3,2,1,0:T(8,128)(2,1)}) custom-call(s32[8]{0:T(128)} %copy-done.31, s32[1]{0:T(128)} %slice.133.own_ref, bf16[3,2,256,1024]{3,2,1,0:T(8,128)(2,1)} %bitcast.254, bf16[3,2,256,512]{3,2,1,0:T(8,128)(2,1)} %bitcast.260, ...), custom_call_target="tpu_custom_call" | custom-call | flops 40000000000 | bytes 80000000 | tf_op jit(solution)/shard_map/self_forward/pallas_call | solution.py:262
  395.0 7.2 fusion.88
  405.8 8.8 convolution_convert_fusion.4
  414.6 33.9 %cross_forward.1 = (bf16[3,2,256,1024]{3,2,1,0:T(8,128)(2,1)}, bf16[3,2,8,512,512]{4,3,2,1,0:T(8,128)(2,1)}) custom-call(bf16[3,2,256,1024]{3,2,1,0:T(8,128)(2,1)} %bitcast.316, bf16[2,512,1024]{2,1,0:T(8,128)(2,1)} %bitcast.328, bf16[2,512,1024]{2,1,0:T(8,128)(2,1)} %bitcast.330), custom_call_target="tpu_custom_call" | custom-call | flops 25999998976 | bytes 20000000 | tf_op jit(solution)/shard_map/cross_forward/pallas_call | solution.py:415
  448.5 8.8 fusion.89
  460.8 8.1 all-gather.25.cloned.1.call-done
  468.9 24.1 %multiply_convert_fusion.1 = (bf16[1536,4096]{1,0:T(8,128)(2,1)}, f32[1536,4096]{1,0:T(8,128)}) fusion(bf16[1024,4096]{1,0:T(8,128)(2,1)} %all-gather.25.cloned.1.call-done, f32[1536,1024]{1,0:T(8,128)} %copy-done.2, f32[1024]{0:T(1024)S(1)} %bitcast.288, f32[1024]{0:T(1024)S(1)} %bitcast.274, f32[1536]{0:T(1024)S(1)} %add_rsqrt_fusion.1, ...), kind=kOutput, calls=%fused_computation.7 | convolution fusion | flops 12924223488 | bytes 52449280 | tf_op jit(solution)/shard_map/dot_general | solution.py:29
  493.0 55.0 %all-gather.27.cloned.1.call-done = bf16[4096,1024]{1,0:T(8,128)(2,1)} async-done(((bf16[128,1024]{1,0:T(8,128)(2,1)}), bf16[4096,1024]{1,0:T(8,128)(2,1)}) %all-gather.27.cloned.1.call-update) | async-done | bytes 8388624 | tf_op jit(solution)/shard_map/all_gather | solution.py:487
  548.0 19.5 %fusion.90 = (f32[1536]{0:T(1024)S(1)}, f32[1536,1024]{1,0:T(8,128)S(1)}) fusion(bf16[1536,4096]{1,0:T(8,128)(2,1)} %get-tuple-element.197, bf16[4096,1024]{1,0:T(8,128)(2,1)} %all-gather.27.cloned.1.call-done, f32[1024]{0:T(1024)S(1)} %bitcast.289, f32[1024]{0:T(1024)S(1)} %bitcast.275, f32[1536]{0:T(1024)S(1)} %add_rsqrt_fusion.1, ...), kind=kOutput, calls=%fused_computation.186 | convolution fusion | flops 12894337024 | bytes 33581056 | tf_op jit(solution)/shard_map/dot_general | solution.py:29
  571.5 4.2 subtract_multiply_fusion.2
  578.4 18.4 %convolution_convert_fusion = bf16[4096,1024]{1,0:T(8,128)(2,1)} fusion(bf16[1536,4096]{1,0:T(8,128)(2,1)} %get-tuple-element.197, f32[1536,1024]{1,0:T(8,128)S(1)} %get-tuple-element.164), kind=kOutput, calls=%fused_computation.13 | convolution fusion | flops 12890669056 | bytes 27262976 | tf_op jit(solution)/shard_map/dot_general | solution.py:25
  596.8 28.3 %multiply_convert_fusion = bf16[1536,4096]{1,0:T(8,128)(2,1)} fusion(bf16[4096,1024]{1,0:T(8,128)(2,1)} %all-gather.27.cloned.1.call-done, f32[1536,4096]{1,0:T(8,128)} %get-tuple-element.198, f32[1536,1024]{1,0:T(8,128)} %copy-done.10), kind=kOutput, calls=%fused_computation.6 | convolution fusion | flops 12961972224 | bytes 52428800 | tf_op jit(solution)/shard_map/dot_general | solution.py:21
  625.1 22.0 %multiply_reduce_fusion = (f32[1024]{0:T(1024)S(1)}, f32[1536]{0:T(1024)S(1)}, f32[1536]{0:T(1024)S(1)}, f32[1024]{0:T(1024)S(1)}, f32[1536,1024]{1,0:T(8,128)}) fusion(f32[1536,1024]{1,0:T(8,128)S(1)} %bitcast.242, f32[1536]{0:T(1024)S(1)} %add_rsqrt_fusion.1, f32[1536]{0:T(1024)S(1)} %broadcast_multiply_fusion.6, f32[1024]{0:T(1024)S(1)} %bitcast.276, ...), kind=kOutput, calls=%fused_computation.22 | convolution fusion | flops 12900625408 | bytes 39882752 | tf_op jit(solution)/shard_map/dot_general | solution.py:21
  647.1 4.8 subtract_multiply_fusion.1
  651.9 5.0 convolution_convert_fusion.3
  656.9 42.4 %cross_backward.1 = (bf16[3,2,256,1024]{3,2,1,0:T(8,128)(2,1)}, bf16[2,512,1024]{2,1,0:T(8,128)(2,1)}, bf16[2,512,1024]{2,1,0:T(8,128)(2,1)}) custom-call(bf16[3,2,256,1024]{3,2,1,0:T(8,128)(2,1)} %bitcast.317, bf16[2,512,1024]{2,1,0:T(8,128)(2,1)} %bitcast.329, bf16[2,512,1024]{2,1,0:T(8,128)(2,1)} %bitcast.331, ...), custom_call_target="tpu_custom_call" | custom-call | flops 60000002048 | bytes 30000000 | tf_op jit(solution)/shard_map/cross_backward/pallas_call | solution.py:433
  699.3 11.3 multiply_reduce_fusion.1
  711.3 8.7 convolution_convert_fusion.13
  720.1 9.2 convolution_convert_fusion.14
  729.3 6.0 subtract_multiply_fusion
  738.1 4.7 convolution_convert_fusion.15
  743.9 4.1 fusion.40
  751.8 7.9 convolution_convert_fusion.2
  759.7 128.1 %self_backward.1 = (bf16[3,2,256,1024]{3,2,1,0:T(8,128)(2,1)}, bf16[3,2,256,512]{3,2,1,0:T(8,128)(2,1)}, bf16[2,2,256,1024]{3,2,1,0:T(8,128)(2,1)}, bf16[2,2,256...) custom-call(s32[8]{0:T(128)} %copy-done.31, s32[1]{0:T(128)} %slice.133.own_ref, ...), custom_call_target="tpu_custom_call" | custom-call | flops 89999998976 | bytes 100000000 | tf_op jit(solution)/shard_map/self_backward/pallas_call | solution.py:299
  887.8 7.2 fusion.62
  895.0 6.4 add_convert_fusion
  901.5 6.6 convert_bitcast_fusion.1
  908.8 21.7 %convolution_convert_fusion.1 = bf16[1024,4096]{1,0:T(8,128)(2,1)} fusion(bf16[1536,4096]{1,0:T(8,128)(2,1)} %multiply_convert_fusion, f32[1536,1024]{1,0:T(8,128)} %copy-done.2, f32[1024]{0:T(1024)S(1)} %bitcast.290, f32[1024]{0:T(1024)S(1)} %bitcast.278, f32[1536]{0:T(1024)S(1)} %copy-done.28, f32[1536]{0:T(1024)S(1)} %copy-done.21), kind=kOutput, calls=%fused_computation.14 | convolution fusion | flops 12896960512 | bytes 27283456 | tf_op jit(solution)/shard_map/dot_general | solution.py:25
  932.1 4.1 fusion.46
  941.1 6.5 copy.165
  953.5 4.7 fusion.14
  960.9 5.0 fusion.16
  976.2 10.1 copy.163
  986.5 6.2 fusion.43
  992.7 5.9 add_add_fusion
  998.9 4.7 fusion.60
  1006.0 6.1 convolution_add_fusion.2
  1012.0 5.9 psum.8
  1018.5 7.9 all_gather.65
  1027.2 43.0 %reduce-scatter.21.cloned.1.call-done = bf16[32,1024]{1,0:T(8,128)(2,1)} async-done(((bf16[1024,1024]{1,0:T(8,128)(2,1)}), bf16[32,1024]{1,0:T(8,128)(2,1)}) %reduce-scatter.21.cloned.1.call-update) | async-done | bytes 65552 | tf_op jit(solution)/shard_map/reduce_scatter | solution.py:491
  1070.3 11.8 all_gather.63
  1082.9 123.5 %reduce-scatter.19.cloned.1.call-done = bf16[32,1024]{1,0:T(8,128)(2,1)} async-done(((bf16[1024,1024]{1,0:T(8,128)(2,1)}), bf16[32,1024]{1,0:T(8,128)(2,1)}) %reduce-scatter.19.cloned.1.call-update) | async-done | bytes 65552 | tf_op jit(solution)/shard_map/reduce_scatter | solution.py:491
  1206.4 11.8 all_gather.62
  1219.0 21.9 %reduce-scatter.17.cloned.1.call-done = bf16[2,128,1024]{2,1,0:T(8,128)(2,1)} async-done(((bf16[2,512,1024]{2,1,0:T(8,128)(2,1)}), bf16[2,128,1024]{2,1,0:T(8,128)(2,1)}) %reduce-scatter.17.cloned.1.call-update) | async-done | bytes 524304 | tf_op jit(solution)/shard_map/reduce_scatter | solution.py:645
  1243.1 44.7 %reduce-scatter.15.cloned.1.call-done = bf16[2,256,1024]{1,2,0:T(8,128)(2,1)} async-done(((bf16[2,1024,1024]{1,2,0:T(8,128)(2,1)}), bf16[2,256,1024]{1,2,0:T(8,128)(2,1)}) %reduce-scatter.15.cloned.1.call-update) | async-done | bytes 1048592 | tf_op jit(solution)/shard_map/reduce_scatter | solution.py:669
  1290.5 144.2 %reduce-scatter.25.cloned.1.call-done = bf16[32,4096]{1,0:T(8,128)(2,1)} async-done(((bf16[1024,4096]{1,0:T(8,128)(2,1)}), bf16[32,4096]{1,0:T(8,128)(2,1)}) %reduce-scatter.25.cloned.1.call-update) | async-done | bytes 262160 | tf_op jit(solution)/shard_map/reduce_scatter | solution.py:491
  1434.8 141.2 %reduce-scatter.33.cloned.1.call-done = bf16[32,2048]{1,0:T(8,128)(2,1)} async-done(((bf16[1024,2048]{1,0:T(8,128)(2,1)}), bf16[32,2048]{1,0:T(8,128)(2,1)}) %reduce-scatter.33.cloned.1.call-update) | async-done | bytes 131088 | tf_op jit(solution)/shard_map/reduce_scatter | solution.py:491
  1576.0 12.6 all_gather.64
  1591.6 6.7 fusion.6
  1598.2 125.2 %reduce-scatter.31.cloned.1.call-done = bf16[32,3584]{1,0:T(8,128)(2,1)} async-done(((bf16[1024,3584]{1,0:T(8,128)(2,1)}), bf16[32,3584]{1,0:T(8,128)(2,1)}) %reduce-scatter.31.cloned.1.call-update) | async-done | bytes 229392 | tf_op jit(solution)/shard_map/reduce_scatter | solution.py:491
  1723.5 13.0 all_gather.61
  1746.2 15.5 all-gather.29.cloned.1.call-done
  (310 shorter events, 114.6 us)
Async XLA Ops:
  7.2 12.9 copy-start
  7.2 6.2 copy-start.14
  7.2 6.2 copy-start.15
  7.2 7.0 copy-start.19
  7.2 62.7 %all-gather.33.cloned.1.call-start = ((), (), s32[]{:S(2)}) async-start(), calls=%async_computation.27 | async-start | bytes 5242880 | tf_op jit(solution)/shard_map/all_gather | solution.py:576
  11.5 11.1 copy-start.62
  11.5 17.0 copy-start.32
  12.6 66.3 %all-gather.21.cloned.1.call-start = ((), (), s32[]{:S(2)}) async-start(), calls=%async_computation.14 | async-start | bytes 2621440 | tf_op jit(solution)/shard_map/all_gather | solution.py:577
  13.4 125.7 %all-gather.19.cloned.1.call-start = ((), (), s32[]{:S(2)}) async-start(), calls=%async_computation.13 | async-start | bytes 4325376 | tf_op jit(solution)/shard_map/all_gather | solution.py:487
  14.1 200.0 %all-gather.13.cloned.1.call-start = ((), (), s32[]{:S(2)}) async-start(), calls=%async_computation.10 | async-start | bytes 7569408 | tf_op jit(solution)/shard_map/all_gather | solution.py:487
  15.3 379.7 %all-gather.15.cloned.1.call-start = ((), (), s32[]{:S(2)}) async-start(), calls=%async_computation.11 | async-start | bytes 2162688 | tf_op jit(solution)/shard_map/all_gather | solution.py:487
  16.8 14.8 copy-start.49
  16.8 14.8 copy-start.50
  16.8 14.8 copy-start.51
  16.8 14.8 copy-start.52
  16.9 14.8 copy-start.53
  16.9 14.8 copy-start.54
  16.9 388.9 %all-gather.17.cloned.1.call-start = ((), (), s32[]{:S(2)}) async-start(), calls=%async_computation.12 | async-start | bytes 2162688 | tf_op jit(solution)/shard_map/all_gather | solution.py:487
  18.4 430.0 %all-gather.23.cloned.1.call-start = ((), (), s32[]{:S(2)}) async-start(), calls=%async_computation.15 | async-start | bytes 2162688 | tf_op jit(solution)/shard_map/all_gather | solution.py:487
  20.0 448.9 %all-gather.25.cloned.1.call-start = ((), (), s32[]{:S(2)}) async-start(), calls=%async_computation.16 | async-start | bytes 8650752 | tf_op jit(solution)/shard_map/all_gather | solution.py:487
  20.8 527.2 %all-gather.27.cloned.1.call-start = ((), (), s32[]{:S(2)}) async-start(), calls=%async_computation.17 | async-start | bytes 8650752 | tf_op jit(solution)/shard_map/all_gather | solution.py:487
  22.6 976.0 %reduce-scatter.27.cloned.1.call-start = ((), (), s32[]{:S(2)}) async-start(), calls=%async_computation.25 | async-start | bytes 8650752 | tf_op jit(solution)/shard_map/reduce_scatter | solution.py:491
  22.7 35.1 %copy-start.31 = (s32[8]{0:T(128)}, s32[8]{0:T(128)S(1)}, u32[]{:S(2)}) copy-start(s32[8]{0:T(128)S(1)} %dynamic_slice.48.blocks) | copy-start | bytes 100
  28.6 41.3 %copy-start.47 = (s32[1024]{0:T(1024)}, s32[1024]{0:T(1024)S(1)}, u32[]{:S(2)}) copy-start(s32[1024]{0:T(1024)S(1)} %iota_subtract_fusion) | copy-start | bytes 12292
  29.9 40.0 %copy-start.43 = (s32[1024]{0:T(1024)}, s32[1024]{0:T(1024)S(1)}, u32[]{:S(2)}) copy-start(s32[1024]{0:T(1024)S(1)} %add.195) | copy-start | bytes 12292
  55.2 393.3 %copy-start.39 = (f32[1,1024]{1,0:T(1,128)}, f32[1,1024]{1,0:T(1,128)S(1)}, u32[]{:S(2)}) copy-start(f32[1,1024]{1,0:T(1,128)S(1)} %get-tuple-element.177) | copy-start | bytes 12292
  55.2 393.3 %copy-start.45 = (f32[1,1024]{1,0:T(1,128)}, f32[1,1024]{1,0:T(1,128)S(1)}, u32[]{:S(2)}) copy-start(f32[1,1024]{1,0:T(1,128)S(1)} %get-tuple-element.178) | copy-start | bytes 12292
  234.5 10.9 slice-start.6
  402.2 46.3 %copy-start.22 = (f32[1536]{0:T(1024)}, f32[1536]{0:T(1024)S(1)}, u32[]{:S(2)}) copy-start(f32[1536]{0:T(1024)S(1)} %broadcast_multiply_fusion.7) | copy-start | bytes 18436
  405.7 42.8 %copy-start.29 = (f32[1536]{0:T(1024)}, f32[1536]{0:T(1024)S(1)}, u32[]{:S(2)}) copy-start(f32[1536]{0:T(1024)S(1)} %add_rsqrt_fusion.2) | copy-start | bytes 18436
  457.4 11.5 copy-start.37
  457.4 11.5 copy-start.41
  457.4 189.6 %copy-start.20 = (f32[1536]{0:T(1024)}, f32[1536]{0:T(1024)S(1)}, u32[]{:S(2)}) copy-start(f32[1536]{0:T(1024)S(1)} %broadcast_multiply_fusion.6) | copy-start | bytes 18436
  460.8 186.3 %copy-start.27 = (f32[1536]{0:T(1024)}, f32[1536]{0:T(1024)S(1)}, u32[]{:S(2)}) copy-start(f32[1536]{0:T(1024)S(1)} %add_rsqrt_fusion.1) | copy-start | bytes 18436
  548.0 20.3 %slice-start = ((s8[6291456]{0:T(1024)(128)(4,1)}), s8[4194304]{0:T(1024)(128)(4,1)S(1)}, s32[]{:S(2)}) async-start(s8[6291456]{0:T(1024)(128)(4,1)} %bitcast.239), calls=%async_computation.31 | async-start | bytes 8388608
  548.0 20.3 %slice-start.1 = ((s8[6291456]{0:T(1024)(128)(4,1)}), s8[2097152]{0:T(1024)(128)(4,1)S(1)}, s32[]{:S(2)}) async-start(s8[6291456]{0:T(1024)(128)(4,1)} %bitcast.239), calls=%async_computation.32 | async-start | bytes 4194304
  596.7 28.3 %slice-start.2 = ((s8[6291456]{0:T(1024)(128)(4,1)}), s8[2097152]{0:T(1024)(128)(4,1)S(1)}, s32[]{:S(2)}) async-start(s8[6291456]{0:T(1024)(128)(4,1)} %bitcast.241), calls=%async_computation.33 | async-start | bytes 4194304
  596.7 415.3 %reduce-scatter.29.cloned.1.call-start = ((), (), s32[]{:S(2)}) async-start(), calls=%async_computation.28 | async-start | bytes 36864 | tf_op jit(solution)/shard_map/reduce_scatter | solution.py:688
  596.8 28.3 %slice-start.3 = ((s8[6291456]{0:T(1024)(128)(4,1)}), s8[4194304]{0:T(1024)(128)(4,1)S(1)}, s32[]{:S(2)}) async-start(s8[6291456]{0:T(1024)(128)(4,1)} %bitcast.241), calls=%async_computation.34 | async-start | bytes 8388608
  656.9 42.4 %copy-start.23 = (f32[1536]{0:T(1024)S(1)}, f32[1536]{0:T(1024)}, u32[]{:S(2)}) copy-start(f32[1536]{0:T(1024)} %copy-done.22) | copy-start | bytes 18436
  656.9 42.4 %copy-start.30 = (f32[1536]{0:T(1024)S(1)}, f32[1536]{0:T(1024)}, u32[]{:S(2)}) copy-start(f32[1536]{0:T(1024)} %copy-done.29) | copy-start | bytes 18436
  656.9 42.4 %copy-start.40 = (f32[1,1024]{1,0:T(1,128)S(1)}, f32[1,1024]{1,0:T(1,128)}, u32[]{:S(2)}) copy-start(f32[1,1024]{1,0:T(1,128)} %copy-done.39) | copy-start | bytes 12292
  656.9 42.4 %copy-start.60 = (bf16[1024,1024]{1,0:T(8,128)(2,1)S(1)}, bf16[1024,1024]{1,0:T(8,128)(2,1)}, u32[]{:S(2)}) copy-start(bf16[1024,1024]{1,0:T(8,128)(2,1)} %all-gather.17.cloned.1.call-done) | copy-start | bytes 6291460
  699.3 11.3 copy-start.34
  699.3 11.3 copy-start.35
  711.2 8.8 copy-start.46
  711.2 307.3 %reduce-scatter.23.cloned.1.call-start = ((), (), s32[]{:S(2)}) async-start(), calls=%async_computation.22 | async-start | bytes 2162688 | tf_op jit(solution)/shard_map/reduce_scatter | solution.py:491
  720.0 350.2 %reduce-scatter.21.cloned.1.call-start = ((), (), s32[]{:S(2)}) async-start(), calls=%async_computation.21 | async-start | bytes 2162688 | tf_op jit(solution)/shard_map/reduce_scatter | solution.py:491
  729.3 477.1 %reduce-scatter.19.cloned.1.call-start = ((), (), s32[]{:S(2)}) async-start(), calls=%async_computation.20 | async-start | bytes 2162688 | tf_op jit(solution)/shard_map/reduce_scatter | solution.py:491
  729.3 8.8 copy-start.68
  742.8 498.2 %reduce-scatter.17.cloned.1.call-start = ((), (), s32[]{:S(2)}) async-start(), calls=%async_computation.19 | async-start | bytes 2621440 | tf_op jit(solution)/shard_map/reduce_scatter | solution.py:645
  751.7 536.0 %reduce-scatter.15.cloned.1.call-start = ((), (), s32[]{:S(2)}) async-start(), calls=%async_computation.18 | async-start | bytes 5242880 | tf_op jit(solution)/shard_map/reduce_scatter | solution.py:669
  887.8 7.2 copy-start.65
  895.0 6.4 copy-start.44
  895.0 6.4 copy-start.48
  908.1 526.6 %reduce-scatter.25.cloned.1.call-start = ((), (), s32[]{:S(2)}) async-start(), calls=%async_computation.23 | async-start | bytes 8650752 | tf_op jit(solution)/shard_map/reduce_scatter | solution.py:491
  930.5 645.5 %reduce-scatter.33.cloned.1.call-start = ((), (), s32[]{:S(2)}) async-start(), calls=%async_computation.30 | async-start | bytes 4325376 | tf_op jit(solution)/shard_map/reduce_scatter | solution.py:491
  947.7 775.8 %reduce-scatter.31.cloned.1.call-start = ((), (), s32[]{:S(2)}) async-start(), calls=%async_computation.29 | async-start | bytes 7569408 | tf_op jit(solution)/shard_map/reduce_scatter | solution.py:491
  986.4 6.3 slice-start.4
  986.4 757.0 %all-gather.31.cloned.1.call-start = ((), (), s32[]{:S(2)}) async-start(), calls=%async_computation.26 | async-start | bytes 1310720 | tf_op jit(solution)/shard_map/all_gather | solution.py:492
  986.4 6.2 slice-start.5
  986.5 6.2 copy-start.13
  998.6 763.1 %all-gather.29.cloned.1.call-start = ((), (), s32[]{:S(2)}) async-start(), calls=%async_computation.24 | async-start | bytes 1310720 | tf_op jit(solution)/shard_map/all_gather | solution.py:492
  1739.2 25.3 %copy-start.1 = (bf16[128,4096]{1,0:T(8,128)(2,1)S(1)}, bf16[128,4096]{1,0:T(8,128)(2,1)}, u32[]{:S(2)}) copy-start(bf16[128,4096]{1,0:T(8,128)(2,1)} %param.43) | copy-start | bytes 3145732
  (41 other events, 140.8 us)
Sparse Core Ops, SparseCore 0:
  12.7 36.9 all-gather.32
  51.3 22.5 all-gather.20
  77.3 61.7 all-gather.18
  142.3 71.8 all-gather.12
  217.5 54.7 all-gather.14
  275.5 55.2 all-gather.16
  334.2 55.1 all-gather.22
  392.9 75.9 all-gather.24
  472.3 75.6 all-gather.26
  596.9 142.8 reduce-scatter.26
  743.5 53.8 reduce-scatter.28
  799.5 134.1 reduce-scatter.22
  936.0 134.1 reduce-scatter.20
  1072.4 133.9 reduce-scatter.18
  1208.8 32.1 reduce-scatter.16
  1243.3 44.3 reduce-scatter.14
  1289.9 144.7 reduce-scatter.24
  1436.9 139.0 reduce-scatter.32
  1578.3 145.1 reduce-scatter.30
  1724.9 18.5 all-gather.30
  1745.0 16.6 all-gather.28

commit v2 on v1

--- a/solution.py
+++ b/solution.py
@@ -135,6 +135,7 @@
 
 
 def self_backward_kernel(
+    group,
     blocks,
     own_ref,
     query_ref,
@@ -284,56 +285,73 @@
             jax.ShapeDtypeStruct((seqs, width // 128, slots, total, 128), BF16),
         ],
         compiler_params=pltpu.CompilerParams(vmem_limit_bytes=LIMIT),
-        cost_estimate=estimate(40e9, 80e6),
+        cost_estimate=estimate(150e9, 80e6),
         name="self_forward",
     )(blocks, own, query, rel, own_key, own_value, keys, values, index)
 
 
 def self_backward(
-    blocks, own, query, own_key, own_value, keys, values, hot, mixed, grad, probs, own_probs
+    group, blocks, own, query, own_key, own_value, keys, values, hot, mixed, grad, probs, own_probs
 ):
     streams, seqs, rows, width = query.shape
     seq = keys.shape[1]
     slots = rows // BLK
     total = 2 * streams * BLK
+
+    def lines(count):
+        return pl.BlockSpec((count, 1, rows, 256), lambda n, g, b, o: (0, n, 0, g[0]))
+
+    def result(count, lanes):
+        return pl.BlockSpec((count, 1, rows, lanes), lambda n, g, b, o: (0, n, 0, 0))
+
+    def shape(count, lanes):
+        return jax.ShapeDtypeStruct((count, seqs, rows, lanes), BF16)
+
+    def stored(lanes):
+        return pl.BlockSpec((1, 2, slots, total, lanes), lambda n, g, b, o: (n, g[0], 0, 0, 0))
+
+    memory = pl.BlockSpec((1, seq, 256), lambda n, g, b, o: (n, 0, g[0]))
+    memory_result = pl.BlockSpec((1, seq, 256), lambda n, g, b, o: (n, 0, 0))
+    memory_shape = jax.ShapeDtypeStruct((seqs, seq, 256), BF16)
     return pl.pallas_call(
         self_backward_kernel,
-        grid=(seqs, width // 256),
-        in_specs=[
-            smem_spec(),
-            smem_spec(),
-            group_spec(streams, rows, 256),
-            group_spec(streams - 1, rows, 256),
-            group_spec(streams - 1, rows, 256),
-            full_spec(seq, 256),
-            full_spec(seq, 256),
-            whole_spec(hot),
-            group_spec(streams, rows, 256),
-            group_spec(streams, rows, 256),
-            prob_spec(slots, total, seq),
-            prob_spec(slots, total, 128),
+        grid_spec=pltpu.PrefetchScalarGridSpec(
+            num_scalar_prefetch=3,
+            grid=(seqs,),
+            in_specs=[
+                lines(streams),
+                lines(streams - 1),
+                lines(streams - 1),
+                memory,
+                memory,
+                pl.BlockSpec(hot.shape, lambda n, g, b, o: (0, 0)),
+                lines(streams),
+                lines(streams),
+                stored(seq),
+                stored(128),
+            ],
+            out_specs=[
+                result(streams, 256),
+                result(streams, 128),
+                result(streams - 1, 256),
+                result(streams - 1, 256),
+                memory_result,
+                memory_result,
+            ],
+            scratch_shapes=[pltpu.VMEM((seq, 256), F32), pltpu.VMEM((seq, 256), F32)],
+        ),
+        out_shape=[
+            shape(streams, 256),
+            shape(streams, 128),
+            shape(streams - 1, 256),
+            shape(streams - 1, 256),
+            memory_shape,
+            memory_shape,
         ],
-        out_specs=[
-            group_spec(streams, rows, 256),
-            group_spec(streams, rows, 128),
-            group_spec(streams - 1, rows, 256),
-            group_spec(streams - 1, rows, 256),
-            full_spec(seq, 256),
-            full_spec(seq, 256),
-        ],
-        out_shape=[
-            jax.ShapeDtypeStruct(query.shape, BF16),
-            jax.ShapeDtypeStruct((streams, seqs, rows, width // 2), BF16),
-            jax.ShapeDtypeStruct(own_key.shape, BF16),
-            jax.ShapeDtypeStruct(own_key.shape, BF16),
-            jax.ShapeDtypeStruct(keys.shape, BF16),
-            jax.ShapeDtypeStruct(keys.shape, BF16),
-        ],
-        scratch_shapes=[pltpu.VMEM((seq, 256), F32), pltpu.VMEM((seq, 256), F32)],
         compiler_params=pltpu.CompilerParams(vmem_limit_bytes=LIMIT),
-        cost_estimate=estimate(90e9, 100e6),
+        cost_estimate=estimate(145e9 / 4, 100e6 / 4),
         name="self_backward",
-    )(blocks, own, query, own_key, own_value, keys, values, hot, mixed, grad, probs, own_probs)
+    )(group, blocks, own, query, own_key, own_value, keys, values, hot, mixed, grad, probs, own_probs)
 
 
 def cross_forward_kernel(query_ref, key_ref, value_ref, out_ref, prob_ref):
@@ -422,7 +440,7 @@
             jax.ShapeDtypeStruct((streams, seqs, width // 128, 2 * rows, memory), BF16),
         ],
         compiler_params=pltpu.CompilerParams(vmem_limit_bytes=LIMIT),
-        cost_estimate=estimate(26e9, 20e6),
+        cost_estimate=estimate(38e9, 40e6),
         name="cross_forward",
     )(query, keys, values)
 
@@ -449,7 +467,7 @@
         ],
         scratch_shapes=[pltpu.VMEM((memory, 256), F32), pltpu.VMEM((memory, 256), F32)],
         compiler_params=pltpu.CompilerParams(vmem_limit_bytes=LIMIT),
-        cost_estimate=estimate(60e9, 30e6),
+        cost_estimate=estimate(47e9, 50e6),
         name="cross_backward",
     )(query, keys, values, mixed, grad, probs)
 
@@ -481,15 +499,185 @@
 FULL = ("fsdp", "ctx")
 
 
+PARTNER = [(0, 1), (1, 0), (2, 3), (3, 2)]
+ACROSS = [(0, 2), (2, 0), (1, 3), (3, 1)]
+
+
 def gather(shard, ranks):
     rows = shard.shape[0] // ranks
     piece = lax.dynamic_slice_in_dim(shard, lax.axis_index("ctx") * rows, rows)
     return lax.all_gather(piece, FULL, axis=0, tiled=True)
 
 
-def reduce_rows(grad):
-    piece = lax.psum_scatter(grad.astype(BF16), FULL, scatter_dimension=0, tiled=True)
-    return lax.all_gather(piece, "ctx", axis=0, tiled=True).astype(F32)
+def swap(value):
+    return lax.ppermute(value, "ctx", PARTNER)
+
+
+def pass_across(value):
+    return lax.ppermute(value, "ctx", ACROSS)
+
+
+def tie(*values):
+    return lax.optimization_barrier(values)
+
+
+def spread(piece):
+    across = pass_across(piece)
+    return piece, swap(piece), across, swap(across)
+
+
+def place_kernel(rank, first, second, third, fourth, out_ref):
+    for step, ref in enumerate((first, second, third, fourth)):
+
+        @pl.when((rank[0] ^ step) == pl.program_id(0))
+        def _():
+            out_ref[:, 0] = ref[...]
+
+
+def place(pieces):
+    outer, rows, columns = pieces[0].shape
+    return pl.pallas_call(
+        place_kernel,
+        grid=(4,),
+        in_specs=[smem_spec()] + [whole_block(piece) for piece in pieces],
+        out_specs=pl.BlockSpec((outer, 1, rows, columns), lambda step: (0, step, 0, 0)),
+        out_shape=jax.ShapeDtypeStruct((outer, 4, rows, columns), pieces[0].dtype),
+        compiler_params=pltpu.CompilerParams(vmem_limit_bytes=LIMIT),
+        cost_estimate=estimate(0, 8 * pieces[0].size * 2),
+        name="place",
+    )(lax.axis_index("ctx").reshape(1), *pieces)
+
+
+def whole_block(value):
+    return pl.BlockSpec(
+        value.shape, lambda step: (0,) * value.ndim, pipeline_mode=pl.Buffered(1)
+    )
+
+
+def gather_half(shard, ranks):
+    if ranks != 4:
+        return gather(shard, ranks)
+    rows = shard.shape[0] // ranks
+    piece = lax.dynamic_slice_in_dim(shard, lax.axis_index("ctx") * rows, rows)
+    return lax.all_gather(piece, "fsdp", axis=0, tiled=False)
+
+
+def gather_pass(piece, ranks):
+    if ranks != 4:
+        return (piece,)
+    return piece, swap(piece), pass_across(piece)
+
+
+def gather_rest(pieces, ranks):
+    if ranks != 4:
+        return pieces[0]
+    piece, partner, across = pieces
+    return place((piece, partner, across, swap(across))).reshape(-1, piece.shape[2])
+
+
+def gather_rows(value, ranks):
+    if ranks != 4:
+        return lax.all_gather(value, "ctx", axis=1, tiled=True)
+    return place(spread(value)).reshape(value.shape[0], -1, value.shape[2])
+
+
+def column_part(count, *groups):
+    def part(index, step):
+        parts = []
+        for group in groups:
+            total = 0.0
+            for left, right in group:
+                columns = right.shape[1] // count
+                right = lax.dynamic_slice_in_dim(right, index * columns, columns, axis=1)
+                total = total + dot_tn(left, right)
+            parts.append(total)
+        return parts[0] if len(parts) == 1 else jnp.concatenate(parts, axis=1)
+
+    return part
+
+
+def block_part(count, value):
+    rows = value.shape[1] // count
+
+    def part(index, step):
+        return lax.dynamic_slice_in_dim(value, index * rows, rows, axis=1).astype(F32)
+
+    return part
+
+
+class Exchange:
+    def __init__(self, ranks, part):
+        self.ranks = ranks
+        self.part = part
+        self.rank = lax.axis_index("ctx")
+
+    def begin(self):
+        if self.ranks != 4:
+            every = [self.part(index, index).astype(BF16) for index in range(self.ranks)]
+            self.values = (jnp.stack(every),)
+            return
+        corner = self.part(self.rank ^ 3, 3).astype(BF16)
+        self.values = (corner, self.part(self.rank ^ 1, 1).astype(BF16))
+
+    def turn(self):
+        if self.ranks != 4:
+            return
+        corner, partner = (swap(value) for value in self.values)
+        side = (self.part(self.rank ^ 2, 2) + corner.astype(F32)).astype(BF16)
+        self.values = (side, partner)
+
+    def fetch(self):
+        if self.ranks == 4:
+            side, partner = self.values
+            self.values = (pass_across(side), partner)
+
+    def end(self):
+        if self.ranks != 4:
+            mine = lax.psum_scatter(self.values[0], "ctx", scatter_dimension=0, tiled=True)
+            return mine[0].astype(F32)
+        side, partner = self.values
+        return self.part(self.rank, 0) + partner.astype(F32) + side.astype(F32)
+
+
+def hold(value, *items):
+    packed = [item.values if isinstance(item, Exchange) else item for item in items]
+    value, packed = tie(value, packed)
+    for item, new in zip(items, packed):
+        if isinstance(item, Exchange):
+            item.values = new
+    others = [new for item, new in zip(items, packed) if not isinstance(item, Exchange)]
+    return (value, *others) if others else value
+
+
+def scatter(total):
+    return lax.psum_scatter(total.astype(BF16), "fsdp", scatter_dimension=0, tiled=True)
+
+
+def collect(ranks, piece):
+    if ranks != 4:
+        whole = lax.all_gather(piece, "ctx", axis=0, tiled=False)
+        return [whole[index].astype(F32) for index in range(ranks)]
+    rank = lax.axis_index("ctx")
+    pieces = spread(piece)
+    ordered = []
+    for index in range(4):
+        chosen = pieces[3]
+        for step in range(3):
+            chosen = jnp.where((rank ^ step) == index, pieces[step], chosen)
+        ordered.append(chosen.astype(F32))
+    return ordered
+
+
+def columns_of(pieces, start, columns):
+    return jnp.concatenate([piece[:, start : start + columns] for piece in pieces], axis=1)
+
+
+def total_over(value, axis, size):
+    step = 1
+    while step < size:
+        value = value + lax.ppermute(value, axis, [(index, index ^ step) for index in range(size)])
+        step *= 2
+    return value
 
 
 def flat(value):
@@ -530,6 +718,7 @@
 
 def body(
     ranks,
+    shards,
     hidden,
     encoded,
     assign,
@@ -564,31 +753,27 @@
     places = (assign[:, None] * BLK + jnp.arange(BLK, dtype=jnp.int32)[None, :]).reshape(-1)
     order = (places[None, :] == (seq - 1 - jnp.arange(seq, dtype=jnp.int32))[:, None]).astype(BF16)
 
-    full_main = gather(jnp.concatenate([w_query, head_major(w_rel), w_key, w_value], axis=1), ranks)
-    cut = w_query.shape[1] + w_rel.shape[1]
-    w_query, w_rel = full_main[:, :width], full_main[:, width:cut]
-    w_key, w_value = full_main[:, cut : cut + width], full_main[:, cut + width :]
-    norms = jnp.stack([gain_one, shift_one, gain_two, shift_two, gain_three, shift_three])
-    norms = lax.all_gather(norms, "fsdp", axis=1, tiled=True).astype(F32)
-    gain_one, shift_one, gain_two, shift_two, gain_three, shift_three = (
-        norms[place : place + 1] for place in range(6)
-    )
-    main = lax.all_gather(hidden[:, :, 0, :], "ctx", axis=1, tiled=True)
-    memory = lax.all_gather(encoded, "ctx", axis=1, tiled=True)
-    w_out = gather(w_out, ranks)
-    full_cross = gather(jnp.concatenate([c_key, c_value], axis=1), ranks)
-    c_key, c_value = full_cross[:, :width], full_cross[:, width:]
-    c_query = gather(c_query, ranks)
-    c_out = gather(c_out, ranks)
-    w_inner = gather(w_inner, ranks)
-    w_outer = gather(w_outer, ranks)
-
     stacked = jnp.transpose(hidden, (2, 0, 1, 3))
     shape = stacked.shape
+    parts = [w_key, w_value, w_query, head_major(w_rel)]
+    full = gather(jnp.concatenate(parts, axis=1), ranks)
+    main = gather_rows(hidden[:, :, 0, :], ranks)
+    memory = gather_rows(encoded, ranks)
+    main = jnp.einsum("mu,nud->nmd", order, main, preferred_element_type=F32).astype(BF16)
+    norms = [gain_one, shift_one, gain_two, shift_two, gain_three, shift_three]
+    norms = jnp.pad(jnp.stack(norms, axis=1), ((0, 0), (0, 122)))
+    middle = jnp.concatenate([w_out, c_query, c_key, c_value, c_out, norms], axis=1)
+    full, main, memory, stacked, middle, w_inner, w_outer = tie(
+        full, main, memory, stacked, middle, w_inner, w_outer
+    )
+    middle = gather_pass(gather_half(middle, ranks), ranks)
+    w_inner = gather_half(w_inner, ranks)
+    w_outer = gather_half(w_outer, ranks)
+    w_key, w_value, w_query = (full[:, start : start + width] for start in range(0, 3 * width, width))
+    w_rel = full[:, 3 * width :]
     lines = flat(stacked)
     own_shape = (streams - 1,) + shape[1:]
     own_lines = flat(stacked[1:])
-    main = jnp.einsum("mu,nud->nmd", order, main, preferred_element_type=F32).astype(BF16)
     main_lines = flat(main)
     main_shape = main.shape
     query = dot_nn(lines, w_query).astype(BF16).reshape(shape)
@@ -600,6 +785,17 @@
     mixed, probs, own_probs = self_forward(
         own_blocks, own, query, rel, own_keys, own_values, keys, values, index
     )
+    mixed, middle, w_inner, w_outer = tie(mixed, middle, w_inner, w_outer)
+    w_inner = gather_pass(w_inner, ranks)
+    w_outer = gather_pass(w_outer, ranks)
+    full = gather_rest(middle, ranks)
+    w_out, c_query, c_key, c_value, c_out = (
+        full[:, start : start + width] for start in range(0, 5 * width, width)
+    )
+    norms = jnp.transpose(full[:, 5 * width :])[:6].astype(F32)
+    gain_one, shift_one, gain_two, shift_two, gain_three, shift_three = (
+        norms[index : index + 1] for index in range(6)
+    )
     normal_one, rate_one = normalize(lines.astype(F32) + dot_nn(flat(mixed), w_out))
     h_one = normal_one * gain_one + shift_one
     h_one_low = h_one.astype(BF16)
@@ -608,6 +804,9 @@
     cross_keys = dot_nn(memory_lines, c_key).astype(BF16).reshape(memory.shape)
     cross_values = dot_nn(memory_lines, c_value).astype(BF16).reshape(memory.shape)
     cross_mixed, cross_probs = cross_forward(cross_query, cross_keys, cross_values)
+    cross_mixed, w_inner, w_outer = tie(cross_mixed, w_inner, w_outer)
+    w_inner = gather_rest(w_inner, ranks)
+    w_outer = gather_rest(w_outer, ranks)
     normal_two, rate_two = normalize(h_one + dot_nn(flat(cross_mixed), c_out))
     h_two = normal_two * gain_two + shift_two
     h_two_low = h_two.astype(BF16)
@@ -619,90 +818,195 @@
     grad = flat(jnp.transpose(cotangent, (2, 0, 1, 3))).astype(F32)
     grad_three, gain_three, shift_three = norm_back(grad, normal_three, rate_three, gain_three)
     grad_low = grad_three.astype(BF16)
-    w_outer_grad = reduce_rows(dot_tn(active, grad_low))
+    outer = Exchange(ranks, column_part(ranks, [(active, grad_low)]))
+    outer.begin()
+    grad_low = hold(grad_low, outer)
     grad_inner = (dot_nt(grad_low, w_outer) * slope.astype(F32)).astype(BF16)
-    w_inner_grad = reduce_rows(dot_tn(h_two_low, grad_inner))
+    inner = Exchange(ranks, column_part(ranks, [(h_two_low, grad_inner)]))
+    inner.begin()
+    outer.turn()
+    grad_inner = hold(grad_inner, inner, outer)
+    outer.fetch()
     grad_h_two = grad_three + dot_nt(grad_inner, w_inner)
     grad_two, gain_two, shift_two = norm_back(grad_h_two, normal_two, rate_two, gain_two)
-    grad_low = grad_two.astype(BF16)
-    c_out_grad = reduce_rows(dot_tn(flat(cross_mixed), grad_low))
+    c_out_low = grad_two.astype(BF16)
+    inner.turn()
+    grad_low = hold(c_out_low, inner)
+    inner.fetch()
     grad_mixed = dot_nt(grad_low, c_out).astype(BF16).reshape(shape)
     cross_query_grad, key_grad, value_grad = cross_backward(
         cross_query, cross_keys, cross_values, cross_mixed, grad_mixed, cross_probs
     )
+    cross_query_grad = hold(cross_query_grad, inner, outer)
+    inner_total, outer_total = inner.end().astype(BF16), outer.end().astype(BF16)
+    cross_query_grad, inner_total, outer_total = tie(cross_query_grad, inner_total, outer_total)
+    depth = width // shards
+    layers = outer_total.shape[0] // width
+    outer_total = outer_total.reshape(shards, layers, depth, -1)
+    parts = [outer_total[:, layer].reshape(width, -1) for layer in range(layers)]
+    ffn_piece = scatter(jnp.concatenate([inner_total] + parts, axis=1))
     cross_query_grad = flat(cross_query_grad)
     key_grad, value_grad = flat(key_grad), flat(value_grad)
-    c_query_grad = reduce_rows(dot_tn(h_one_low, cross_query_grad))
     grad_h_one = grad_two + dot_nt(cross_query_grad, c_query)
     grad_one, gain_one, shift_one = norm_back(grad_h_one, normal_one, rate_one, gain_one)
     grad_low = grad_one.astype(BF16)
-    w_out_grad = reduce_rows(dot_tn(flat(mixed), grad_low))
     grad_mixed = dot_nt(grad_low, w_out).astype(BF16).reshape(shape)
-    cross_grad = reduce_rows(
-        jnp.concatenate([dot_tn(memory_lines, key_grad), dot_tn(memory_lines, value_grad)], axis=1)
-    )
+    centre = Exchange(
+        ranks,
+        column_part(
+            ranks,
+            [(flat(mixed), grad_low)],
+            [(h_one_low, cross_query_grad)],
+            [(memory_lines, key_grad)],
+            [(memory_lines, value_grad)],
+            [(flat(cross_mixed), c_out_low)],
+        ),
+    )
+    centre.begin()
     encoded_grad = (dot_nt(key_grad, c_key) + dot_nt(value_grad, c_value)).astype(BF16)
-    encoded_grad = lax.psum_scatter(
-        encoded_grad.reshape(memory.shape), "ctx", scatter_dimension=1, tiled=True
-    ).astype(F32)
-    query_grad, rel_grad, own_key_grad, own_value_grad, key_grad, value_grad = self_backward(
-        own_blocks,
-        own,
-        query,
-        own_keys,
-        own_values,
-        keys,
-        values,
-        hot,
-        mixed,
-        grad_mixed,
-        probs,
-        own_probs,
-    )
-    query_grad, rel_grad = flat(query_grad), flat(rel_grad)
-    own_key_grad, own_value_grad = flat(own_key_grad), flat(own_value_grad)
-    key_grad, value_grad = flat(key_grad), flat(value_grad)
+    centre.turn()
+    memory_exchange = Exchange(ranks, block_part(ranks, encoded_grad.reshape(memory.shape)))
+    memory_exchange.begin()
+    norms = jnp.stack([gain_one, shift_one, gain_two, shift_two, gain_three, shift_three])
+    grad_mixed, norms = hold(grad_mixed, centre, memory_exchange, norms)
+    centre.fetch()
+    memory_exchange.turn()
+    memory_exchange.fetch()
+    rank = lax.axis_index("ctx")
+    steps = (3, 1, 2, 0)
+    places = [rank ^ step if ranks == 4 else jnp.int32(index) for index, step in enumerate(steps)]
+    back = {}
+
+    def first_part(index, step):
+        query_grad, rel_grad, own_key_grad, own_value_grad, key_grad, value_grad = back[step]
+        own_grad = jnp.concatenate([own_key_grad, own_value_grad], axis=1)
+        main_grad = jnp.concatenate([key_grad, value_grad], axis=1)
+        return jnp.concatenate(
+            [
+                dot_tn(lines, query_grad),
+                dot_tn(lines, rel_grad),
+                dot_tn(own_lines, own_grad) + dot_tn(main_lines, main_grad),
+            ],
+            axis=1,
+        )
+
+    first = Exchange(ranks, first_part)
+    for turn, step in enumerate(steps):
+        results = self_backward(
+            places[turn].reshape(1),
+            own_blocks,
+            own,
+            query,
+            own_keys,
+            own_values,
+            keys,
+            values,
+            hot,
+            mixed,
+            grad_mixed,
+            probs,
+            own_probs,
+        )
+        if turn < 3:
+            grad_mixed, results = tie(grad_mixed, results)
+        back[step] = [flat(value) for value in results]
+        if turn == 1:
+            if ranks == 4:
+                first.begin()
+            grad_mixed = hold(grad_mixed, centre, memory_exchange)
+            centre_total = centre.end().astype(BF16)
+            encoded_grad = memory_exchange.end()
+            if ranks == 4:
+                grad_mixed, centre_total = hold(grad_mixed, first, centre_total)
+            centre_piece = scatter(centre_total)
+        if turn == 2 and ranks == 4:
+            first.turn()
+            grad_mixed = hold(grad_mixed, first)
+            first.fetch()
+    joined = [jnp.concatenate(values, axis=1) for values in zip(*(back[step] for step in steps))]
+    query_grad, rel_grad, own_key_grad, own_value_grad, key_grad, value_grad = joined
+    if ranks == 4:
+        back[0][0], key_grad = hold(back[0][0], first, key_grad)
+        first_total = first.end().astype(BF16)
+        key_grad, first_total = tie(key_grad, first_total)
+    else:
+        whole = column_part(
+            ranks,
+            [(lines, query_grad)],
+            [(lines, rel_grad)],
+            [(own_lines, own_key_grad), (main_lines, key_grad)],
+            [(own_lines, own_value_grad), (main_lines, value_grad)],
+        )
+        first = Exchange(ranks, whole)
+        first.begin()
+        first_total = first.end().astype(BF16)
+    first_piece = scatter(first_total)
+
+    def reorder(weight):
+        columns = weight.shape[1] // len(steps)
+        return jnp.concatenate(
+            [
+                lax.dynamic_slice_in_dim(weight, index * columns, columns, axis=1)
+                for index in places
+            ],
+            axis=1,
+        )
+
+    w_query, w_rel, w_key, w_value = (
+        reorder(weight) for weight in (w_query, w_rel, w_key, w_value)
+    )
     main_grad = (dot_nt(key_grad, w_key) + dot_nt(value_grad, w_value)).astype(BF16)
     main_grad = jnp.einsum(
         "mu,nmd->nud", order, main_grad.reshape(main_shape), preferred_element_type=F32
     ).astype(BF16)
-    main_grad = lax.psum_scatter(main_grad, "ctx", scatter_dimension=1, tiled=True).astype(F32)
-    full_grad = reduce_rows(
-        jnp.concatenate(
-            [
-                dot_tn(lines, query_grad),
-                dot_tn(lines, rel_grad),
-                dot_tn(own_lines, own_key_grad) + dot_tn(main_lines, key_grad),
-                dot_tn(own_lines, own_value_grad) + dot_tn(main_lines, value_grad),
-            ],
-            axis=1,
-        )
-    )
+    main_exchange = Exchange(ranks, block_part(ranks, main_grad))
+    main_exchange.begin()
+    main_exchange.turn()
+    main_exchange.fetch()
     own_grad = dot_nt(own_key_grad, w_key) + dot_nt(own_value_grad, w_value)
-    grad_lines = grad_one + dot_nt(query_grad, w_query) + dot_nt(rel_grad, w_rel)
+    grad_lines = grad_one + dot_nt(query_grad, w_query)
+    grad_lines = grad_lines + dot_nt(rel_grad, w_rel)
     grad_lines = grad_lines.reshape(shape) + jnp.concatenate(
-        [main_grad[None], own_grad.reshape(own_shape)], axis=0
+        [main_exchange.end()[None], own_grad.reshape(own_shape)], axis=0
     )
     grad_hidden = jnp.transpose(grad_lines, (1, 2, 0, 3))
-    norms = jnp.stack([gain_one, shift_one, gain_two, shift_two, gain_three, shift_three])
-    norms = lax.psum_scatter(lax.psum(norms, "ctx"), "fsdp", scatter_dimension=1, tiled=True)
+    norms = total_over(total_over(norms, "ctx", ranks), "fsdp", shards)
+    count = norms.shape[1] // shards
+    norms = lax.dynamic_slice_in_dim(norms, lax.axis_index("fsdp") * count, count, axis=1)
     gain_one, shift_one, gain_two, shift_two, gain_three, shift_three = (
-        norms[place] for place in range(6)
-    )
+        norms[index] for index in range(6)
+    )
+    pieces = collect(ranks, ffn_piece)
+    columns = width // ranks
+    cut = layers * columns
+    w_inner_grad = columns_of(pieces, 0, cut)
+    w_outer_grad = jnp.concatenate(
+        [columns_of(pieces, cut + layer * columns, columns) for layer in range(layers)], axis=0
+    )
+    pieces = collect(ranks, centre_piece)
+    w_out_grad, c_query_grad, c_key_grad, c_value_grad, c_out_grad = (
+        columns_of(pieces, start * columns, columns) for start in range(5)
+    )
+    pieces = collect(ranks, first_piece)
+    rel_columns = w_rel.shape[1] // ranks
+    w_query_grad = columns_of(pieces, 0, columns)
+    w_rel_grad = columns_of(pieces, columns, rel_columns)
+    w_key_grad = columns_of(pieces, columns + rel_columns, columns)
+    w_value_grad = columns_of(pieces, 2 * columns + rel_columns, columns)
     return (
         output,
         grad_hidden,
         encoded_grad,
-        full_grad[:, :width],
-        full_grad[:, cut : cut + width],
-        full_grad[:, cut + width :],
-        bucket_major(full_grad[:, width:cut]),
+        w_query_grad,
+        w_key_grad,
+        w_value_grad,
+        bucket_major(w_rel_grad),
         w_out_grad,
         gain_one,
         shift_one,
         c_query_grad,
-        cross_grad[:, :width],
-        cross_grad[:, width:],
+        c_key_grad,
+        c_value_grad,
         c_out_grad,
         gain_two,
         shift_two,
@@ -721,7 +1025,7 @@
     in_specs = (rows, P("fsdp", "ctx", None), P(), P()) + weights + (rows,)
     out_specs = (rows, rows, P("fsdp", "ctx", None)) + weights
     return jax.shard_map(
-        functools.partial(body, mesh.shape["ctx"]),
+        functools.partial(body, mesh.shape["ctx"], mesh.shape["fsdp"]),
         mesh=mesh,
         in_specs=in_specs,
         out_specs=out_specs,

time: 1780 us -> 1150 us (0.65)
  waiting for transfers between devices: 851 us -> 118 us
  blocking collectives: 85.8 us -> 0 us
  Pallas kernels: 341 us -> 392 us
  other arithmetic: 53.5 us -> 96.7 us
  starting transfers between devices: 1.29 us -> 43.9 us
  matrix products: 340 us -> 366 us
  local copies, waits for them, and re-layouts: 77 us -> 100 us
    reduce_scatter x10 -> x1, waiting for transfers between devices: 644 us -> 0.01 us  [scatter(): lax.psum_scatter(total.astype(BF16), 'fsdp', scatter_dimension=0, tiled=T...]
    all_gather x7 -> x1, waiting for transfers between devices: 189 us -> 10.6 us  [gather(): return lax.all_gather(piece, FULL, axis=0, tiled=True)]
    ppermute x0 -> x47, waiting for transfers between devices: none -> 95.6 us  [the longest x14 89.6 us: pass_across(): return lax.ppermute(value, 'ctx', ACROSS)]
    all_gather x6 -> x0, blocking collectives: 79.9 us -> none  [the longest x5 57 us: reduce_rows(): return lax.all_gather(piece, 'ctx', axis=0, tiled=True).astype(F32)]
    pallas_call x1 -> x9, Pallas kernels: 128 us -> 179 us  [the longest x4 148 us: self_backward(): pl.pallas_call(self_backward_kernel, grid_spec=pltpu.PrefetchScalarGridSp...]
    convert_element_type x6 -> x18, other arithmetic: 10.2 us -> 54.5 us  [the longest x5 14.5 us: turn(): side = (self.part(self.rank ^ 2, 2) + corner.astype(F32)).astype(BF16)]
    ppermute x0 -> x47, starting transfers between devices: none -> 43.4 us  [the longest x28 26.1 us: swap(): return lax.ppermute(value, 'ctx', PARTNER)]
    dot_general x13 -> x44, matrix products: 91.5 us -> 134 us  [dot_tn(): lax.dot_general(left, right, (((0,), (0,)), ((), ())), preferred_element_...]
  transfers between devices with their start and end apart: 21 -> 54, of which waited for: 13 -> 11; matrix products, arithmetic and copies ran while one was open for 23% -> 35% of each run, Pallas kernels for 19% -> 34%
where the time goes in v2:
time: 1150 us; the launch traced here: 1140 us
  Pallas kernels  392 us (34%)
  matrix products  366 us (32%)
  waiting for transfers between devices  118 us (10%)
  local copies, waits for them, and re-layouts  100 us (9%)
  other arithmetic  96.7 us (8%)
  starting transfers between devices  43.9 us (4%)
  between operations  22.2 us (2%)
    pallas_call x4, Pallas kernels, self_backward(): pl.pallas_call(self_backward_kernel, grid_spec=pltpu.PrefetchScalarGridSp...  148 us
    pallas_call x1, Pallas kernels, self_forward(): pl.pallas_call(self_forward_kernel, grid=(seqs, width // 256), in_specs=[...  137 us
    dot_general x44, matrix products, dot_tn(): lax.dot_general(left, right, (((0,), (0,)), ((), ())), preferred_element_...  134 us
    dot_general x13, matrix products, dot_nn(): return jnp.dot(left, right, preferred_element_type=F32)  112 us
    dot_general x13, matrix products, dot_nt(): lax.dot_general(left, right, (((1,), (1,)), ((), ())), preferred_element_...  106 us
    ppermute x14, waiting for transfers between devices, pass_across(): return lax.ppermute(value, 'ctx', ACROSS)  89.6 us
    unnamed x355, local copies, waits for them, and re-layouts  57.8 us
    pallas_call x1, Pallas kernels, cross_backward(): pl.pallas_call(cross_backward_kernel, grid=(seqs, width // 256, streams),...  42.1 us
  transfers between devices with their start and end apart: 54, of which 11 were waited for; matrix products, arithmetic and copies ran while one was open for 35% of the time, Pallas kernels for 34%

profile of v2, /device:TPU:1, one launch (start us, length us, event | category | flops | bytes accessed | tf_op | source)
XLA Modules:
  0.0 1138.6 jit_solution(15442010793183605075)
XLA Ops:
  18.4 22.8 %collective-permute-done.1.third = bf16[2,256,1024]{2,1,0:T(8,128)(2,1)S(1)} collective-permute-done((bf16[2,256,1024]{2,1,0:T(8,128)(2,1)S(1)}, bf16[2,256,1024]{2,1,0:T(8,128)(2,1)S(1)}, u32[]{:S(2)}, u32[]{:S(2)}) %collective-permute-start.1) | collective-permute-done | bytes 1048608 | tf_op jit(solution)/shard_map/ppermute | solution.py:517
  45.0 14.0 %collective-permute-done.4.third = bf16[2,128,1024]{2,1,0:T(8,128)(2,1)} collective-permute-done((bf16[2,128,1024]{2,1,0:T(8,128)(2,1)}, bf16[2,128,1024]{2,1,0:T(8,128)(2,1)}, u32[]{:S(2)}, u32[]{:S(2)}) %collective-permute-start.4) | collective-permute-done | bytes 524320 | tf_op jit(solution)/shard_map/ppermute | solution.py:517
  69.9 4.7 place.5
  74.6 8.9 convert_bitcast_fusion.1
  83.5 10.6 all-gather.8.cloned.1.call-done
  110.9 6.9 copy.147
  118.6 5.2 convolution_convert_fusion.12
  125.8 5.3 convolution_convert_fusion.8
  131.1 5.4 convolution_convert_fusion.11
  136.5 4.8 convolution_convert_fusion.5
  141.3 6.3 convolution_convert_fusion.7
  147.6 6.3 convolution_convert_fusion.6
  155.3 136.9 %self_forward.1 = (bf16[3,2,256,1024]{3,2,1,0:T(8,128)(2,1)}, bf16[2,8,8,192,1024]{4,3,2,1,0:T(8,128)(2,1)}, bf16[2,8,8,192,128]{4,3,2,1,0:T(8,128)(2,1)}) custom-call(s32[8]{0:T(128)} %copy-done.91, s32[1]{0:T(128)} %slice.311.own_ref, bf16[3,2,256,1024]{3,2,1,0:T(8,128)(2,1)} %bitcast.423, bf16[3,2,256,512]{3,2,1,0:T(8,128)(2,1)} %bitcast.474, ...), custom_call_target="tpu_custom_call" | custom-call | flops 149999992832 | bytes 80000000 | tf_op jit(solution)/shard_map/self_forward/pallas_call | solution.py:263
  311.8 8.4 place.7
  321.2 6.1 convolution_convert_fusion.10
  327.3 5.4 convolution_convert_fusion.9
  332.7 7.1 fusion.270
  340.6 3.7 multiply_reduce_fusion.7
  346.5 7.6 convolution_convert_fusion.4
  354.1 33.5 %cross_forward.1 = (bf16[3,2,256,1024]{3,2,1,0:T(8,128)(2,1)}, bf16[3,2,8,512,512]{4,3,2,1,0:T(8,128)(2,1)}) custom-call(bf16[3,2,256,1024]{3,2,1,0:T(8,128)(2,1)} %bitcast.442, bf16[2,512,1024]{2,1,0:T(8,128)(2,1)} %bitcast.460, bf16[2,512,1024]{2,1,0:T(8,128)(2,1)} %bitcast.462), custom_call_target="tpu_custom_call" | custom-call | flops 38000001024 | bytes 40000000 | tf_op jit(solution)/shard_map/cross_forward/pallas_call | solution.py:433
  387.5 13.9 %collective-permute-done.12.third = bf16[8,128,1024]{2,1,0:T(8,128)(2,1)} collective-permute-done((bf16[8,128,1024]{2,1,0:T(8,128)(2,1)}, bf16[8,128,1024]{2,1,0:T(8,128)(2,1)}, u32[]{:S(2)}, u32[]{:S(2)}) %collective-permute-start.12) | collective-permute-done | bytes 2097184 | tf_op jit(solution)/shard_map/ppermute | solution.py:517
  401.5 11.2 fusion.271
  424.5 7.1 place.8
  431.6 22.5 %multiply_convert_fusion.1 = (bf16[1536,4096]{1,0:T(8,128)(2,1)}, f32[1536,4096]{1,0:T(8,128)}) fusion(bf16[1536,1024]{1,0:T(8,128)(2,1)} %fusion.11, bf16[1024,4096]{1,0:T(8,128)(2,1)} %bitcast.316), kind=kOutput, calls=%fused_computation.7 | convolution fusion | flops 12916359168 | bytes 49283072 | tf_op jit(solution)/shard_map/dot_general | solution.py:29
  454.1 7.2 place.9
  461.3 19.3 %fusion.272 = (f32[1536]{0:T(1024)S(1)}, f32[1536,1024]{1,0:T(8,128)S(1)}) fusion(bf16[1536,4096]{1,0:T(8,128)(2,1)} %get-tuple-element.488, bf16[4096,1024]{1,0:T(8,128)(2,1)} %bitcast.318, f32[1024]{0:T(1024)S(1)} %bitcast.399, f32[1024]{0:T(1024)S(1)} %bitcast.392, f32[1536]{0:T(1024)S(1)} %add_rsqrt_fusion.1, f32[1536,1024]{1,0:T(8,128)} %get-tuple-element.487, ...), kind=kOutput, calls=%fused_computation.445 | convolution fusion | flops 12894337024 | bytes 33581056 | tf_op jit(solution)/shard_map/dot_general | solution.py:29
  484.5 5.2 fusion.253
  489.8 10.8 convolution_convert_fusion.1
  500.6 9.9 convolution_convert_fusion
  510.5 24.2 %multiply_convert_fusion = bf16[1536,4096]{1,0:T(8,128)(2,1)} fusion(bf16[1536,1024]{1,0:T(8,128)(2,1)} %copy-done.30, bf16[4096,1024]{1,0:T(8,128)(2,1)S(1)} %bitcast.321, f32[1536,4096]{1,0:T(8,128)} %get-tuple-element.489), kind=kOutput, calls=%fused_computation.6 | convolution fusion | flops 12960399360 | bytes 49283072 | tf_op jit(solution)/shard_map/dot_general | solution.py:21
  534.7 6.9 fusion.99
  541.5 4.7 fusion.102
  546.8 5.1 fusion.39
  554.9 10.3 fusion.182
  565.2 5.2 fusion.37
  570.4 10.0 add_convert_fusion.8
  581.0 22.1 %multiply_reduce_fusion = (f32[1024]{0:T(1024)S(1)}, f32[1536]{0:T(1024)S(1)}, f32[1536]{0:T(1024)S(1)}, f32[1024]{0:T(1024)S(1)}, f32[1536,1024]{1,0:T(8,128)}) fusion(f32[1536,1024]{1,0:T(8,128)S(1)} %bitcast.288, f32[1536]{0:T(1024)S(1)} %add_rsqrt_fusion.1, f32[1536]{0:T(1024)S(1)} %broadcast_multiply_fusion.6, f32[1024]{0:T(1024)S(1)} %bitcast.393, ...), kind=kOutput, calls=%fused_computation.20 | convolution fusion | flops 12900625408 | bytes 39882752 | tf_op jit(solution)/shard_map/dot_general | solution.py:21
  603.1 5.9 fusion.252
  609.0 5.0 add_convert_fusion.7
  614.0 6.4 convolution_convert_fusion.3
  621.8 42.1 %cross_backward.1 = (bf16[3,2,256,1024]{3,2,1,0:T(8,128)(2,1)}, bf16[2,512,1024]{2,1,0:T(8,128)(2,1)}, bf16[2,512,1024]{2,1,0:T(8,128)(2,1)}) custom-call(bf16[3,2,256,1024]{3,2,1,0:T(8,128)(2,1)} %bitcast.443, bf16[2,512,1024]{2,1,0:T(8,128)(2,1)} %bitcast.461, bf16[2,512,1024]{2,1,0:T(8,128)(2,1)} %bitcast.463, ...), custom_call_target="tpu_custom_call" | custom-call | flops 46999998464 | bytes 50000000 | tf_op jit(solution)/shard_map/cross_backward/pallas_call | solution.py:451
  663.9 4.7 fusion.107
  668.7 4.1 add_convert_fusion.4
  682.0 7.6 multiply_reduce_fusion.1
  689.6 4.3 fusion.251
  745.6 6.5 convolution_convert_fusion.2
  755.0 36.9 %self_backward.4 = (bf16[3,2,256,256]{3,2,1,0:T(8,128)(2,1)}, bf16[3,2,256,128]{3,2,1,0:T(8,128)(2,1)}, bf16[2,2,256,256]{3,2,1,0:T(8,128)(2,1)}, bf16[2,2,256,2...) custom-call(s32[1]{0:T(128)} %bitcast.69.group, s32[8]{0:T(128)} %copy-done.91, ...), custom_call_target="tpu_custom_call" | custom-call | flops 36250001408 | bytes 25000000 | tf_op jit(solution)/shard_map/self_backward/pallas_call | solution.py:316
  793.9 37.2 %self_backward.5 = (bf16[3,2,256,256]{3,2,1,0:T(8,128)(2,1)}, bf16[3,2,256,128]{3,2,1,0:T(8,128)(2,1)}, bf16[2,2,256,256]{3,2,1,0:T(8,128)(2,1)}, bf16[2,2,256,2...) custom-call(s32[1]{0:T(128)} %bitcast.71.group, s32[8]{0:T(128)} %copy-done.91, ...), custom_call_target="tpu_custom_call" | custom-call | flops 36250001408 | bytes 25000000 | tf_op jit(solution)/shard_map/self_backward/pallas_call | solution.py:316
  866.4 7.5 add_convert_fusion.2
  873.9 36.9 %self_backward.6 = (bf16[3,2,256,256]{3,2,1,0:T(8,128)(2,1)}, bf16[3,2,256,128]{3,2,1,0:T(8,128)(2,1)}, bf16[2,2,256,256]{3,2,1,0:T(8,128)(2,1)}, bf16[2,2,256,2...) custom-call(s32[1]{0:T(128)} %bitcast.89.group, s32[8]{0:T(128)} %copy-done.91, ...), custom_call_target="tpu_custom_call" | custom-call | flops 36250001408 | bytes 25000000 | tf_op jit(solution)/shard_map/self_backward/pallas_call | solution.py:316
  910.8 4.9 collective-permute-start.27
  915.8 4.4 copy.191
  936.3 37.3 %self_backward.7 = (bf16[3,2,256,256]{3,2,1,0:T(8,128)(2,1)}, bf16[3,2,256,128]{3,2,1,0:T(8,128)(2,1)}, bf16[2,2,256,256]{3,2,1,0:T(8,128)(2,1)}, bf16[2,2,256,2...) custom-call(s32[1]{0:T(128)} %bitcast.3.rank.group, s32[8]{0:T(128)} %copy-done.91, ...), custom_call_target="tpu_custom_call" | custom-call | flops 36250001408 | bytes 25000000 | tf_op jit(solution)/shard_map/self_backward/pallas_call | solution.py:316
  979.9 8.0 fusion.12
  988.0 4.4 fusion.96
  996.1 4.0 fusion.123
  1000.2 4.7 add_add_fusion
  1010.7 15.0 %collective-permute-done.44 = bf16[128,2048]{1,0:T(8,128)(2,1)} collective-permute-done((bf16[128,2048]{1,0:T(8,128)(2,1)}, bf16[128,2048]{1,0:T(8,128)(2,1)}, u32[]{:S(2)}, u32[]{:S(2)}) %collective-permute-start.44) | collective-permute-done | bytes 524320 | tf_op jit(solution)/shard_map/ppermute | solution.py:517
  1032.0 7.1 add_convert_fusion
  1039.2 5.2 fusion.47
  1062.4 5.1 maximum_maximum_fusion
  1068.1 20.9 %collective-permute-done.36 = bf16[128,1280]{0,1:T(8,128)(2,1)} collective-permute-done((bf16[128,1280]{0,1:T(8,128)(2,1)S(1)}, bf16[128,1280]{0,1:T(8,128)(2,1)}, u32[]{:S(2)}, u32[]{:S(2)}) %collective-permute-start.36) | collective-permute-done | bytes 327712 | tf_op jit(solution)/shard_map/ppermute | solution.py:517
  1095.0 6.6 fusion.6
  1104.2 11.4 %reduce-scatter.10.cloned.1.call-done = bf16[128,896]{1,0:T(8,128)(2,1)} async-done(((bf16[1024,896]{1,0:T(8,128)(2,1)}), bf16[128,896]{1,0:T(8,128)(2,1)}) %reduce-scatter.10.cloned.1.call-update) | async-done | bytes 229392
  (621 shorter events, 266.7 us)
Async XLA Ops:
  7.2 110.7 %copy-start = (bf16[128,4096]{1,0:T(8,128)(2,1)S(1)}, bf16[128,4096]{1,0:T(8,128)(2,1)}, u32[]{:S(2)}) copy-start(bf16[128,4096]{1,0:T(8,128)(2,1)} %param.43) | copy-start | bytes 3145732
  7.2 87.0 %all-gather.8.cloned.1.call-start = ((), (), s32[]{:S(2)}) async-start(), calls=%async_computation.3 | async-start | bytes 7569408 | tf_op jit(solution)/shard_map/all_gather | solution.py:509
  10.2 143.8 %all-gather.10.cloned.1.call-start = ((), (), s32[]{:S(2)}) async-start(), calls=%async_computation.5 | async-start | bytes 3022848 | tf_op jit(solution)/shard_map/all_gather | solution.py:562
  14.4 45.9 %copy-start.102 = (bf16[128]{0:T(256)(128)(2,1)S(1)}, bf16[128]{0:T(256)(128)(2,1)}, u32[]{:S(2)}) copy-start(bf16[128]{0:T(256)(128)(2,1)} %param.36) | copy-start | bytes 772
  14.4 45.9 %copy-start.103 = (bf16[128]{0:T(256)(128)(2,1)S(1)}, bf16[128]{0:T(256)(128)(2,1)}, u32[]{:S(2)}) copy-start(bf16[128]{0:T(256)(128)(2,1)} %param.41) | copy-start | bytes 772
  14.4 45.9 %copy-start.104 = (bf16[128]{0:T(256)(128)(2,1)S(1)}, bf16[128]{0:T(256)(128)(2,1)}, u32[]{:S(2)}) copy-start(bf16[128]{0:T(256)(128)(2,1)} %param.42) | copy-start | bytes 772
  14.5 45.9 %copy-start.105 = (bf16[128]{0:T(256)(128)(2,1)S(1)}, bf16[128]{0:T(256)(128)(2,1)}, u32[]{:S(2)}) copy-start(bf16[128]{0:T(256)(128)(2,1)} %param.45) | copy-start | bytes 772
  14.5 45.9 %copy-start.106 = (bf16[128]{0:T(256)(128)(2,1)S(1)}, bf16[128]{0:T(256)(128)(2,1)}, u32[]{:S(2)}) copy-start(bf16[128]{0:T(256)(128)(2,1)} %param.46) | copy-start | bytes 772
  14.6 55.3 %copy-start.12 = (bf16[2,256,1024]{2,1,0:T(8,128)(2,1)}, bf16[2,256,1024]{2,1,0:T(8,128)(2,1)S(1)}, u32[]{:S(2)}) copy-start(bf16[2,256,1024]{2,1,0:T(8,128)(2,1)S(1)} %slice_bitcast_fusion.first) | copy-start | bytes 3145732
  14.6 26.6 %collective-permute-start.1 = (bf16[2,256,1024]{2,1,0:T(8,128)(2,1)S(1)}, bf16[2,256,1024]{2,1,0:T(8,128)(2,1)S(1)}, u32[]{:S(2)}, u32[]{:S(2)}) collective-permute-start(bf16[2,256,1024]{2,1,0:T(8,128)(2,1)S(1)} %slice_bitcast_fusion.first), channel_id=1, source_target_pairs={{0,16},{16,0},{8,24},{24,8},{1,17},{17,1},{9,25},{25,9},{2,18},{18... | collective-permute-start | bytes 3145736 | tf_op jit(solution)/shard_map/ppermute | solution.py:517
  16.7 53.2 %collective-permute-start = (bf16[2,256,1024]{2,1,0:T(8,128)(2,1)S(1)}, bf16[2,256,1024]{2,1,0:T(8,128)(2,1)}, u32[]{:S(2)}, u32[]{:S(2)}) collective-permute-start(bf16[2,256,1024]{2,1,0:T(8,128)(2,1)S(1)} %slice_bitcast_fusion.first), channel_id=1, source_target_pairs={{0,8},{8,0},{16,24},{24,16},{1,9},{9,1},{17,25},{25,17},{2,10},{10... | collective-permute-start | bytes 3145736 | tf_op jit(solution)/shard_map/ppermute | solution.py:513
  17.6 48.6 %collective-permute-start.3 = (bf16[2,128,1024]{2,1,0:T(8,128)(2,1)}, bf16[2,128,1024]{2,1,0:T(8,128)(2,1)}, u32[]{:S(2)}, u32[]{:S(2)}) collective-permute-start(bf16[2,128,1024]{2,1,0:T(8,128)(2,1)} %first.1), channel_id=1, source_target_pairs={{0,8},{8,0},{16,24},{24,16},{1,9},{9,1},{17,25},{25,17},{2,10},{10... | collective-permute-start | bytes 1572872 | tf_op jit(solution)/shard_map/ppermute | solution.py:513
  17.6 41.4 %collective-permute-start.4 = (bf16[2,128,1024]{2,1,0:T(8,128)(2,1)}, bf16[2,128,1024]{2,1,0:T(8,128)(2,1)}, u32[]{:S(2)}, u32[]{:S(2)}) collective-permute-start(bf16[2,128,1024]{2,1,0:T(8,128)(2,1)} %first.1), channel_id=1, source_target_pairs={{0,16},{16,0},{8,24},{24,8},{1,17},{17,1},{9,25},{25,9},{2,18},{18... | collective-permute-start | bytes 1572872 | tf_op jit(solution)/shard_map/ppermute | solution.py:517
  41.2 28.7 %collective-permute-start.2 = (bf16[2,256,1024]{2,1,0:T(8,128)(2,1)S(1)}, bf16[2,256,1024]{2,1,0:T(8,128)(2,1)}, u32[]{:S(2)}, u32[]{:S(2)}) collective-permute-start(bf16[2,256,1024]{2,1,0:T(8,128)(2,1)S(1)} %collective-permute-done.1.third), channel_id=1, source_target_pairs={{0,8},{8,0},{16,24},{24,16},{1,9},{9,1},{17,25},{25,17},{2,10},{10... | collective-permute-start | bytes 3145736 | tf_op jit(solution)/shard_map/ppermute | solution.py:513
  59.0 7.2 collective-permute-start.5
  95.9 196.3 %all-gather.12.cloned.1.call-start = ((), (), s32[]{:S(2)}) async-start(), calls=%async_computation.6 | async-start | bytes 2359296 | tf_op jit(solution)/shard_map/all_gather | solution.py:562
  123.8 168.4 %all-gather.14.cloned.1.call-start = ((), (), s32[]{:S(2)}) async-start(), calls=%async_computation.7 | async-start | bytes 2359296 | tf_op jit(solution)/shard_map/all_gather | solution.py:562
  153.9 851.1 %reduce-scatter.8.cloned.1.call-start = ((), (), s32[]{:S(2)}) async-start(), calls=%async_computation.4 | async-start | bytes 4718592 | tf_op jit(solution)/shard_map/reduce_scatter | solution.py:653
  153.9 138.3 %collective-permute-start.6 = (bf16[8,32,5248]{2,1,0:T(8,128)(2,1)}, bf16[8,32,5248]{2,1,0:T(8,128)(2,1)}, u32[]{:S(2)}, u32[]{:S(2)}) collective-permute-start(bf16[8,32,5248]{2,1,0:T(8,128)(2,1)} %bitcast.338), channel_id=1, source_target_pairs={{0,8},{8,0},{16,24},{24,16},{1,9},{9,1},{17,25},{25,17},{2,10},{10... | collective-permute-start | bytes 8060936 | tf_op jit(solution)/shard_map/ppermute | solution.py:513
  154.3 138.0 %collective-permute-start.7 = (bf16[8,32,5248]{2,1,0:T(8,128)(2,1)}, bf16[8,32,5248]{2,1,0:T(8,128)(2,1)}, u32[]{:S(2)}, u32[]{:S(2)}) collective-permute-start(bf16[8,32,5248]{2,1,0:T(8,128)(2,1)} %bitcast.339), channel_id=1, source_target_pairs={{0,16},{16,0},{8,24},{24,8},{1,17},{17,1},{9,25},{25,9},{2,18},{18... | collective-permute-start | bytes 8060936 | tf_op jit(solution)/shard_map/ppermute | solution.py:517
  292.3 19.6 %collective-permute-start.8 = (bf16[8,32,5248]{2,1,0:T(8,128)(2,1)}, bf16[8,32,5248]{2,1,0:T(8,128)(2,1)}, u32[]{:S(2)}, u32[]{:S(2)}) collective-permute-start(bf16[8,32,5248]{2,1,0:T(8,128)(2,1)} %collective-permute-done.7.third), channel_id=1, source_target_pairs={{0,8},{8,0},{16,24},{24,16},{1,9},{9,1},{17,25},{25,17},{2,10},{10... | collective-permute-start | bytes 8060936 | tf_op jit(solution)/shard_map/ppermute | solution.py:513
  309.6 78.0 %collective-permute-start.9 = (bf16[8,32,4096]{2,1,0:T(8,128)(2,1)S(1)}, bf16[8,32,4096]{2,1,0:T(8,128)(2,1)}, u32[]{:S(2)}, u32[]{:S(2)}) collective-permute-start(bf16[8,32,4096]{2,1,0:T(8,128)(2,1)S(1)} %bitcast.342), channel_id=1, source_target_pairs={{0,8},{8,0},{16,24},{24,16},{1,9},{9,1},{17,25},{25,17},{2,10},{10... | collective-permute-start | bytes 6291464 | tf_op jit(solution)/shard_map/ppermute | solution.py:513
  309.7 77.9 %collective-permute-start.10 = (bf16[8,32,4096]{2,1,0:T(8,128)(2,1)S(1)}, bf16[8,32,4096]{2,1,0:T(8,128)(2,1)}, u32[]{:S(2)}, u32[]{:S(2)}) collective-permute-start(bf16[8,32,4096]{2,1,0:T(8,128)(2,1)S(1)} %bitcast.343), channel_id=1, source_target_pairs={{0,16},{16,0},{8,24},{24,8},{1,17},{17,1},{9,25},{25,9},{2,18},{18... | collective-permute-start | bytes 6291464 | tf_op jit(solution)/shard_map/ppermute | solution.py:517
  309.7 77.8 %collective-permute-start.11 = (bf16[8,128,1024]{2,1,0:T(8,128)(2,1)}, bf16[8,128,1024]{2,1,0:T(8,128)(2,1)}, u32[]{:S(2)}, u32[]{:S(2)}) collective-permute-start(bf16[8,128,1024]{2,1,0:T(8,128)(2,1)} %bitcast.35.first), channel_id=1, source_target_pairs={{0,8},{8,0},{16,24},{24,16},{1,9},{9,1},{17,25},{25,17},{2,10},{10... | collective-permute-start | bytes 6291464 | tf_op jit(solution)/shard_map/ppermute | solution.py:513
  310.4 91.1 %collective-permute-start.12 = (bf16[8,128,1024]{2,1,0:T(8,128)(2,1)}, bf16[8,128,1024]{2,1,0:T(8,128)(2,1)}, u32[]{:S(2)}, u32[]{:S(2)}) collective-permute-start(bf16[8,128,1024]{2,1,0:T(8,128)(2,1)} %bitcast.35.first), channel_id=1, source_target_pairs={{0,16},{16,0},{8,24},{24,8},{1,17},{17,1},{9,25},{25,9},{2,18},{18... | collective-permute-start | bytes 6291464 | tf_op jit(solution)/shard_map/ppermute | solution.py:517
  340.6 60.9 %copy-start.89 = (f32[1,1024]{1,0:T(1,128)}, f32[1,1024]{1,0:T(1,128)S(1)}, u32[]{:S(2)}) copy-start(f32[1,1024]{1,0:T(1,128)S(1)} %get-tuple-element.469) | copy-start | bytes 12292
  340.6 60.9 %copy-start.85 = (f32[1536]{0:T(1024)}, f32[1536]{0:T(1024)S(1)}, u32[]{:S(2)}) copy-start(f32[1536]{0:T(1024)S(1)} %broadcast_multiply_fusion.7) | copy-start | bytes 18436
  344.3 57.2 %copy-start.87 = (f32[1536]{0:T(1024)}, f32[1536]{0:T(1024)S(1)}, u32[]{:S(2)}) copy-start(f32[1536]{0:T(1024)S(1)} %add_rsqrt_fusion.2) | copy-start | bytes 18436
  412.7 10.5 collective-permute-start.13
  413.9 40.1 %collective-permute-start.14 = (bf16[8,128,1024]{2,1,0:T(8,128)(2,1)}, bf16[8,128,1024]{2,1,0:T(8,128)(2,1)}, u32[]{:S(2)}, u32[]{:S(2)}) collective-permute-start(bf16[8,128,1024]{2,1,0:T(8,128)(2,1)} %collective-permute-done.12.third), channel_id=1, source_target_pairs={{0,8},{8,0},{16,24},{24,16},{1,9},{9,1},{17,25},{25,17},{2,10},{10... | collective-permute-start | bytes 6291464 | tf_op jit(solution)/shard_map/ppermute | solution.py:513
  546.3 24.2 %collective-permute-start.15 = (bf16[4096,256]{1,0:T(8,128)(2,1)}, bf16[4096,256]{1,0:T(8,128)(2,1)S(1)}, u32[]{:S(2)}, u32[]{:S(2)}) collective-permute-start(bf16[4096,256]{1,0:T(8,128)(2,1)} %convolution_convert_fusion.1), channel_id=1, source_target_pairs={{0,8},{8,0},{16,24},{24,16},{1,9},{9,1},{17,25},{25,17},{2,10},{10... | collective-permute-start | bytes 6291464 | tf_op jit(solution)/shard_map/ppermute | solution.py:513
  553.8 26.6 %collective-permute-start.16 = (bf16[4096,256]{1,0:T(8,128)(2,1)}, bf16[4096,256]{1,0:T(8,128)(2,1)}, u32[]{:S(2)}, u32[]{:S(2)}) collective-permute-start(bf16[4096,256]{1,0:T(8,128)(2,1)} %convolution_convert_fusion), channel_id=1, source_target_pairs={{0,8},{8,0},{16,24},{24,16},{1,9},{9,1},{17,25},{25,17},{2,10},{10... | collective-permute-start | bytes 6291464 | tf_op jit(solution)/shard_map/ppermute | solution.py:513
  580.4 28.6 %collective-permute-start.17 = (bf16[1024,1024]{1,0:T(8,128)(2,1)}, bf16[1024,1024]{1,0:T(8,128)(2,1)}, u32[]{:S(2)}, u32[]{:S(2)}) collective-permute-start(bf16[1024,1024]{1,0:T(8,128)(2,1)} %fusion.99), channel_id=1, source_target_pairs={{0,8},{8,0},{16,24},{24,16},{1,9},{9,1},{17,25},{25,17},{2,10},{10... | collective-permute-start | bytes 6291464 | tf_op jit(solution)/shard_map/ppermute | solution.py:513
  580.4 33.6 %collective-permute-start.18 = (bf16[1024,1024]{1,0:T(8,128)(2,1)}, bf16[1024,1024]{1,0:T(8,128)(2,1)}, u32[]{:S(2)}, u32[]{:S(2)}) collective-permute-start(bf16[1024,1024]{1,0:T(8,128)(2,1)} %fusion.102), channel_id=1, source_target_pairs={{0,8},{8,0},{16,24},{24,16},{1,9},{9,1},{17,25},{25,17},{2,10},{10... | collective-permute-start | bytes 6291464 | tf_op jit(solution)/shard_map/ppermute | solution.py:513
  580.9 92.9 %collective-permute-start.20 = (bf16[4096,256]{1,0:T(8,128)(2,1)}, bf16[4096,256]{1,0:T(8,128)(2,1)}, u32[]{:S(2)}, u32[]{:S(2)}) collective-permute-start(bf16[4096,256]{1,0:T(8,128)(2,1)} %add_convert_fusion.8), channel_id=1, source_target_pairs={{0,16},{16,0},{8,24},{24,8},{1,17},{17,1},{9,25},{25,9},{2,18},{18... | collective-permute-start | bytes 6291464 | tf_op jit(solution)/shard_map/ppermute | solution.py:517
  620.4 53.4 %collective-permute-start.19 = (bf16[1024,1024]{1,0:T(8,128)(2,1)}, bf16[1024,1024]{1,0:T(8,128)(2,1)S(1)}, u32[]{:S(2)}, u32[]{:S(2)}) collective-permute-start(bf16[1024,1024]{1,0:T(8,128)(2,1)} %add_convert_fusion.7), channel_id=1, source_target_pairs={{0,16},{16,0},{8,24},{24,8},{1,17},{17,1},{9,25},{25,9},{2,18},{18... | collective-permute-start | bytes 6291464 | tf_op jit(solution)/shard_map/ppermute | solution.py:517
  713.2 38.9 %collective-permute-start.21 = (bf16[1024,1280]{0,1:T(8,128)(2,1)}, bf16[1024,1280]{0,1:T(8,128)(2,1)}, u32[]{:S(2)}, u32[]{:S(2)}) collective-permute-start(bf16[1024,1280]{0,1:T(8,128)(2,1)} %fusion.142), channel_id=1, source_target_pairs={{0,8},{8,0},{16,24},{24,16},{1,9},{9,1},{17,25},{25,17},{2,10},{10... | collective-permute-start | bytes 7864328 | tf_op jit(solution)/shard_map/ppermute | solution.py:513
  720.7 34.3 %collective-permute-start.22 = (bf16[1024,1280]{0,1:T(8,128)(2,1)}, bf16[1024,1280]{0,1:T(8,128)(2,1)}, u32[]{:S(2)}, u32[]{:S(2)}) collective-permute-start(bf16[1024,1280]{0,1:T(8,128)(2,1)} %fusion.139), channel_id=1, source_target_pairs={{0,8},{8,0},{16,24},{24,16},{1,9},{9,1},{17,25},{25,17},{2,10},{10... | collective-permute-start | bytes 7864328 | tf_op jit(solution)/shard_map/ppermute | solution.py:513
  726.3 333.9 %reduce-scatter.12.cloned.1.call-start = ((), (), s32[]{:S(2)}) async-start(), calls=%async_computation.9 | async-start | bytes 2949120
  792.0 74.4 %collective-permute-start.23 = (bf16[1024,1280]{0,1:T(8,128)(2,1)S(1)}, bf16[1024,1280]{0,1:T(8,128)(2,1)}, u32[]{:S(2)}, u32[]{:S(2)}) collective-permute-start(bf16[1024,1280]{0,1:T(8,128)(2,1)S(1)} %add_convert_fusion.3), channel_id=1, source_target_pairs={{0,16},{16,0},{8,24},{24,8},{1,17},{17,1},{9,25},{25,9},{2,18},{18... | collective-permute-start | bytes 7864328 | tf_op jit(solution)/shard_map/ppermute | solution.py:517
  792.4 61.6 %collective-permute-start.24 = (bf16[2,128,1024]{2,1,0:T(8,128)(2,1)}, bf16[2,128,1024]{2,1,0:T(8,128)(2,1)}, u32[]{:S(2)}, u32[]{:S(2)}) collective-permute-start(bf16[2,128,1024]{2,1,0:T(8,128)(2,1)} %get-tuple-element.224), channel_id=1, source_target_pairs={{0,8},{8,0},{16,24},{24,16},{1,9},{9,1},{17,25},{25,17},{2,10},{10... | collective-permute-start | bytes 1572872 | tf_op jit(solution)/shard_map/ppermute | solution.py:513
  793.4 69.3 %collective-permute-start.26 = (bf16[2,128,1024]{2,1,0:T(8,128)(2,1)}, bf16[2,128,1024]{2,1,0:T(8,128)(2,1)}, u32[]{:S(2)}, u32[]{:S(2)}) collective-permute-start(bf16[2,128,1024]{2,1,0:T(8,128)(2,1)} %get-tuple-element.225), channel_id=1, source_target_pairs={{0,8},{8,0},{16,24},{24,16},{1,9},{9,1},{17,25},{25,17},{2,10},{10... | collective-permute-start | bytes 1572872 | tf_op jit(solution)/shard_map/ppermute | solution.py:513
  793.5 50.6 %collective-permute-start.39 = (f32[6,1024]{1,0:T(8,128)}, f32[6,1024]{1,0:T(8,128)}, u32[]{:S(2)}, u32[]{:S(2)}) collective-permute-start(f32[6,1024]{1,0:T(8,128)} %stack.55), channel_id=1, source_target_pairs={{0,8},{8,0},{16,24},{24,16},{1,9},{9,1},{17,25},{25,17},{2,10},{10... | collective-permute-start | bytes 73736 | tf_op jit(solution)/shard_map/ppermute | solution.py:678
  844.9 5.1 collective-permute-start.40
  850.0 2.8 collective-permute-start.41
  852.8 5.3 collective-permute-start.42
  855.5 10.1 collective-permute-start.25
  858.1 4.0 collective-permute-start.43
  910.8 22.0 %collective-permute-start.27 = (bf16[1024,896]{0,1:T(8,128)(2,1)}, bf16[1024,896]{0,1:T(8,128)(2,1)}, u32[]{:S(2)}, u32[]{:S(2)}) collective-permute-start(bf16[1024,896]{0,1:T(8,128)(2,1)} %pad_maximum_fusion.4), channel_id=1, source_target_pairs={{0,8},{8,0},{16,24},{24,16},{1,9},{9,1},{17,25},{25,17},{2,10},{10... | collective-permute-start | bytes 5505032 | tf_op jit(solution)/shard_map/ppermute | solution.py:513
  915.7 20.5 %collective-permute-start.28 = (bf16[1024,896]{0,1:T(8,128)(2,1)}, bf16[1024,896]{0,1:T(8,128)(2,1)}, u32[]{:S(2)}, u32[]{:S(2)}) collective-permute-start(bf16[1024,896]{0,1:T(8,128)(2,1)} %pad_maximum_fusion.5), channel_id=1, source_target_pairs={{0,8},{8,0},{16,24},{24,16},{1,9},{9,1},{17,25},{25,17},{2,10},{10... | collective-permute-start | bytes 5505032 | tf_op jit(solution)/shard_map/ppermute | solution.py:513
  920.3 195.3 %reduce-scatter.10.cloned.1.call-start = ((), (), s32[]{:S(2)}) async-start(), calls=%async_computation.8 | async-start | bytes 2064384
  973.6 54.0 %collective-permute-start.29 = (bf16[1024,896]{0,1:T(8,128)(2,1)}, bf16[1024,896]{0,1:T(8,128)(2,1)}, u32[]{:S(2)}, u32[]{:S(2)}) collective-permute-start(bf16[1024,896]{0,1:T(8,128)(2,1)} %fusion.26), channel_id=1, source_target_pairs={{0,16},{16,0},{8,24},{24,8},{1,17},{17,1},{9,25},{25,9},{2,18},{18... | collective-permute-start | bytes 5505032 | tf_op jit(solution)/shard_map/ppermute | solution.py:517
  1004.9 20.8 %collective-permute-start.44 = (bf16[128,2048]{1,0:T(8,128)(2,1)}, bf16[128,2048]{1,0:T(8,128)(2,1)}, u32[]{:S(2)}, u32[]{:S(2)}) collective-permute-start(bf16[128,2048]{1,0:T(8,128)(2,1)} %reduce-scatter.8.cloned.1.call-done), channel_id=1, source_target_pairs={{0,16},{16,0},{8,24},{24,8},{1,17},{17,1},{9,25},{25,9},{2,18},{18... | collective-permute-start | bytes 1572872 | tf_op jit(solution)/shard_map/ppermute | solution.py:517
  1009.4 41.7 %collective-permute-start.45 = (bf16[128,2048]{1,0:T(8,128)(2,1)}, bf16[128,2048]{1,0:T(8,128)(2,1)S(1)}, u32[]{:S(2)}, u32[]{:S(2)}) collective-permute-start(bf16[128,2048]{1,0:T(8,128)(2,1)} %reduce-scatter.8.cloned.1.call-done), channel_id=1, source_target_pairs={{0,8},{8,0},{16,24},{24,16},{1,9},{9,1},{17,25},{25,17},{2,10},{10... | collective-permute-start | bytes 1572872 | tf_op jit(solution)/shard_map/ppermute | solution.py:513
  1025.7 25.4 %collective-permute-start.46 = (bf16[128,2048]{1,0:T(8,128)(2,1)}, bf16[128,2048]{1,0:T(8,128)(2,1)}, u32[]{:S(2)}, u32[]{:S(2)}) collective-permute-start(bf16[128,2048]{1,0:T(8,128)(2,1)} %collective-permute-done.44), channel_id=1, source_target_pairs={{0,8},{8,0},{16,24},{24,16},{1,9},{9,1},{17,25},{25,17},{2,10},{10... | collective-permute-start | bytes 1572872 | tf_op jit(solution)/shard_map/ppermute | solution.py:513
  1047.9 7.3 collective-permute-start.31
  1047.9 41.9 %collective-permute-start.30 = (bf16[2,256,1024]{1,2,0:T(8,128)(2,1)}, bf16[2,256,1024]{1,2,0:T(8,128)(2,1)}, u32[]{:S(2)}, u32[]{:S(2)}) collective-permute-start(bf16[2,256,1024]{1,2,0:T(8,128)(2,1)} %get-tuple-element.378), channel_id=1, source_target_pairs={{0,8},{8,0},{16,24},{24,16},{1,9},{9,1},{17,25},{25,17},{2,10},{10... | collective-permute-start | bytes 3145736 | tf_op jit(solution)/shard_map/ppermute | solution.py:513
  1057.0 32.8 %collective-permute-start.32 = (bf16[2,256,1024]{1,2,0:T(8,128)(2,1)S(1)}, bf16[2,256,1024]{1,2,0:T(8,128)(2,1)S(1)}, u32[]{:S(2)}, u32[]{:S(2)}) collective-permute-start(bf16[2,256,1024]{1,2,0:T(8,128)(2,1)S(1)} %fusion.89), channel_id=1, source_target_pairs={{0,16},{16,0},{8,24},{24,8},{1,17},{17,1},{9,25},{25,9},{2,18},{18... | collective-permute-start | bytes 3145736 | tf_op jit(solution)/shard_map/ppermute | solution.py:517
  1061.4 27.5 %collective-permute-start.36 = (bf16[128,1280]{0,1:T(8,128)(2,1)S(1)}, bf16[128,1280]{0,1:T(8,128)(2,1)}, u32[]{:S(2)}, u32[]{:S(2)}) collective-permute-start(bf16[128,1280]{0,1:T(8,128)(2,1)S(1)} %copy.192), channel_id=1, source_target_pairs={{0,16},{16,0},{8,24},{24,8},{1,17},{17,1},{9,25},{25,9},{2,18},{18... | collective-permute-start | bytes 983048 | tf_op jit(solution)/shard_map/ppermute | solution.py:517
  1067.5 34.1 %collective-permute-start.37 = (bf16[128,1280]{0,1:T(8,128)(2,1)S(1)}, bf16[128,1280]{0,1:T(8,128)(2,1)S(1)}, u32[]{:S(2)}, u32[]{:S(2)}) collective-permute-start(bf16[128,1280]{0,1:T(8,128)(2,1)S(1)} %copy.192), channel_id=1, source_target_pairs={{0,8},{8,0},{16,24},{24,16},{1,9},{9,1},{17,25},{25,17},{2,10},{10... | collective-permute-start | bytes 983048 | tf_op jit(solution)/shard_map/ppermute | solution.py:513
  1088.9 12.7 %collective-permute-start.38 = (bf16[128,1280]{0,1:T(8,128)(2,1)}, bf16[128,1280]{0,1:T(8,128)(2,1)}, u32[]{:S(2)}, u32[]{:S(2)}) collective-permute-start(bf16[128,1280]{0,1:T(8,128)(2,1)} %collective-permute-done.36), channel_id=1, source_target_pairs={{0,8},{8,0},{16,24},{24,16},{1,9},{9,1},{17,25},{25,17},{2,10},{10... | collective-permute-start | bytes 983048 | tf_op jit(solution)/shard_map/ppermute | solution.py:513
  1116.7 5.6 collective-permute-start.33
  1120.0 6.8 collective-permute-start.34
  1122.2 4.6 collective-permute-start.35
  (152 other events, 1028.1 us)
Sparse Core Ops, SparseCore 0:
  11.4 82.7 all-gather.7
  96.9 51.8 all-gather.9
  151.5 47.4 all-gather.11
  201.6 47.6 all-gather.13
  726.4 86.0 reduce-scatter.7
  920.4 68.3 reduce-scatter.11
  1051.3 64.2 reduce-scatter.9

commit v3 on v2

--- a/solution.py
+++ b/solution.py
@@ -38,10 +38,9 @@
     return jnp.concatenate([jnp.where(low, value, zero), jnp.where(low, zero, value)], axis=0)
 
 
-def self_parts(place, query_ref, own_key_ref, own_value_ref):
-    slot, pair = place // 2, place % 2
+def self_parts(slot, pair, query_ref, own_key_ref, own_value_ref):
     rows = pl.ds(pl.multiple_of(slot * BLK, BLK), BLK)
-    lanes = pl.ds(pl.multiple_of(pair * 128, 128), 128)
+    lanes = slice(128 * pair, 128 * (pair + 1))
     total = query_ref.shape[0] * BLK
     low = low_lanes(total)
     query = query_ref[:, 0, rows, lanes].reshape(total, 128)
@@ -51,7 +50,35 @@
     own_key = jnp.concatenate([zero, own_key], axis=0)
     own_value = own_value_ref[:, 0, rows, lanes].reshape(total - BLK, 128).astype(F32)
     own_value = jnp.concatenate([zero, own_value], axis=0)
-    return slot, pair, rows, lanes, low, pairs, own_key, own_value
+    return rows, lanes, low, pairs, own_key, own_value
+
+
+def slot_pairs(blocks, seq, work):
+    def step(place, carry):
+        first, second = blocks[2 * place], blocks[2 * place + 1]
+        turned = (first > second).astype(jnp.int32)
+        near, far = 2 * place + turned, 2 * place + 1 - turned
+        near_block, far_block = jnp.minimum(first, second), jnp.maximum(first, second)
+        whole = seq // CHUNK
+        count = (near_block * BLK) // CHUNK + 1
+        for parts in range(1, whole // 2 + 1):
+
+            @pl.when(count == parts)
+            def _():
+                work(
+                    [
+                        (slot, block, pair, chunks * CHUNK)
+                        for slot, block, chunks in (
+                            (near, near_block, parts),
+                            (far, far_block, whole + 1 - parts),
+                        )
+                        for pair in range(2)
+                    ]
+                )
+
+        return carry
+
+    lax.fori_loop(0, blocks.shape[0] // 2, step, 0)
 
 
 def self_forward_kernel(
@@ -72,15 +99,14 @@
     streams = query_ref.shape[0]
     total = streams * BLK
 
-    def step(place, carry):
-        slot, pair, rows, lanes, low, pairs, own_key, own_value = self_parts(
-            place, query_ref, own_key_ref, own_value_ref
+    def scored(slot, block, pair, width):
+        rows, lanes, low, pairs, own_key, own_value = self_parts(
+            slot, pair, query_ref, own_key_ref, own_value_ref
         )
-        block = blocks[slot]
+        span = slice(seq - width, seq)
         rel = rel_ref[:, 0, rows, :].reshape(total, 128).astype(F32)
-        table = jnp.concatenate(
-            [pltpu.roll(rel, pair * 64, 1), pltpu.roll(rel, pair * 64 + 96, 1)], axis=0
-        )
+        first = pltpu.roll(rel, 64, 1) if pair else rel
+        table = jnp.concatenate([first, pltpu.roll(rel, 32 if pair else 96, 1)], axis=0)
         lane = lax.broadcasted_iota(jnp.int32, (2 * total, 128), 1)
         own = jnp.where(lane == own_ref[0], table, 0.0)
         own = own + pairs.astype(F32) * jnp.concatenate([own_key, own_key], axis=0)
@@ -88,50 +114,51 @@
         row = lax.broadcasted_iota(jnp.int32, (2 * total, 1), 0)
         main = jnp.logical_or(row < BLK, jnp.logical_and(row >= total, row < total + BLK))
         own = jnp.where(main, FILLER, own)
-        count = (block * BLK) // CHUNK + 1
-        for parts in range(1, seq // CHUNK + 1):
-            width = parts * CHUNK
-
-            @pl.when(count == parts)
-            def _():
-                span = slice(seq - width, seq)
-                index = index_ref[rows, span]
-                bias = [
-                    jnp.take_along_axis(
-                        table,
-                        jnp.concatenate([index[:, start : start + 128]] * (2 * streams), axis=0),
-                        axis=1,
-                    )
-                    for start in range(0, width, 128)
-                ]
-                scores = dot_nt(pairs, key_ref[0, span, lanes]) + jnp.concatenate(bias, axis=1)
-                column = lax.broadcasted_iota(jnp.int32, (2 * total, CHUNK), 1)
-                seen = column >= width - BLK * (block + 1)
-                first = jnp.where(seen, scores[:, :CHUNK], FILLER)
-                scores = (
-                    jnp.concatenate([first, scores[:, CHUNK:]], axis=1) if parts > 1 else first
-                )
-                top = jnp.maximum(jnp.max(scores, axis=1, keepdims=True), own)
-                weights = jnp.exp(scores - top)
-                own_weight = jnp.exp(own - top)
-                inverse = 1.0 / (jnp.sum(weights, axis=1, keepdims=True) + own_weight)
-                probs = (weights * inverse).astype(BF16)
-                prob_ref[0, pair, slot, :, span] = probs
-                own_prob = own_weight * inverse
-                own_prob_ref[0, pair, slot] = jnp.broadcast_to(own_prob, (2 * total, 128)).astype(
-                    BF16
-                )
-                mixed = dot_nn(probs, value_ref[0, span, lanes])
-                result = jnp.where(
-                    low,
-                    mixed[:total] + own_prob[:total] * own_value,
-                    mixed[total:] + own_prob[total:] * own_value,
-                )
-                out_ref[:, 0, rows, lanes] = result.astype(BF16).reshape(streams, BLK, 128)
-
-        return carry
-
-    lax.fori_loop(0, 2 * blocks.shape[0], step, 0)
+        index = index_ref[rows, span]
+        bias = [
+            jnp.take_along_axis(
+                table,
+                jnp.concatenate([index[:, start : start + 128]] * (2 * streams), axis=0),
+                axis=1,
+            )
+            for start in range(0, width, 128)
+        ]
+        scores = dot_nt(pairs, key_ref[0, span, lanes]) + jnp.concatenate(bias, axis=1)
+        column = lax.broadcasted_iota(jnp.int32, (2 * total, CHUNK), 1)
+        seen = column >= width - BLK * (block + 1)
+        first = jnp.where(seen, scores[:, :CHUNK], FILLER)
+        scores = first if width == CHUNK else jnp.concatenate([first, scores[:, CHUNK:]], axis=1)
+        top = jnp.maximum(jnp.max(scores, axis=1, keepdims=True), own)
+        return scores, own, top, own_value
+
+    def work(items):
+        stage = [scored(*item) for item in items]
+        stage = [
+            (jnp.exp(scores - top), jnp.exp(own - top), own_value)
+            for scores, own, top, own_value in stage
+        ]
+        stage = [
+            (weights, own, 1.0 / (jnp.sum(weights, axis=1, keepdims=True) + own), own_value)
+            for weights, own, own_value in stage
+        ]
+        low = low_lanes(total)
+        for (slot, block, pair, width), (weights, own, inverse, own_value) in zip(items, stage):
+            rows = pl.ds(pl.multiple_of(slot * BLK, BLK), BLK)
+            lanes = slice(128 * pair, 128 * (pair + 1))
+            span = slice(seq - width, seq)
+            probs = (weights * inverse).astype(BF16)
+            prob_ref[0, pair, slot, :, span] = probs
+            own_prob = own * inverse
+            own_prob_ref[0, pair, slot] = jnp.broadcast_to(own_prob, (2 * total, 128)).astype(BF16)
+            mixed = dot_nn(probs, value_ref[0, span, lanes])
+            result = jnp.where(
+                low,
+                mixed[:total] + own_prob[:total] * own_value,
+                mixed[total:] + own_prob[total:] * own_value,
+            )
+            out_ref[:, 0, rows, lanes] = result.astype(BF16).reshape(streams, BLK, 128)
+
+    slot_pairs(blocks, seq, work)
 
 
 def self_backward_kernel(
@@ -163,11 +190,11 @@
     key_total[...] = jnp.zeros_like(key_total)
     value_total[...] = jnp.zeros_like(value_total)
 
-    def step(place, carry):
-        slot, pair, rows, lanes, low, pairs, own_key, own_value = self_parts(
-            place, query_ref, own_key_ref, own_value_ref
+    def scored(slot, block, pair, width):
+        rows, lanes, low, pairs, own_key, own_value = self_parts(
+            slot, pair, query_ref, own_key_ref, own_value_ref
         )
-        block = blocks[slot]
+        span = slice(seq - width, seq)
         grads = pair_rows(grad_ref[:, 0, rows, lanes].reshape(total, 128), low)
         wide = grads.astype(F32)
         mixed = out_ref[:, 0, rows, lanes].reshape(total, 128).astype(F32)
@@ -183,50 +210,53 @@
         part = own_prob * wide
         part = (part[:total] + part[total:])[BLK:]
         grad_own_value_ref[:, 0, rows, lanes] = part.astype(BF16).reshape(streams - 1, BLK, 128)
-        count = (block * BLK) // CHUNK + 1
-        for parts in range(1, seq // CHUNK + 1):
-            width = parts * CHUNK
-
-            @pl.when(count == parts)
-            def _():
-                span = slice(seq - width, seq)
-                probs = prob_ref[0, pair, slot, :, span]
-                grad_probs = dot_nt(grads, value_ref[0, span, lanes])
-                grad_scores = probs.astype(F32) * (grad_probs - delta)
-                low_scores = grad_scores.astype(BF16)
-                value_total[span, lanes] += dot_tn(probs, grads)
-                key_total[span, lanes] += dot_tn(low_scores, pairs)
-                moved = dot_nn(low_scores, key_ref[0, span, lanes])
-                moved = jnp.where(
-                    low,
-                    moved[:total] + grad_own[:total] * own_key,
-                    moved[total:] + grad_own[total:] * own_key,
-                )
-                grad_query_ref[:, 0, rows, lanes] = (
-                    (moved * SCALE).astype(BF16).reshape(streams, BLK, 128)
-                )
-                pad = jnp.zeros((BLK, 128), F32)
-                skewed = []
-                for start in range(0, 2 * total, BLK):
-                    piece = jnp.concatenate([grad_scores[start : start + BLK], pad], axis=1)
-                    skewed.append(pltpu.roll(piece, 0, 1, stride=1, stride_axis=0).astype(BF16))
-                begin = pl.multiple_of(BLK * (block + 1) - width + CHUNK, BLK)
-                hots = hot_ref[pl.ds(begin, width + 128), :]
-                sums = dot_nn(jnp.concatenate(skewed, axis=0), hots)
-                lane = lax.broadcasted_iota(jnp.int32, (2 * total, 128), 1)
-                sums = sums + jnp.where(lane == own_ref[0], grad_own, 0.0)
-                sums = pltpu.roll(sums[:total], pair * 64, 1) + pltpu.roll(
-                    sums[total:], pair * 64 + BUCKETS, 1
-                )
-                lane = lax.broadcasted_iota(jnp.int32, (total, 128), 1)
-                mine = jnp.logical_and(lane >= 64 * pair, lane < 64 * pair + 64)
-                before = grad_rel_ref[:, 0, rows, :].reshape(total, 128)
-                sums = jnp.where(mine, sums.astype(BF16), before)
-                grad_rel_ref[:, 0, rows, :] = sums.reshape(streams, BLK, 128)
-
-        return carry
-
-    lax.fori_loop(0, 2 * blocks.shape[0], step, 0)
+        probs = prob_ref[0, pair, slot, :, span]
+        grad_probs = dot_nt(grads, value_ref[0, span, lanes])
+        grad_scores = probs.astype(F32) * (grad_probs - delta)
+        return pairs, grads, own_key, grad_own, probs, grad_scores
+
+    def skew(block, width, grad_scores, grad_own):
+        pad = jnp.zeros((BLK, 128), F32)
+        skewed = []
+        for start in range(0, 2 * total, BLK):
+            piece = jnp.concatenate([grad_scores[start : start + BLK], pad], axis=1)
+            skewed.append(pltpu.roll(piece, 0, 1, stride=1, stride_axis=0).astype(BF16))
+        begin = pl.multiple_of(BLK * (block + 1) - width + CHUNK, BLK)
+        sums = dot_nn(jnp.concatenate(skewed, axis=0), hot_ref[pl.ds(begin, width + 128), :])
+        lane = lax.broadcasted_iota(jnp.int32, (2 * total, 128), 1)
+        return sums + jnp.where(lane == own_ref[0], grad_own, 0.0)
+
+    def work(items):
+        stage = [scored(*item) for item in items]
+        low = low_lanes(total)
+        sums = []
+        for (slot, block, pair, width), values in zip(items, stage):
+            pairs, grads, own_key, grad_own, probs, grad_scores = values
+            rows = pl.ds(pl.multiple_of(slot * BLK, BLK), BLK)
+            lanes = slice(128 * pair, 128 * (pair + 1))
+            span = slice(seq - width, seq)
+            low_scores = grad_scores.astype(BF16)
+            value_total[span, lanes] += dot_tn(probs, grads)
+            key_total[span, lanes] += dot_tn(low_scores, pairs)
+            moved = dot_nn(low_scores, key_ref[0, span, lanes])
+            moved = jnp.where(
+                low,
+                moved[:total] + grad_own[:total] * own_key,
+                moved[total:] + grad_own[total:] * own_key,
+            )
+            grad_query_ref[:, 0, rows, lanes] = (
+                (moved * SCALE).astype(BF16).reshape(streams, BLK, 128)
+            )
+            sums.append(skew(block, width, grad_scores, grad_own))
+        for place in range(0, len(items), 2):
+            slot = items[place][0]
+            rows = pl.ds(pl.multiple_of(slot * BLK, BLK), BLK)
+            result = sums[place][:total] + pltpu.roll(sums[place][total:], BUCKETS, 1)
+            result = result + pltpu.roll(sums[place + 1][:total], 2 * BUCKETS, 1)
+            result = result + pltpu.roll(sums[place + 1][total:], 3 * BUCKETS, 1)
+            grad_rel_ref[:, 0, rows, :] = result.astype(BF16).reshape(streams, BLK, 128)
+
+    slot_pairs(blocks, seq, work)
     grad_key_ref[0] = key_total[...].astype(BF16)
     grad_value_ref[0] = value_total[...].astype(BF16)
 
@@ -285,7 +315,7 @@
             jax.ShapeDtypeStruct((seqs, width // 128, slots, total, 128), BF16),
         ],
         compiler_params=pltpu.CompilerParams(vmem_limit_bytes=LIMIT),
-        cost_estimate=estimate(150e9, 80e6),
+        cost_estimate=estimate(88e9, 80e6),
         name="self_forward",
     )(blocks, own, query, rel, own_key, own_value, keys, values, index)
 
@@ -349,7 +379,7 @@
             memory_shape,
         ],
         compiler_params=pltpu.CompilerParams(vmem_limit_bytes=LIMIT),
-        cost_estimate=estimate(145e9 / 4, 100e6 / 4),
+        cost_estimate=estimate(27e9, 25e6),
         name="self_backward",
     )(group, blocks, own, query, own_key, own_value, keys, values, hot, mixed, grad, probs, own_probs)
 
@@ -611,25 +641,28 @@
         self.part = part
         self.rank = lax.axis_index("ctx")
 
-    def begin(self):
+    def begin(self, both=True):
         if self.ranks != 4:
             every = [self.part(index, index).astype(BF16) for index in range(self.ranks)]
             self.values = (jnp.stack(every),)
             return
-        corner = self.part(self.rank ^ 3, 3).astype(BF16)
-        self.values = (corner, self.part(self.rank ^ 1, 1).astype(BF16))
+        self.values = (self.part(self.rank ^ 3, 3).astype(BF16),)
+        if both:
+            self.late()
+
+    def late(self):
+        self.values = self.values + (self.part(self.rank ^ 1, 1).astype(BF16),)
 
     def turn(self):
         if self.ranks != 4:
             return
-        corner, partner = (swap(value) for value in self.values)
+        corner, partner = swap(self.values[0]), self.values[1:]
         side = (self.part(self.rank ^ 2, 2) + corner.astype(F32)).astype(BF16)
-        self.values = (side, partner)
+        self.values = (side,) + tuple(swap(value) for value in partner)
 
     def fetch(self):
         if self.ranks == 4:
-            side, partner = self.values
-            self.values = (pass_across(side), partner)
+            self.values = (pass_across(self.values[0]),) + self.values[1:]
 
     def end(self):
         if self.ranks != 4:
@@ -785,9 +818,8 @@
     mixed, probs, own_probs = self_forward(
         own_blocks, own, query, rel, own_keys, own_values, keys, values, index
     )
-    mixed, middle, w_inner, w_outer = tie(mixed, middle, w_inner, w_outer)
+    mixed, middle, w_inner = tie(mixed, middle, w_inner)
     w_inner = gather_pass(w_inner, ranks)
-    w_outer = gather_pass(w_outer, ranks)
     full = gather_rest(middle, ranks)
     w_out, c_query, c_key, c_value, c_out = (
         full[:, start : start + width] for start in range(0, 5 * width, width)
@@ -800,17 +832,20 @@
     h_one = normal_one * gain_one + shift_one
     h_one_low = h_one.astype(BF16)
     cross_query = dot_nn(h_one_low, c_query).astype(BF16).reshape(shape)
+    cross_query, w_outer = tie(cross_query, w_outer)
+    w_outer = gather_pass(w_outer, ranks)
     memory_lines = flat(memory)
     cross_keys = dot_nn(memory_lines, c_key).astype(BF16).reshape(memory.shape)
     cross_values = dot_nn(memory_lines, c_value).astype(BF16).reshape(memory.shape)
     cross_mixed, cross_probs = cross_forward(cross_query, cross_keys, cross_values)
-    cross_mixed, w_inner, w_outer = tie(cross_mixed, w_inner, w_outer)
+    cross_mixed, w_inner = tie(cross_mixed, w_inner)
     w_inner = gather_rest(w_inner, ranks)
-    w_outer = gather_rest(w_outer, ranks)
     normal_two, rate_two = normalize(h_one + dot_nn(flat(cross_mixed), c_out))
     h_two = normal_two * gain_two + shift_two
     h_two_low = h_two.astype(BF16)
     active, slope = gelu_parts(dot_nn(h_two_low, w_inner))
+    active, w_outer = tie(active, w_outer)
+    w_outer = gather_rest(w_outer, ranks)
     normal_three, rate_three = normalize(h_two + dot_nn(active, w_outer))
     output = (normal_three * gain_three + shift_three).astype(BF16)
     output = jnp.transpose(output.reshape(shape), (1, 2, 0, 3))
@@ -873,7 +908,7 @@
     memory_exchange.turn()
     memory_exchange.fetch()
     rank = lax.axis_index("ctx")
-    steps = (3, 1, 2, 0)
+    steps = (3, 2, 1, 0)
     places = [rank ^ step if ranks == 4 else jnp.int32(index) for index, step in enumerate(steps)]
     back = {}
 
@@ -910,25 +945,31 @@
         if turn < 3:
             grad_mixed, results = tie(grad_mixed, results)
         back[step] = [flat(value) for value in results]
-        if turn == 1:
+        if turn == 0 and ranks == 4:
+            first.begin(False)
+            grad_mixed = hold(grad_mixed, first)
+        if turn == 1 and ranks == 4:
+            first.turn()
+            grad_mixed = hold(grad_mixed, first)
+            first.fetch()
+        if turn == 2:
             if ranks == 4:
-                first.begin()
+                first.late()
             grad_mixed = hold(grad_mixed, centre, memory_exchange)
             centre_total = centre.end().astype(BF16)
             encoded_grad = memory_exchange.end()
+            grad_mixed, centre_total = tie(grad_mixed, centre_total)
             if ranks == 4:
-                grad_mixed, centre_total = hold(grad_mixed, first, centre_total)
+                side, partner = first.values
+                grad_mixed, partner = tie(grad_mixed, partner)
+                first.values = (side, swap(partner))
             centre_piece = scatter(centre_total)
-        if turn == 2 and ranks == 4:
-            first.turn()
-            grad_mixed = hold(grad_mixed, first)
-            first.fetch()
     joined = [jnp.concatenate(values, axis=1) for values in zip(*(back[step] for step in steps))]
     query_grad, rel_grad, own_key_grad, own_value_grad, key_grad, value_grad = joined
     if ranks == 4:
-        back[0][0], key_grad = hold(back[0][0], first, key_grad)
+        back[0][0] = hold(back[0][0], first)
         first_total = first.end().astype(BF16)
-        key_grad, first_total = tie(key_grad, first_total)
+        key_grad, own_key_grad, first_total = tie(key_grad, own_key_grad, first_total)
     else:
         whole = column_part(
             ranks,

time: 1150 us -> 1030 us (0.90)
  Pallas kernels: 392 us -> 279 us
    pallas_call x1, Pallas kernels: 137 us -> 76 us  [self_forward(): pl.pallas_call(self_forward_kernel, grid=(seqs, width // 256), in_specs=[...]
    pallas_call x4, Pallas kernels: 148 us -> 95 us  [self_backward(): pl.pallas_call(self_backward_kernel, grid_spec=pltpu.PrefetchScalarGridSp...]
    ppermute x14, waiting for transfers between devices: 89.6 us -> 63.6 us  [pass_across(): return lax.ppermute(value, 'ctx', ACROSS)]
    all_gather x3, waiting for transfers between devices: 0.05 us -> 18.7 us  [gather_half(): return lax.all_gather(piece, 'fsdp', axis=0, tiled=False)]
    unnamed x9, waiting for transfers between devices: 11.5 us -> 27.6 us
    unnamed x355 -> x335, local copies, waits for them, and re-layouts: 57.8 us -> 53.7 us
  transfers between devices with their start and end apart: 54 -> 54, of which waited for: 11 -> 10; matrix products, arithmetic and copies ran while one was open for 35% -> 42% of each run, Pallas kernels for 34% -> 27%
where the time goes in v3:
time: 1030 us; the launch traced here: 1020 us
  matrix products  377 us (37%)
  Pallas kernels  279 us (27%)
  waiting for transfers between devices  125 us (12%)
  local copies, waits for them, and re-layouts  89.3 us (9%)
  other arithmetic  87.3 us (8%)
  starting transfers between devices  41.6 us (4%)
  between operations  22 us (2%)
    dot_general x44, matrix products, dot_tn(): lax.dot_general(left, right, (((0,), (0,)), ((), ())), preferred_element_...  134 us
    dot_general x13, matrix products, dot_nt(): lax.dot_general(left, right, (((1,), (1,)), ((), ())), preferred_element_...  116 us
    dot_general x13, matrix products, dot_nn(): return jnp.dot(left, right, preferred_element_type=F32)  109 us
    pallas_call x4, Pallas kernels, self_backward(): pl.pallas_call(self_backward_kernel, grid_spec=pltpu.PrefetchScalarGridSp...  95 us
    pallas_call x1, Pallas kernels, self_forward(): pl.pallas_call(self_forward_kernel, grid=(seqs, width // 256), in_specs=[...  76 us
    ppermute x14, waiting for transfers between devices, pass_across(): return lax.ppermute(value, 'ctx', ACROSS)  63.6 us
    unnamed x335, local copies, waits for them, and re-layouts  53.7 us
    pallas_call x1, Pallas kernels, cross_backward(): pl.pallas_call(cross_backward_kernel, grid=(seqs, width // 256, streams),...  42 us
  transfers between devices with their start and end apart: 54, of which 10 were waited for; matrix products, arithmetic and copies ran while one was open for 42% of the time, Pallas kernels for 27%

profile of v3, /device:TPU:1, one launch (start us, length us, event | category | flops | bytes accessed | tf_op | source)
XLA Modules:
  0.0 1020.5 jit_solution(7260514182151224504)
XLA Ops:
  24.5 17.0 %collective-permute-done.1.third = bf16[2,256,1024]{2,1,0:T(8,128)(2,1)} collective-permute-done((bf16[2,256,1024]{2,1,0:T(8,128)(2,1)S(1)}, bf16[2,256,1024]{2,1,0:T(8,128)(2,1)}, u32[]{:S(2)}, u32[]{:S(2)}) %collective-permute-start.1) | collective-permute-done | bytes 1048608 | tf_op jit(solution)/shard_map/ppermute | solution.py:547
  52.1 7.1 collective-permute-done.4.third
  66.5 5.7 place.5
  72.1 9.0 convert_bitcast_fusion.1
  81.1 13.0 %all-gather.8.cloned.1.call-done = bf16[1024,3584]{1,0:T(8,128)(2,1)} async-done(((bf16[32,3584]{1,0:T(8,128)(2,1)}), bf16[1024,3584]{1,0:T(8,128)(2,1)}) %all-gather.8.cloned.1.call-update) | async-done | bytes 7340048 | tf_op jit(solution)/shard_map/all_gather | solution.py:539
  95.9 6.9 copy.147
  105.6 5.3 convolution_convert_fusion.8
  110.9 5.5 convolution_convert_fusion.11
  120.0 4.8 convolution_convert_fusion.5
  124.8 6.3 convolution_convert_fusion.6
  131.1 6.3 convolution_convert_fusion.7
  137.9 18.6 %all-gather.10.cloned.1.call-done = bf16[256,5248]{1,0:T(8,128)(2,1)} async-done(((bf16[32,5248]{1,0:T(8,128)(2,1)}), bf16[256,5248]{1,0:T(8,128)(2,1)}) %all-gather.10.cloned.1.call-update) | async-done | bytes 2686992 | tf_op jit(solution)/shard_map/all_gather | solution.py:592
  160.0 76.0 %self_forward.1 = (bf16[3,2,256,1024]{3,2,1,0:T(8,128)(2,1)}, bf16[2,8,8,192,1024]{4,3,2,1,0:T(8,128)(2,1)}, bf16[2,8,8,192,128]{4,3,2,1,0:T(8,128)(2,1)}) custom-call(s32[8]{0:T(128)} %copy-done.89, s32[1]{0:T(128)} %slice.311.own_ref, bf16[3,2,256,1024]{3,2,1,0:T(8,128)(2,1)} %bitcast.439, bf16[3,2,256,512]{3,2,1,0:T(8,128)(2,1)} %bitcast.490, ...), custom_call_target="tpu_custom_call" | custom-call | flops 88000004096 | bytes 80000000 | tf_op jit(solution)/shard_map/self_forward/pallas_call | solution.py:293
  245.3 8.4 place.7
  254.6 9.7 fusion.262
  268.8 5.4 convolution_convert_fusion.9
  274.3 5.5 convolution_convert_fusion.10
  282.7 6.4 convolution_convert_fusion.4
  292.7 33.6 %cross_forward.1 = (bf16[3,2,256,1024]{3,2,1,0:T(8,128)(2,1)}, bf16[3,2,8,512,512]{4,3,2,1,0:T(8,128)(2,1)}) custom-call(bf16[3,2,256,1024]{3,2,1,0:T(8,128)(2,1)} %bitcast.454, bf16[2,512,1024]{2,1,0:T(8,128)(2,1)} %bitcast.478, bf16[2,512,1024]{2,1,0:T(8,128)(2,1)} %bitcast.476), custom_call_target="tpu_custom_call" | custom-call | flops 38000001024 | bytes 40000000 | tf_op jit(solution)/shard_map/cross_forward/pallas_call | solution.py:463
  326.7 8.8 fusion.263
  341.9 7.1 place.8
  349.0 22.6 %multiply_convert_fusion.1 = (bf16[1536,4096]{1,0:T(8,128)(2,1)}, f32[1536,4096]{1,0:T(8,128)}) fusion(bf16[1536,1024]{1,0:T(8,128)(2,1)} %fusion.11, bf16[1024,4096]{1,0:T(8,128)(2,1)} %bitcast.319), kind=kOutput, calls=%fused_computation.7 | convolution fusion | flops 12916359168 | bytes 49283072 | tf_op jit(solution)/shard_map/dot_general | solution.py:29
  382.1 7.2 place.9
  389.3 19.3 %fusion.264 = (f32[1536]{0:T(1024)S(1)}, f32[1536,1024]{1,0:T(8,128)S(1)}) fusion(bf16[1536,4096]{1,0:T(8,128)(2,1)} %get-tuple-element.183, bf16[4096,1024]{1,0:T(8,128)(2,1)} %bitcast.321, f32[1024]{0:T(1024)S(1)} %bitcast.415, f32[1024]{0:T(1024)S(1)} %bitcast.408, f32[1536]{0:T(1024)S(1)} %add_rsqrt_fusion.1, f32[1536,1024]{1,0:T(8,128)} %copy-done.2, ...), kind=kOutput, calls=%fused_computation.440 | convolution fusion | flops 12894337024 | bytes 33581056 | tf_op jit(solution)/shard_map/dot_general | solution.py:29
  412.6 5.3 fusion.245
  419.5 9.8 convolution_convert_fusion
  429.3 9.9 convolution_convert_fusion.1
  442.7 25.7 %multiply_convert_fusion = bf16[1536,4096]{1,0:T(8,128)(2,1)} fusion(bf16[1536,1024]{1,0:T(8,128)(2,1)S(1)} %copy-done.28, bf16[4096,1024]{1,0:T(8,128)(2,1)S(1)} %bitcast.324, f32[1536,4096]{1,0:T(8,128)} %get-tuple-element.495), kind=kOutput, calls=%fused_computation.6 | convolution fusion | flops 12960399360 | bytes 49283072 | tf_op jit(solution)/shard_map/dot_general | solution.py:21
  468.4 7.2 fusion.42
  475.7 4.7 fusion.97
  480.4 4.7 fusion.94
  485.1 5.0 fusion.40
  490.2 6.5 fusion.12
  497.5 22.1 %multiply_reduce_fusion = (f32[1024]{0:T(1024)S(1)}, f32[1536]{0:T(1024)S(1)}, f32[1536]{0:T(1024)S(1)}, f32[1024]{0:T(1024)S(1)}, f32[1536,1024]{1,0:T(8,128)}) fusion(f32[1536,1024]{1,0:T(8,128)S(1)} %bitcast.291, f32[1536]{0:T(1024)S(1)} %add_rsqrt_fusion.1, f32[1536]{0:T(1024)S(1)} %broadcast_multiply_fusion.6, f32[1024]{0:T(1024)S(1)} %bitcast.409, ...), kind=kOutput, calls=%fused_computation.20 | convolution fusion | flops 12900625408 | bytes 39882752 | tf_op jit(solution)/shard_map/dot_general | solution.py:21
  519.6 5.9 fusion.244
  525.5 4.9 add_convert_fusion.6
  530.4 6.5 convolution_convert_fusion.3
  538.1 42.0 %cross_backward.1 = (bf16[3,2,256,1024]{3,2,1,0:T(8,128)(2,1)}, bf16[2,512,1024]{2,1,0:T(8,128)(2,1)}, bf16[2,512,1024]{2,1,0:T(8,128)(2,1)}) custom-call(bf16[3,2,256,1024]{3,2,1,0:T(8,128)(2,1)} %bitcast.455, bf16[2,512,1024]{2,1,0:T(8,128)(2,1)} %bitcast.479, bf16[2,512,1024]{2,1,0:T(8,128)(2,1)} %bitcast.477, ...), custom_call_target="tpu_custom_call" | custom-call | flops 46999998464 | bytes 50000000 | tf_op jit(solution)/shard_map/cross_backward/pallas_call | solution.py:481
  580.2 4.7 fusion.102
  585.0 4.1 add_convert_fusion.4
  590.8 11.6 %fusion.14 = bf16[4096,256]{1,0:T(8,128)(2,1)} fusion(bf16[1536,4096]{1,0:T(8,128)(2,1)} %get-tuple-element.183, bf16[4096,256]{1,0:T(8,128)(2,1)} %collective-permute-done.20, bf16[4096,256]{1,0:T(8,128)(2,1)} %collective-permute-done.16, bf16[1536,1024]{1,0:T(8,128)(2,1)} %copy-done.27, s32[]{:T(128)S(6)} %select_n.352), kind=kOutput, calls=%fused_computation.52 | convolution fusion | flops 3226468352 | bytes 19660804 | tf_op jit(solution)/shard_map/dot_general | solution.py:25
  605.3 7.8 multiply_reduce_fusion.1
  613.2 4.1 fusion.243
  631.4 4.3 convolution_dynamic-update-slice_fusion.1
  665.6 3.7 convolution_dynamic-update-slice_fusion.3
  669.3 6.5 convolution_convert_fusion.2
  675.8 4.4 add_convert_fusion.3
  680.7 23.7 %self_backward.4 = (bf16[3,2,256,256]{3,2,1,0:T(8,128)(2,1)}, bf16[3,2,256,128]{3,2,1,0:T(8,128)(2,1)}, bf16[2,2,256,256]{3,2,1,0:T(8,128)(2,1)}, bf16[2,2,256,2...) custom-call(s32[1]{0:T(128)} %bitcast.69.group, s32[8]{0:T(128)} %copy-done.89, ...), custom_call_target="tpu_custom_call" | custom-call | flops 27000000512 | bytes 25000000 | tf_op jit(solution)/shard_map/self_backward/pallas_call | solution.py:346
  716.3 23.8 %self_backward.5 = (bf16[3,2,256,256]{3,2,1,0:T(8,128)(2,1)}, bf16[3,2,256,128]{3,2,1,0:T(8,128)(2,1)}, bf16[2,2,256,256]{3,2,1,0:T(8,128)(2,1)}, bf16[2,2,256,2...) custom-call(s32[1]{0:T(128)} %bitcast.79.group, s32[8]{0:T(128)} %copy-done.89, ...), custom_call_target="tpu_custom_call" | custom-call | flops 27000000512 | bytes 25000000 | tf_op jit(solution)/shard_map/self_backward/pallas_call | solution.py:346
  760.3 24.0 %self_backward.6 = (bf16[3,2,256,256]{3,2,1,0:T(8,128)(2,1)}, bf16[3,2,256,128]{3,2,1,0:T(8,128)(2,1)}, bf16[2,2,256,256]{3,2,1,0:T(8,128)(2,1)}, bf16[2,2,256,2...) custom-call(s32[1]{0:T(128)} %bitcast.89.group, s32[8]{0:T(128)} %copy-done.89, ...), custom_call_target="tpu_custom_call" | custom-call | flops 27000000512 | bytes 25000000 | tf_op jit(solution)/shard_map/self_backward/pallas_call | solution.py:346
  794.0 21.1 %collective-permute-done.26 = bf16[2,128,1024]{2,1,0:T(8,128)(2,1)} collective-permute-done((bf16[2,128,1024]{2,1,0:T(8,128)(2,1)}, bf16[2,128,1024]{2,1,0:T(8,128)(2,1)}, u32[]{:S(2)}, u32[]{:S(2)}) %collective-permute-start.26) | collective-permute-done | bytes 524320 | tf_op jit(solution)/shard_map/ppermute | solution.py:547
  815.1 5.5 add_convert_fusion.2
  820.6 4.5 copy.191
  827.0 23.5 %self_backward.7 = (bf16[3,2,256,256]{3,2,1,0:T(8,128)(2,1)}, bf16[3,2,256,128]{3,2,1,0:T(8,128)(2,1)}, bf16[2,2,256,256]{3,2,1,0:T(8,128)(2,1)}, bf16[2,2,256,2...) custom-call(s32[1]{0:T(128)} %bitcast.3.rank.group, s32[8]{0:T(128)} %copy-done.89, ...), custom_call_target="tpu_custom_call" | custom-call | flops 27000000512 | bytes 25000000 | tf_op jit(solution)/shard_map/self_backward/pallas_call | solution.py:346
  867.1 9.9 fusion.15
  881.5 8.5 add_convert_fusion
  890.1 7.7 fusion.50
  899.1 3.9 convert_add_fusion.1
  903.1 4.6 add_add_fusion
  909.1 4.4 fusion.190
  916.7 7.7 fusion.91
  925.4 18.4 %collective-permute-done.44 = bf16[128,2048]{1,0:T(8,128)(2,1)} collective-permute-done((bf16[128,2048]{1,0:T(8,128)(2,1)}, bf16[128,2048]{1,0:T(8,128)(2,1)}, u32[]{:S(2)}, u32[]{:S(2)}) %collective-permute-start.44) | collective-permute-done | bytes 524320 | tf_op jit(solution)/shard_map/ppermute | solution.py:547
  950.7 6.7 fusion.6
  964.3 27.5 %reduce-scatter.10.cloned.1.call-done = bf16[128,896]{1,0:T(8,128)(2,1)} async-done(((bf16[1024,896]{1,0:T(8,128)(2,1)}), bf16[128,896]{1,0:T(8,128)(2,1)}) %reduce-scatter.10.cloned.1.call-update) | async-done | bytes 229392
  (604 shorter events, 245.9 us)
Async XLA Ops:
  7.2 97.7 %copy-start = (bf16[128,4096]{1,0:T(8,128)(2,1)S(1)}, bf16[128,4096]{1,0:T(8,128)(2,1)}, u32[]{:S(2)}) copy-start(bf16[128,4096]{1,0:T(8,128)(2,1)} %param.43) | copy-start | bytes 3145732
  7.2 87.0 %all-gather.8.cloned.1.call-start = ((), (), s32[]{:S(2)}) async-start(), calls=%async_computation.3 | async-start | bytes 7569408 | tf_op jit(solution)/shard_map/all_gather | solution.py:539
  10.3 146.3 %all-gather.10.cloned.1.call-start = ((), (), s32[]{:S(2)}) async-start(), calls=%async_computation.5 | async-start | bytes 3022848 | tf_op jit(solution)/shard_map/all_gather | solution.py:592
  14.7 35.7 %copy-start.90 = (s32[1055]{0:T(1024)S(1)}, s32[1055]{0:T(1024)}, u32[]{:S(2)}) copy-start(s32[1055]{0:T(1024)} %param.29) | copy-start | bytes 12664
  14.8 45.8 %copy-start.10 = (bf16[2,256,1024]{2,1,0:T(8,128)(2,1)}, bf16[2,256,1024]{2,1,0:T(8,128)(2,1)S(1)}, u32[]{:S(2)}) copy-start(bf16[2,256,1024]{2,1,0:T(8,128)(2,1)S(1)} %slice_bitcast_fusion.first) | copy-start | bytes 3145732
  14.8 26.7 %collective-permute-start.1 = (bf16[2,256,1024]{2,1,0:T(8,128)(2,1)S(1)}, bf16[2,256,1024]{2,1,0:T(8,128)(2,1)}, u32[]{:S(2)}, u32[]{:S(2)}) collective-permute-start(bf16[2,256,1024]{2,1,0:T(8,128)(2,1)S(1)} %slice_bitcast_fusion.first), channel_id=1, source_target_pairs={{0,16},{16,0},{8,24},{24,8},{1,17},{17,1},{9,25},{25,9},{2,18},{18... | collective-permute-start | bytes 3145736 | tf_op jit(solution)/shard_map/ppermute | solution.py:547
  16.9 49.6 %collective-permute-start = (bf16[2,256,1024]{2,1,0:T(8,128)(2,1)S(1)}, bf16[2,256,1024]{2,1,0:T(8,128)(2,1)}, u32[]{:S(2)}, u32[]{:S(2)}) collective-permute-start(bf16[2,256,1024]{2,1,0:T(8,128)(2,1)S(1)} %slice_bitcast_fusion.first), channel_id=1, source_target_pairs={{0,8},{8,0},{16,24},{24,16},{1,9},{9,1},{17,25},{25,17},{2,10},{10... | collective-permute-start | bytes 3145736 | tf_op jit(solution)/shard_map/ppermute | solution.py:543
  17.8 41.4 %collective-permute-start.4 = (bf16[2,128,1024]{2,1,0:T(8,128)(2,1)S(1)}, bf16[2,128,1024]{2,1,0:T(8,128)(2,1)}, u32[]{:S(2)}, u32[]{:S(2)}) collective-permute-start(bf16[2,128,1024]{2,1,0:T(8,128)(2,1)S(1)} %copy-done.51), channel_id=1, source_target_pairs={{0,16},{16,0},{8,24},{24,8},{1,17},{17,1},{9,25},{25,9},{2,18},{18... | collective-permute-start | bytes 1572872 | tf_op jit(solution)/shard_map/ppermute | solution.py:547
  17.8 43.1 %collective-permute-start.3 = (bf16[2,128,1024]{2,1,0:T(8,128)(2,1)S(1)}, bf16[2,128,1024]{2,1,0:T(8,128)(2,1)}, u32[]{:S(2)}, u32[]{:S(2)}) collective-permute-start(bf16[2,128,1024]{2,1,0:T(8,128)(2,1)S(1)} %copy-done.51), channel_id=1, source_target_pairs={{0,8},{8,0},{16,24},{24,16},{1,9},{9,1},{17,25},{25,17},{2,10},{10... | collective-permute-start | bytes 1572872 | tf_op jit(solution)/shard_map/ppermute | solution.py:543
  19.0 41.9 %copy-start.89 = (s32[8]{0:T(128)}, s32[8]{0:T(128)S(1)}, u32[]{:S(2)}) copy-start(s32[8]{0:T(128)S(1)} %dynamic_slice.199.blocks) | copy-start | bytes 100
  41.5 25.0 %collective-permute-start.2 = (bf16[2,256,1024]{2,1,0:T(8,128)(2,1)}, bf16[2,256,1024]{2,1,0:T(8,128)(2,1)}, u32[]{:S(2)}, u32[]{:S(2)}) collective-permute-start(bf16[2,256,1024]{2,1,0:T(8,128)(2,1)} %collective-permute-done.1.third), channel_id=1, source_target_pairs={{0,8},{8,0},{16,24},{24,16},{1,9},{9,1},{17,25},{25,17},{2,10},{10... | collective-permute-start | bytes 3145736 | tf_op jit(solution)/shard_map/ppermute | solution.py:543
  59.2 3.0 collective-permute-start.5
  104.6 131.5 %all-gather.12.cloned.1.call-start = ((), (), s32[]{:S(2)}) async-start(), calls=%async_computation.6 | async-start | bytes 2359296 | tf_op jit(solution)/shard_map/all_gather | solution.py:592
  137.4 151.7 %all-gather.14.cloned.1.call-start = ((), (), s32[]{:S(2)}) async-start(), calls=%async_computation.7 | async-start | bytes 2359296 | tf_op jit(solution)/shard_map/all_gather | solution.py:592
  156.6 79.5 %collective-permute-start.6 = (bf16[8,32,5248]{2,1,0:T(8,128)(2,1)}, bf16[8,32,5248]{2,1,0:T(8,128)(2,1)}, u32[]{:S(2)}, u32[]{:S(2)}) collective-permute-start(bf16[8,32,5248]{2,1,0:T(8,128)(2,1)} %bitcast.342), channel_id=1, source_target_pairs={{0,8},{8,0},{16,24},{24,16},{1,9},{9,1},{17,25},{25,17},{2,10},{10... | collective-permute-start | bytes 8060936 | tf_op jit(solution)/shard_map/ppermute | solution.py:543
  158.8 77.2 %collective-permute-start.7 = (bf16[8,32,5248]{2,1,0:T(8,128)(2,1)}, bf16[8,32,5248]{2,1,0:T(8,128)(2,1)}, u32[]{:S(2)}, u32[]{:S(2)}) collective-permute-start(bf16[8,32,5248]{2,1,0:T(8,128)(2,1)} %bitcast.343), channel_id=1, source_target_pairs={{0,16},{16,0},{8,24},{24,8},{1,17},{17,1},{9,25},{25,9},{2,18},{18... | collective-permute-start | bytes 8060936 | tf_op jit(solution)/shard_map/ppermute | solution.py:547
  236.1 9.2 collective-permute-start.8
  244.5 671.5 %reduce-scatter.8.cloned.1.call-start = ((), (), s32[]{:S(2)}) async-start(), calls=%async_computation.4 | async-start | bytes 4718592 | tf_op jit(solution)/shard_map/reduce_scatter | solution.py:686
  244.5 81.8 %collective-permute-start.10 = (bf16[8,32,4096]{2,1,0:T(8,128)(2,1)S(1)}, bf16[8,32,4096]{2,1,0:T(8,128)(2,1)}, u32[]{:S(2)}, u32[]{:S(2)}) collective-permute-start(bf16[8,32,4096]{2,1,0:T(8,128)(2,1)S(1)} %bitcast.346), channel_id=1, source_target_pairs={{0,16},{16,0},{8,24},{24,8},{1,17},{17,1},{9,25},{25,9},{2,18},{18... | collective-permute-start | bytes 6291464 | tf_op jit(solution)/shard_map/ppermute | solution.py:547
  244.9 81.5 %collective-permute-start.9 = (bf16[8,32,4096]{2,1,0:T(8,128)(2,1)S(1)}, bf16[8,32,4096]{2,1,0:T(8,128)(2,1)}, u32[]{:S(2)}, u32[]{:S(2)}) collective-permute-start(bf16[8,32,4096]{2,1,0:T(8,128)(2,1)S(1)} %bitcast.347), channel_id=1, source_target_pairs={{0,8},{8,0},{16,24},{24,16},{1,9},{9,1},{17,25},{25,17},{2,10},{10... | collective-permute-start | bytes 6291464 | tf_op jit(solution)/shard_map/ppermute | solution.py:543
  264.3 62.4 %copy-start.83 = (f32[1536]{0:T(1024)}, f32[1536]{0:T(1024)S(1)}, u32[]{:S(2)}) copy-start(f32[1536]{0:T(1024)S(1)} %broadcast_multiply_fusion.7) | copy-start | bytes 18436
  268.2 58.5 %copy-start.85 = (f32[1536]{0:T(1024)}, f32[1536]{0:T(1024)S(1)}, u32[]{:S(2)}) copy-start(f32[1536]{0:T(1024)S(1)} %add_rsqrt_fusion.2) | copy-start | bytes 18436
  268.8 57.9 %copy-start.87 = (f32[1,1024]{1,0:T(1,128)}, f32[1,1024]{1,0:T(1,128)S(1)}, u32[]{:S(2)}) copy-start(f32[1,1024]{1,0:T(1,128)S(1)} %get-tuple-element.475) | copy-start | bytes 12292
  289.1 82.5 %collective-permute-start.12 = (bf16[8,128,1024]{2,1,0:T(8,128)(2,1)}, bf16[8,128,1024]{2,1,0:T(8,128)(2,1)}, u32[]{:S(2)}, u32[]{:S(2)}) collective-permute-start(bf16[8,128,1024]{2,1,0:T(8,128)(2,1)} %bitcast.348), channel_id=1, source_target_pairs={{0,8},{8,0},{16,24},{24,16},{1,9},{9,1},{17,25},{25,17},{2,10},{10... | collective-permute-start | bytes 6291464 | tf_op jit(solution)/shard_map/ppermute | solution.py:543
  291.6 80.1 %collective-permute-start.13 = (bf16[8,128,1024]{2,1,0:T(8,128)(2,1)}, bf16[8,128,1024]{2,1,0:T(8,128)(2,1)}, u32[]{:S(2)}, u32[]{:S(2)}) collective-permute-start(bf16[8,128,1024]{2,1,0:T(8,128)(2,1)} %bitcast.349), channel_id=1, source_target_pairs={{0,16},{16,0},{8,24},{24,8},{1,17},{17,1},{9,25},{25,9},{2,18},{18... | collective-permute-start | bytes 6291464 | tf_op jit(solution)/shard_map/ppermute | solution.py:547
  326.4 14.2 %collective-permute-start.11 = (bf16[8,32,4096]{2,1,0:T(8,128)(2,1)}, bf16[8,32,4096]{2,1,0:T(8,128)(2,1)S(1)}, u32[]{:S(2)}, u32[]{:S(2)}) collective-permute-start(bf16[8,32,4096]{2,1,0:T(8,128)(2,1)} %collective-permute-done.10.third), channel_id=1, source_target_pairs={{0,8},{8,0},{16,24},{24,16},{1,9},{9,1},{17,25},{25,17},{2,10},{10... | collective-permute-start | bytes 6291464 | tf_op jit(solution)/shard_map/ppermute | solution.py:543
  349.0 25.0 %slice-start.14 = ((s8[7340032]{0:T(1024)(128)(4,1)}), s8[4194304]{0:T(1024)(128)(4,1)S(1)}, s32[]{:S(2)}) async-start(s8[7340032]{0:T(1024)(128)(4,1)} %bitcast.327), calls=%async_computation.24 | async-start | bytes 8388608
  371.7 10.4 %collective-permute-start.14 = (bf16[8,128,1024]{2,1,0:T(8,128)(2,1)}, bf16[8,128,1024]{2,1,0:T(8,128)(2,1)}, u32[]{:S(2)}, u32[]{:S(2)}) collective-permute-start(bf16[8,128,1024]{2,1,0:T(8,128)(2,1)} %collective-permute-done.13.third), channel_id=1, source_target_pairs={{0,8},{8,0},{16,24},{24,16},{1,9},{9,1},{17,25},{25,17},{2,10},{10... | collective-permute-start | bytes 6291464 | tf_op jit(solution)/shard_map/ppermute | solution.py:543
  382.1 27.4 %slice-start = ((s8[6291456]{0:T(1024)(128)(4,1)}), s8[2097152]{0:T(1024)(128)(4,1)S(1)}, s32[]{:S(2)}) async-start(s8[6291456]{0:T(1024)(128)(4,1)} %bitcast.284), calls=%async_computation.10 | async-start | bytes 4194304
  439.2 51.0 %collective-permute-start.15 = (bf16[4096,256]{1,0:T(8,128)(2,1)}, bf16[4096,256]{1,0:T(8,128)(2,1)}, u32[]{:S(2)}, u32[]{:S(2)}) collective-permute-start(bf16[4096,256]{1,0:T(8,128)(2,1)} %convolution_convert_fusion.1), channel_id=1, source_target_pairs={{0,8},{8,0},{16,24},{24,16},{1,9},{9,1},{17,25},{25,17},{2,10},{10... | collective-permute-start | bytes 6291464 | tf_op jit(solution)/shard_map/ppermute | solution.py:543
  439.4 57.3 %collective-permute-start.16 = (bf16[4096,256]{1,0:T(8,128)(2,1)}, bf16[4096,256]{1,0:T(8,128)(2,1)}, u32[]{:S(2)}, u32[]{:S(2)}) collective-permute-start(bf16[4096,256]{1,0:T(8,128)(2,1)} %convolution_convert_fusion), channel_id=1, source_target_pairs={{0,8},{8,0},{16,24},{24,16},{1,9},{9,1},{17,25},{25,17},{2,10},{10... | collective-permute-start | bytes 6291464 | tf_op jit(solution)/shard_map/ppermute | solution.py:543
  442.7 25.7 %copy-start.25 = (bf16[1536,1024]{1,0:T(8,128)(2,1)S(1)}, bf16[1536,1024]{1,0:T(8,128)(2,1)}, u32[]{:S(2)}) copy-start(bf16[1536,1024]{1,0:T(8,128)(2,1)} %fusion.11) | copy-start | bytes 9437188
  496.7 28.8 %collective-permute-start.17 = (bf16[1024,1024]{1,0:T(8,128)(2,1)}, bf16[1024,1024]{1,0:T(8,128)(2,1)}, u32[]{:S(2)}, u32[]{:S(2)}) collective-permute-start(bf16[1024,1024]{1,0:T(8,128)(2,1)} %fusion.94), channel_id=1, source_target_pairs={{0,8},{8,0},{16,24},{24,16},{1,9},{9,1},{17,25},{25,17},{2,10},{10... | collective-permute-start | bytes 6291464 | tf_op jit(solution)/shard_map/ppermute | solution.py:543
  497.0 33.5 %collective-permute-start.18 = (bf16[1024,1024]{1,0:T(8,128)(2,1)}, bf16[1024,1024]{1,0:T(8,128)(2,1)}, u32[]{:S(2)}, u32[]{:S(2)}) collective-permute-start(bf16[1024,1024]{1,0:T(8,128)(2,1)} %fusion.97), channel_id=1, source_target_pairs={{0,8},{8,0},{16,24},{24,16},{1,9},{9,1},{17,25},{25,17},{2,10},{10... | collective-permute-start | bytes 6291464 | tf_op jit(solution)/shard_map/ppermute | solution.py:543
  497.2 93.0 %collective-permute-start.20 = (bf16[4096,256]{1,0:T(8,128)(2,1)}, bf16[4096,256]{1,0:T(8,128)(2,1)}, u32[]{:S(2)}, u32[]{:S(2)}) collective-permute-start(bf16[4096,256]{1,0:T(8,128)(2,1)} %fusion.12), channel_id=1, source_target_pairs={{0,16},{16,0},{8,24},{24,8},{1,17},{17,1},{9,25},{25,9},{2,18},{18... | collective-permute-start | bytes 6291464 | tf_op jit(solution)/shard_map/ppermute | solution.py:547
  536.9 53.2 %collective-permute-start.19 = (bf16[1024,1024]{1,0:T(8,128)(2,1)}, bf16[1024,1024]{1,0:T(8,128)(2,1)S(1)}, u32[]{:S(2)}, u32[]{:S(2)}) collective-permute-start(bf16[1024,1024]{1,0:T(8,128)(2,1)} %add_convert_fusion.6), channel_id=1, source_target_pairs={{0,16},{16,0},{8,24},{24,8},{1,17},{17,1},{9,25},{25,9},{2,18},{18... | collective-permute-start | bytes 6291464 | tf_op jit(solution)/shard_map/ppermute | solution.py:547
  631.1 330.0 %reduce-scatter.12.cloned.1.call-start = ((), (), s32[]{:S(2)}) async-start(), calls=%async_computation.9 | async-start | bytes 2949120
  646.2 34.0 %collective-permute-start.22 = (bf16[1024,1280]{0,1:T(8,128)(2,1)}, bf16[1024,1280]{0,1:T(8,128)(2,1)}, u32[]{:S(2)}, u32[]{:S(2)}) collective-permute-start(bf16[1024,1280]{0,1:T(8,128)(2,1)} %fusion.134), channel_id=1, source_target_pairs={{0,8},{8,0},{16,24},{24,16},{1,9},{9,1},{17,25},{25,17},{2,10},{10... | collective-permute-start | bytes 7864328 | tf_op jit(solution)/shard_map/ppermute | solution.py:543
  653.8 22.0 %collective-permute-start.21 = (bf16[1024,1280]{0,1:T(8,128)(2,1)}, bf16[1024,1280]{0,1:T(8,128)(2,1)}, u32[]{:S(2)}, u32[]{:S(2)}) collective-permute-start(bf16[1024,1280]{0,1:T(8,128)(2,1)} %fusion.137), channel_id=1, source_target_pairs={{0,8},{8,0},{16,24},{24,16},{1,9},{9,1},{17,25},{25,17},{2,10},{10... | collective-permute-start | bytes 7864328 | tf_op jit(solution)/shard_map/ppermute | solution.py:543
  680.2 74.9 %collective-permute-start.25 = (bf16[2,128,1024]{2,1,0:T(8,128)(2,1)}, bf16[2,128,1024]{2,1,0:T(8,128)(2,1)}, u32[]{:S(2)}, u32[]{:S(2)}) collective-permute-start(bf16[2,128,1024]{2,1,0:T(8,128)(2,1)} %get-tuple-element.250), channel_id=1, source_target_pairs={{0,8},{8,0},{16,24},{24,16},{1,9},{9,1},{17,25},{25,17},{2,10},{10... | collective-permute-start | bytes 1572872 | tf_op jit(solution)/shard_map/ppermute | solution.py:543
  716.2 24.0 %collective-permute-start.39 = (f32[6,1024]{1,0:T(8,128)S(1)}, f32[6,1024]{1,0:T(8,128)S(1)}, u32[]{:S(2)}, u32[]{:S(2)}) collective-permute-start(f32[6,1024]{1,0:T(8,128)S(1)} %stack.55), channel_id=1, source_target_pairs={{0,8},{8,0},{16,24},{24,16},{1,9},{9,1},{17,25},{25,17},{2,10},{10... | collective-permute-start | bytes 73736 | tf_op jit(solution)/shard_map/ppermute | solution.py:711
  740.2 4.2 collective-permute-start.40
  743.6 14.7 %collective-permute-start.23 = (bf16[1024,896]{0,1:T(8,128)(2,1)S(1)}, bf16[1024,896]{0,1:T(8,128)(2,1)S(1)}, u32[]{:S(2)}, u32[]{:S(2)}) collective-permute-start(bf16[1024,896]{0,1:T(8,128)(2,1)S(1)} %copy-done.39), channel_id=1, source_target_pairs={{0,8},{8,0},{16,24},{24,16},{1,9},{9,1},{17,25},{25,17},{2,10},{10... | collective-permute-start | bytes 5505032 | tf_op jit(solution)/shard_map/ppermute | solution.py:543
  744.5 2.8 collective-permute-start.41
  745.6 69.5 %collective-permute-start.24 = (bf16[1024,1280]{0,1:T(8,128)(2,1)S(1)}, bf16[1024,1280]{0,1:T(8,128)(2,1)}, u32[]{:S(2)}, u32[]{:S(2)}) collective-permute-start(bf16[1024,1280]{0,1:T(8,128)(2,1)S(1)} %add_convert_fusion.3), channel_id=1, source_target_pairs={{0,16},{16,0},{8,24},{24,8},{1,17},{17,1},{9,25},{25,9},{2,18},{18... | collective-permute-start | bytes 7864328 | tf_op jit(solution)/shard_map/ppermute | solution.py:547
  746.5 47.5 %collective-permute-start.27 = (bf16[2,128,1024]{2,1,0:T(8,128)(2,1)}, bf16[2,128,1024]{2,1,0:T(8,128)(2,1)}, u32[]{:S(2)}, u32[]{:S(2)}) collective-permute-start(bf16[2,128,1024]{2,1,0:T(8,128)(2,1)} %get-tuple-element.251), channel_id=1, source_target_pairs={{0,8},{8,0},{16,24},{24,16},{1,9},{9,1},{17,25},{25,17},{2,10},{10... | collective-permute-start | bytes 1572872 | tf_op jit(solution)/shard_map/ppermute | solution.py:543
  747.3 3.2 collective-permute-start.42
  750.5 4.1 collective-permute-start.43
  757.4 57.8 %collective-permute-start.26 = (bf16[2,128,1024]{2,1,0:T(8,128)(2,1)}, bf16[2,128,1024]{2,1,0:T(8,128)(2,1)}, u32[]{:S(2)}, u32[]{:S(2)}) collective-permute-start(bf16[2,128,1024]{2,1,0:T(8,128)(2,1)} %add_convert_fusion.9), channel_id=1, source_target_pairs={{0,16},{16,0},{8,24},{24,8},{1,17},{17,1},{9,25},{25,9},{2,18},{18... | collective-permute-start | bytes 1572872 | tf_op jit(solution)/shard_map/ppermute | solution.py:547
  784.3 92.7 %collective-permute-start.28 = (bf16[1024,896]{0,1:T(8,128)(2,1)}, bf16[1024,896]{0,1:T(8,128)(2,1)}, u32[]{:S(2)}, u32[]{:S(2)}) collective-permute-start(bf16[1024,896]{0,1:T(8,128)(2,1)} %fusion.29), channel_id=1, source_target_pairs={{0,16},{16,0},{8,24},{24,8},{1,17},{17,1},{9,25},{25,9},{2,18},{18... | collective-permute-start | bytes 5505032 | tf_op jit(solution)/shard_map/ppermute | solution.py:547
  825.1 51.9 %collective-permute-start.29 = (bf16[1024,896]{0,1:T(8,128)(2,1)}, bf16[1024,896]{0,1:T(8,128)(2,1)}, u32[]{:S(2)}, u32[]{:S(2)}) collective-permute-start(bf16[1024,896]{0,1:T(8,128)(2,1)} %pad_maximum_fusion.6), channel_id=1, source_target_pairs={{0,8},{8,0},{16,24},{24,16},{1,9},{9,1},{17,25},{25,17},{2,10},{10... | collective-permute-start | bytes 5505032 | tf_op jit(solution)/shard_map/ppermute | solution.py:543
  854.1 137.7 %reduce-scatter.10.cloned.1.call-start = ((), (), s32[]{:S(2)}) async-start(), calls=%async_computation.8 | async-start | bytes 2064384
  899.1 8.6 collective-permute-start.31
  907.7 37.4 %collective-permute-start.30 = (bf16[2,256,1024]{1,2,0:T(8,128)(2,1)}, bf16[2,256,1024]{1,2,0:T(8,128)(2,1)}, u32[]{:S(2)}, u32[]{:S(2)}) collective-permute-start(bf16[2,256,1024]{1,2,0:T(8,128)(2,1)} %get-tuple-element.384), channel_id=1, source_target_pairs={{0,8},{8,0},{16,24},{24,16},{1,9},{9,1},{17,25},{25,17},{2,10},{10... | collective-permute-start | bytes 3145736 | tf_op jit(solution)/shard_map/ppermute | solution.py:543
  908.2 37.0 %collective-permute-start.32 = (bf16[2,256,1024]{1,2,0:T(8,128)(2,1)S(1)}, bf16[2,256,1024]{1,2,0:T(8,128)(2,1)}, u32[]{:S(2)}, u32[]{:S(2)}) collective-permute-start(bf16[2,256,1024]{1,2,0:T(8,128)(2,1)S(1)} %fusion.84), channel_id=1, source_target_pairs={{0,16},{16,0},{8,24},{24,8},{1,17},{17,1},{9,25},{25,9},{2,18},{18... | collective-permute-start | bytes 3145736 | tf_op jit(solution)/shard_map/ppermute | solution.py:547
  916.0 27.8 %collective-permute-start.44 = (bf16[128,2048]{1,0:T(8,128)(2,1)}, bf16[128,2048]{1,0:T(8,128)(2,1)}, u32[]{:S(2)}, u32[]{:S(2)}) collective-permute-start(bf16[128,2048]{1,0:T(8,128)(2,1)} %reduce-scatter.8.cloned.1.call-done), channel_id=1, source_target_pairs={{0,16},{16,0},{8,24},{24,8},{1,17},{17,1},{9,25},{25,9},{2,18},{18... | collective-permute-start | bytes 1572872 | tf_op jit(solution)/shard_map/ppermute | solution.py:547
  924.4 33.0 %collective-permute-start.45 = (bf16[128,2048]{1,0:T(8,128)(2,1)}, bf16[128,2048]{1,0:T(8,128)(2,1)}, u32[]{:S(2)}, u32[]{:S(2)}) collective-permute-start(bf16[128,2048]{1,0:T(8,128)(2,1)} %reduce-scatter.8.cloned.1.call-done), channel_id=1, source_target_pairs={{0,8},{8,0},{16,24},{24,16},{1,9},{9,1},{17,25},{25,17},{2,10},{10... | collective-permute-start | bytes 1572872 | tf_op jit(solution)/shard_map/ppermute | solution.py:543
  943.8 13.6 %collective-permute-start.46 = (bf16[128,2048]{1,0:T(8,128)(2,1)}, bf16[128,2048]{1,0:T(8,128)(2,1)}, u32[]{:S(2)}, u32[]{:S(2)}) collective-permute-start(bf16[128,2048]{1,0:T(8,128)(2,1)} %collective-permute-done.44), channel_id=1, source_target_pairs={{0,8},{8,0},{16,24},{24,16},{1,9},{9,1},{17,25},{25,17},{2,10},{10... | collective-permute-start | bytes 1572872 | tf_op jit(solution)/shard_map/ppermute | solution.py:543
  962.3 31.9 %collective-permute-start.36 = (bf16[128,1280]{0,1:T(8,128)(2,1)S(1)}, bf16[128,1280]{0,1:T(8,128)(2,1)}, u32[]{:S(2)}, u32[]{:S(2)}) collective-permute-start(bf16[128,1280]{0,1:T(8,128)(2,1)S(1)} %copy.192), channel_id=1, source_target_pairs={{0,16},{16,0},{8,24},{24,8},{1,17},{17,1},{9,25},{25,9},{2,18},{18... | collective-permute-start | bytes 983048 | tf_op jit(solution)/shard_map/ppermute | solution.py:547
  964.1 37.1 %collective-permute-start.37 = (bf16[128,1280]{0,1:T(8,128)(2,1)S(1)}, bf16[128,1280]{0,1:T(8,128)(2,1)S(1)}, u32[]{:S(2)}, u32[]{:S(2)}) collective-permute-start(bf16[128,1280]{0,1:T(8,128)(2,1)S(1)} %copy.192), channel_id=1, source_target_pairs={{0,8},{8,0},{16,24},{24,16},{1,9},{9,1},{17,25},{25,17},{2,10},{10... | collective-permute-start | bytes 983048 | tf_op jit(solution)/shard_map/ppermute | solution.py:543
  992.9 6.7 collective-permute-start.33
  994.2 7.0 collective-permute-start.38
  999.5 8.3 collective-permute-start.34
  999.6 8.2 collective-permute-start.35
  (142 other events, 839.3 us)
Sparse Core Ops, SparseCore 0:
  11.4 82.7 all-gather.7
  104.7 51.8 all-gather.9
  159.3 47.3 all-gather.11
  244.6 44.3 all-gather.13
  631.2 85.6 reduce-scatter.7
  854.2 68.3 reduce-scatter.11
  926.0 65.6 reduce-scatter.9

commit v4 on v3

--- a/solution.py
+++ b/solution.py
@@ -952,24 +952,20 @@
             first.turn()
             grad_mixed = hold(grad_mixed, first)
             first.fetch()
-        if turn == 2:
-            if ranks == 4:
-                first.late()
-            grad_mixed = hold(grad_mixed, centre, memory_exchange)
-            centre_total = centre.end().astype(BF16)
-            encoded_grad = memory_exchange.end()
-            grad_mixed, centre_total = tie(grad_mixed, centre_total)
-            if ranks == 4:
-                side, partner = first.values
-                grad_mixed, partner = tie(grad_mixed, partner)
-                first.values = (side, swap(partner))
-            centre_piece = scatter(centre_total)
+        if turn == 2 and ranks == 4:
+            first.late()
+            side, partner = first.values
+            grad_mixed, partner = tie(grad_mixed, partner)
+            first.values = (side, swap(partner))
     joined = [jnp.concatenate(values, axis=1) for values in zip(*(back[step] for step in steps))]
     query_grad, rel_grad, own_key_grad, own_value_grad, key_grad, value_grad = joined
     if ranks == 4:
-        back[0][0] = hold(back[0][0], first)
+        back[0][0] = hold(back[0][0], first, centre, memory_exchange)
+        centre_total = centre.end().astype(BF16)
         first_total = first.end().astype(BF16)
-        key_grad, own_key_grad, first_total = tie(key_grad, own_key_grad, first_total)
+        key_grad, own_key_grad, first_total, centre_total = tie(
+            key_grad, own_key_grad, first_total, centre_total
+        )
     else:
         whole = column_part(
             ranks,
@@ -980,8 +976,10 @@
         )
         first = Exchange(ranks, whole)
         first.begin()
+        centre_total = centre.end().astype(BF16)
         first_total = first.end().astype(BF16)
-    first_piece = scatter(first_total)
+    last_piece = scatter(jnp.concatenate([centre_total, first_total], axis=1))
+    encoded_grad = memory_exchange.end()
 
     def reorder(weight):
         columns = weight.shape[1] // len(steps)
@@ -1024,16 +1022,16 @@
     w_outer_grad = jnp.concatenate(
         [columns_of(pieces, cut + layer * columns, columns) for layer in range(layers)], axis=0
     )
-    pieces = collect(ranks, centre_piece)
+    pieces = collect(ranks, last_piece)
     w_out_grad, c_query_grad, c_key_grad, c_value_grad, c_out_grad = (
         columns_of(pieces, start * columns, columns) for start in range(5)
     )
-    pieces = collect(ranks, first_piece)
     rel_columns = w_rel.shape[1] // ranks
-    w_query_grad = columns_of(pieces, 0, columns)
-    w_rel_grad = columns_of(pieces, columns, rel_columns)
-    w_key_grad = columns_of(pieces, columns + rel_columns, columns)
-    w_value_grad = columns_of(pieces, 2 * columns + rel_columns, columns)
+    start = 5 * columns
+    w_query_grad = columns_of(pieces, start, columns)
+    w_rel_grad = columns_of(pieces, start + columns, rel_columns)
+    w_key_grad = columns_of(pieces, start + columns + rel_columns, columns)
+    w_value_grad = columns_of(pieces, start + 2 * columns + rel_columns, columns)
     return (
         output,
         grad_hidden,

time: 1030 us -> 1020 us (level)
    unnamed x9 -> x7, waiting for transfers between devices: 27.6 us -> 4.04 us
    ppermute x14 -> x13, waiting for transfers between devices: 63.6 us -> 85 us  [pass_across(): return lax.ppermute(value, 'ctx', ACROSS)]
    unnamed x335 -> x365, local copies, waits for them, and re-layouts: 53.7 us -> 58.5 us
    ppermute x28 -> x26, starting transfers between devices: 24.2 us -> 24.9 us  [swap(): return lax.ppermute(value, 'ctx', PARTNER)]
  transfers between devices with their start and end apart: 54 -> 50, of which waited for: 10 -> 12; matrix products, arithmetic and copies ran while one was open for 42% -> 40% of each run, Pallas kernels for 27% -> 27%
where the time goes in v4:
time: 1020 us
  matrix products  367 us (36%)
  Pallas kernels  279 us (27%)
  waiting for transfers between devices  123 us (12%)
  local copies, waits for them, and re-layouts  97 us (10%)
  other arithmetic  88.9 us (9%)
  starting transfers between devices  40.7 us (4%)
  between operations  22 us (2%)
    dot_general x44, matrix products, dot_tn(): lax.dot_general(left, right, (((0,), (0,)), ((), ())), preferred_element_...  134 us
    dot_general x13, matrix products, dot_nn(): return jnp.dot(left, right, preferred_element_type=F32)  109 us
    dot_general x13, matrix products, dot_nt(): lax.dot_general(left, right, (((1,), (1,)), ((), ())), preferred_element_...  109 us
    pallas_call x4, Pallas kernels, self_backward(): pl.pallas_call(self_backward_kernel, grid_spec=pltpu.PrefetchScalarGridSp...  95.1 us
    ppermute x13, waiting for transfers between devices, pass_across(): return lax.ppermute(value, 'ctx', ACROSS)  85 us
    pallas_call x1, Pallas kernels, self_forward(): pl.pallas_call(self_forward_kernel, grid=(seqs, width // 256), in_specs=[...  76.4 us
    unnamed x365, local copies, waits for them, and re-layouts  58.5 us
    pallas_call x1, Pallas kernels, cross_backward(): pl.pallas_call(cross_backward_kernel, grid=(seqs, width // 256, streams),...  42 us
  transfers between devices with their start and end apart: 50, of which 12 were waited for; matrix products, arithmetic and copies ran while one was open for 40% of the time, Pallas kernels for 27%

profile of v4, /device:TPU:1, one launch (start us, length us, event | category | flops | bytes accessed | tf_op | source)
XLA Modules:
  0.0 1017.2 jit_solution(8378782861184595095)
XLA Ops:
  24.5 17.0 %collective-permute-done.1.third = bf16[2,256,1024]{2,1,0:T(8,128)(2,1)} collective-permute-done((bf16[2,256,1024]{2,1,0:T(8,128)(2,1)S(1)}, bf16[2,256,1024]{2,1,0:T(8,128)(2,1)}, u32[]{:S(2)}, u32[]{:S(2)}) %collective-permute-start.1) | collective-permute-done | bytes 1048608 | tf_op jit(solution)/shard_map/ppermute | solution.py:547
  52.0 7.2 collective-permute-done.4.third
  66.4 5.7 place.5
  72.0 9.0 convert_bitcast_fusion.1
  81.0 13.2 %all-gather.8.cloned.1.call-done = bf16[1024,3584]{1,0:T(8,128)(2,1)} async-done(((bf16[32,3584]{1,0:T(8,128)(2,1)}), bf16[1024,3584]{1,0:T(8,128)(2,1)}) %all-gather.8.cloned.1.call-update) | async-done | bytes 7340048 | tf_op jit(solution)/shard_map/all_gather | solution.py:539
  96.0 6.9 copy.147
  105.6 5.3 convolution_convert_fusion.8
  110.9 5.5 convolution_convert_fusion.11
  120.0 4.8 convolution_convert_fusion.5
  124.8 6.3 convolution_convert_fusion.6
  131.1 6.3 convolution_convert_fusion.7
  137.9 18.6 %all-gather.10.cloned.1.call-done = bf16[256,5248]{1,0:T(8,128)(2,1)} async-done(((bf16[32,5248]{1,0:T(8,128)(2,1)}), bf16[256,5248]{1,0:T(8,128)(2,1)}) %all-gather.10.cloned.1.call-update) | async-done | bytes 2686992 | tf_op jit(solution)/shard_map/all_gather | solution.py:592
  160.0 76.4 %self_forward.1 = (bf16[3,2,256,1024]{3,2,1,0:T(8,128)(2,1)}, bf16[2,8,8,192,1024]{4,3,2,1,0:T(8,128)(2,1)}, bf16[2,8,8,192,128]{4,3,2,1,0:T(8,128)(2,1)}) custom-call(s32[8]{0:T(128)} %copy-done.99, s32[1]{0:T(128)} %slice.311.own_ref, bf16[3,2,256,1024]{3,2,1,0:T(8,128)(2,1)} %bitcast.438, bf16[3,2,256,512]{3,2,1,0:T(8,128)(2,1)} %bitcast.489, ...), custom_call_target="tpu_custom_call" | custom-call | flops 88000004096 | bytes 80000000 | tf_op jit(solution)/shard_map/self_forward/pallas_call | solution.py:293
  245.4 8.5 place.7
  254.8 9.6 fusion.258
  269.0 5.4 convolution_convert_fusion.9
  274.4 5.5 convolution_convert_fusion.10
  282.9 6.4 convolution_convert_fusion.4
  292.8 33.6 %cross_forward.1 = (bf16[3,2,256,1024]{3,2,1,0:T(8,128)(2,1)}, bf16[3,2,8,512,512]{4,3,2,1,0:T(8,128)(2,1)}) custom-call(bf16[3,2,256,1024]{3,2,1,0:T(8,128)(2,1)} %bitcast.453, bf16[2,512,1024]{2,1,0:T(8,128)(2,1)} %bitcast.477, bf16[2,512,1024]{2,1,0:T(8,128)(2,1)} %bitcast.475), custom_call_target="tpu_custom_call" | custom-call | flops 38000001024 | bytes 40000000 | tf_op jit(solution)/shard_map/cross_forward/pallas_call | solution.py:463
  326.7 8.8 fusion.259
  341.9 7.0 place.8
  348.9 22.6 %multiply_convert_fusion.1 = (bf16[1536,4096]{1,0:T(8,128)(2,1)}, f32[1536,4096]{1,0:T(8,128)}) fusion(bf16[1536,1024]{1,0:T(8,128)(2,1)} %fusion.11, bf16[1024,4096]{1,0:T(8,128)(2,1)} %bitcast.318), kind=kOutput, calls=%fused_computation.7 | convolution fusion | flops 12916359168 | bytes 49283072 | tf_op jit(solution)/shard_map/dot_general | solution.py:29
  382.0 7.2 place.9
  389.2 19.3 %fusion.260 = (f32[1536]{0:T(1024)S(1)}, f32[1536,1024]{1,0:T(8,128)S(1)}) fusion(bf16[1536,4096]{1,0:T(8,128)(2,1)} %get-tuple-element.181, bf16[4096,1024]{1,0:T(8,128)(2,1)} %bitcast.320, f32[1024]{0:T(1024)S(1)} %bitcast.414, f32[1024]{0:T(1024)S(1)} %bitcast.407, f32[1536]{0:T(1024)S(1)} %add_rsqrt_fusion.1, f32[1536,1024]{1,0:T(8,128)} %copy-done.2, ...), kind=kOutput, calls=%fused_computation.433 | convolution fusion | flops 12894337024 | bytes 33581056 | tf_op jit(solution)/shard_map/dot_general | solution.py:29
  412.4 5.3 fusion.245
  419.4 9.8 convolution_convert_fusion
  429.1 9.9 convolution_convert_fusion.1
  442.6 25.7 %multiply_convert_fusion = bf16[1536,4096]{1,0:T(8,128)(2,1)} fusion(bf16[1536,1024]{1,0:T(8,128)(2,1)S(1)} %copy-done.31, bf16[4096,1024]{1,0:T(8,128)(2,1)S(1)} %bitcast.323, f32[1536,4096]{1,0:T(8,128)} %get-tuple-element.487), kind=kOutput, calls=%fused_computation.6 | convolution fusion | flops 12960399360 | bytes 49283072 | tf_op jit(solution)/shard_map/dot_general | solution.py:21
  468.3 7.2 fusion.42
  475.5 4.7 fusion.97
  480.2 4.7 fusion.94
  485.0 5.0 fusion.40
  490.0 6.5 fusion.12
  497.3 22.1 %multiply_reduce_fusion = (f32[1024]{0:T(1024)S(1)}, f32[1536]{0:T(1024)S(1)}, f32[1536]{0:T(1024)S(1)}, f32[1024]{0:T(1024)S(1)}, f32[1536,1024]{1,0:T(8,128)}) fusion(f32[1536,1024]{1,0:T(8,128)S(1)} %bitcast.290, f32[1536]{0:T(1024)S(1)} %add_rsqrt_fusion.1, f32[1536]{0:T(1024)S(1)} %broadcast_multiply_fusion.6, f32[1024]{0:T(1024)S(1)} %bitcast.408, ...), kind=kOutput, calls=%fused_computation.20 | convolution fusion | flops 12900625408 | bytes 39882752 | tf_op jit(solution)/shard_map/dot_general | solution.py:21
  519.4 5.9 fusion.244
  525.3 4.9 add_convert_fusion.6
  530.2 6.5 convolution_convert_fusion.3
  537.9 42.0 %cross_backward.1 = (bf16[3,2,256,1024]{3,2,1,0:T(8,128)(2,1)}, bf16[2,512,1024]{2,1,0:T(8,128)(2,1)}, bf16[2,512,1024]{2,1,0:T(8,128)(2,1)}) custom-call(bf16[3,2,256,1024]{3,2,1,0:T(8,128)(2,1)} %bitcast.454, bf16[2,512,1024]{2,1,0:T(8,128)(2,1)} %bitcast.478, bf16[2,512,1024]{2,1,0:T(8,128)(2,1)} %bitcast.476, ...), custom_call_target="tpu_custom_call" | custom-call | flops 46999998464 | bytes 50000000 | tf_op jit(solution)/shard_map/cross_backward/pallas_call | solution.py:481
  580.0 4.7 fusion.102
  584.7 4.1 add_convert_fusion.4
  590.6 11.6 %fusion.14 = bf16[4096,256]{1,0:T(8,128)(2,1)} fusion(bf16[1536,4096]{1,0:T(8,128)(2,1)} %get-tuple-element.181, bf16[4096,256]{1,0:T(8,128)(2,1)} %collective-permute-done.20, bf16[4096,256]{1,0:T(8,128)(2,1)} %collective-permute-done.16, bf16[1536,1024]{1,0:T(8,128)(2,1)} %copy-done.30, s32[]{:T(128)S(6)} %select_n.278), kind=kOutput, calls=%fused_computation.52 | convolution fusion | flops 3226468352 | bytes 19660804 | tf_op jit(solution)/shard_map/dot_general | solution.py:25
  605.1 7.8 multiply_reduce_fusion.1
  613.0 4.1 fusion.243
  631.2 4.2 convolution_dynamic-update-slice_fusion.1
  669.2 6.5 convolution_convert_fusion.2
  675.7 4.4 add_convert_fusion.3
  680.6 23.7 %self_backward.4 = (bf16[3,2,256,256]{3,2,1,0:T(8,128)(2,1)}, bf16[3,2,256,128]{3,2,1,0:T(8,128)(2,1)}, bf16[2,2,256,256]{3,2,1,0:T(8,128)(2,1)}, bf16[2,2,256,2...) custom-call(s32[1]{0:T(128)} %bitcast.69.group, s32[8]{0:T(128)} %copy-done.99, ...), custom_call_target="tpu_custom_call" | custom-call | flops 27000000512 | bytes 25000000 | tf_op jit(solution)/shard_map/self_backward/pallas_call | solution.py:346
  716.3 23.8 %self_backward.5 = (bf16[3,2,256,256]{3,2,1,0:T(8,128)(2,1)}, bf16[3,2,256,128]{3,2,1,0:T(8,128)(2,1)}, bf16[2,2,256,256]{3,2,1,0:T(8,128)(2,1)}, bf16[2,2,256,2...) custom-call(s32[1]{0:T(128)} %bitcast.79.group, s32[8]{0:T(128)} %copy-done.99, ...), custom_call_target="tpu_custom_call" | custom-call | flops 27000000512 | bytes 25000000 | tf_op jit(solution)/shard_map/self_backward/pallas_call | solution.py:346
  760.2 23.9 %self_backward.6 = (bf16[3,2,256,256]{3,2,1,0:T(8,128)(2,1)}, bf16[3,2,256,128]{3,2,1,0:T(8,128)(2,1)}, bf16[2,2,256,256]{3,2,1,0:T(8,128)(2,1)}, bf16[2,2,256,2...) custom-call(s32[1]{0:T(128)} %bitcast.89.group, s32[8]{0:T(128)} %copy-done.99, ...), custom_call_target="tpu_custom_call" | custom-call | flops 27000000512 | bytes 25000000 | tf_op jit(solution)/shard_map/self_backward/pallas_call | solution.py:346
  795.4 23.7 %self_backward.7 = (bf16[3,2,256,256]{3,2,1,0:T(8,128)(2,1)}, bf16[3,2,256,128]{3,2,1,0:T(8,128)(2,1)}, bf16[2,2,256,256]{3,2,1,0:T(8,128)(2,1)}, bf16[2,2,256,2...) custom-call(s32[1]{0:T(128)} %bitcast.3.rank.group, s32[8]{0:T(128)} %copy-done.99, ...), custom_call_target="tpu_custom_call" | custom-call | flops 27000000512 | bytes 25000000 | tf_op jit(solution)/shard_map/self_backward/pallas_call | solution.py:346
  835.7 28.1 %collective-permute-done.24 = bf16[1024,896]{0,1:T(8,128)(2,1)S(1)} collective-permute-done((bf16[1024,896]{0,1:T(8,128)(2,1)}, bf16[1024,896]{0,1:T(8,128)(2,1)S(1)}, u32[]{:S(2)}, u32[]{:S(2)}) %collective-permute-start.24) | collective-permute-done | bytes 1835040 | tf_op jit(solution)/shard_map/ppermute | solution.py:547
  866.5 4.2 add_convert_fusion.2
  873.2 6.7 copy.189
  881.7 5.3 fusion.32
  887.1 8.1 fusion.15
  895.3 7.1 add_convert_fusion
  902.5 5.4 fusion.50
  911.0 4.6 add_add_fusion
  920.5 4.3 fusion.91
  928.4 15.9 %collective-permute-done.32 = bf16[2,256,1024]{1,2,0:T(8,128)(2,1)} collective-permute-done((bf16[2,256,1024]{1,2,0:T(8,128)(2,1)S(1)}, bf16[2,256,1024]{1,2,0:T(8,128)(2,1)}, u32[]{:S(2)}, u32[]{:S(2)}) %collective-permute-start.32) | collective-permute-done | bytes 1048608 | tf_op jit(solution)/shard_map/ppermute | solution.py:547
  949.5 6.1 collective-permute-done.41
  956.4 6.7 fusion.6
  975.2 10.7 %collective-permute-done.33 = bf16[128,2176]{0,1:T(8,128)(2,1)S(1)} collective-permute-done((bf16[128,2176]{0,1:T(8,128)(2,1)}, bf16[128,2176]{0,1:T(8,128)(2,1)S(1)}, u32[]{:S(2)}, u32[]{:S(2)}) %collective-permute-start.33) | collective-permute-done | bytes 557088 | tf_op jit(solution)/shard_map/ppermute | solution.py:547
  987.7 4.5 maximum_maximum_fusion
  (621 shorter events, 258.5 us)
Async XLA Ops:
  7.2 97.7 %copy-start = (bf16[128,4096]{1,0:T(8,128)(2,1)S(1)}, bf16[128,4096]{1,0:T(8,128)(2,1)}, u32[]{:S(2)}) copy-start(bf16[128,4096]{1,0:T(8,128)(2,1)} %param.43) | copy-start | bytes 3145732
  7.2 87.0 %all-gather.8.cloned.1.call-start = ((), (), s32[]{:S(2)}) async-start(), calls=%async_computation.2 | async-start | bytes 7569408 | tf_op jit(solution)/shard_map/all_gather | solution.py:539
  10.3 146.3 %all-gather.10.cloned.1.call-start = ((), (), s32[]{:S(2)}) async-start(), calls=%async_computation.4 | async-start | bytes 3022848 | tf_op jit(solution)/shard_map/all_gather | solution.py:592
  14.7 35.7 %copy-start.100 = (s32[1055]{0:T(1024)S(1)}, s32[1055]{0:T(1024)}, u32[]{:S(2)}) copy-start(s32[1055]{0:T(1024)} %param.29) | copy-start | bytes 12664
  14.7 45.8 %copy-start.10 = (bf16[2,256,1024]{2,1,0:T(8,128)(2,1)}, bf16[2,256,1024]{2,1,0:T(8,128)(2,1)S(1)}, u32[]{:S(2)}) copy-start(bf16[2,256,1024]{2,1,0:T(8,128)(2,1)S(1)} %slice_bitcast_fusion.first) | copy-start | bytes 3145732
  14.7 26.7 %collective-permute-start.1 = (bf16[2,256,1024]{2,1,0:T(8,128)(2,1)S(1)}, bf16[2,256,1024]{2,1,0:T(8,128)(2,1)}, u32[]{:S(2)}, u32[]{:S(2)}) collective-permute-start(bf16[2,256,1024]{2,1,0:T(8,128)(2,1)S(1)} %slice_bitcast_fusion.first), channel_id=1, source_target_pairs={{0,16},{16,0},{8,24},{24,8},{1,17},{17,1},{9,25},{25,9},{2,18},{18... | collective-permute-start | bytes 3145736 | tf_op jit(solution)/shard_map/ppermute | solution.py:547
  16.8 49.5 %collective-permute-start = (bf16[2,256,1024]{2,1,0:T(8,128)(2,1)S(1)}, bf16[2,256,1024]{2,1,0:T(8,128)(2,1)}, u32[]{:S(2)}, u32[]{:S(2)}) collective-permute-start(bf16[2,256,1024]{2,1,0:T(8,128)(2,1)S(1)} %slice_bitcast_fusion.first), channel_id=1, source_target_pairs={{0,8},{8,0},{16,24},{24,16},{1,9},{9,1},{17,25},{25,17},{2,10},{10... | collective-permute-start | bytes 3145736 | tf_op jit(solution)/shard_map/ppermute | solution.py:543
  17.8 41.4 %collective-permute-start.4 = (bf16[2,128,1024]{2,1,0:T(8,128)(2,1)S(1)}, bf16[2,128,1024]{2,1,0:T(8,128)(2,1)}, u32[]{:S(2)}, u32[]{:S(2)}) collective-permute-start(bf16[2,128,1024]{2,1,0:T(8,128)(2,1)S(1)} %copy-done.57), channel_id=1, source_target_pairs={{0,16},{16,0},{8,24},{24,8},{1,17},{17,1},{9,25},{25,9},{2,18},{18... | collective-permute-start | bytes 1572872 | tf_op jit(solution)/shard_map/ppermute | solution.py:547
  17.8 43.1 %collective-permute-start.3 = (bf16[2,128,1024]{2,1,0:T(8,128)(2,1)S(1)}, bf16[2,128,1024]{2,1,0:T(8,128)(2,1)}, u32[]{:S(2)}, u32[]{:S(2)}) collective-permute-start(bf16[2,128,1024]{2,1,0:T(8,128)(2,1)S(1)} %copy-done.57), channel_id=1, source_target_pairs={{0,8},{8,0},{16,24},{24,16},{1,9},{9,1},{17,25},{25,17},{2,10},{10... | collective-permute-start | bytes 1572872 | tf_op jit(solution)/shard_map/ppermute | solution.py:543
  19.0 41.9 %copy-start.99 = (s32[8]{0:T(128)}, s32[8]{0:T(128)S(1)}, u32[]{:S(2)}) copy-start(s32[8]{0:T(128)S(1)} %dynamic_slice.199.blocks) | copy-start | bytes 100
  41.4 24.9 %collective-permute-start.2 = (bf16[2,256,1024]{2,1,0:T(8,128)(2,1)}, bf16[2,256,1024]{2,1,0:T(8,128)(2,1)}, u32[]{:S(2)}, u32[]{:S(2)}) collective-permute-start(bf16[2,256,1024]{2,1,0:T(8,128)(2,1)} %collective-permute-done.1.third), channel_id=1, source_target_pairs={{0,8},{8,0},{16,24},{24,16},{1,9},{9,1},{17,25},{25,17},{2,10},{10... | collective-permute-start | bytes 3145736 | tf_op jit(solution)/shard_map/ppermute | solution.py:543
  59.2 3.0 collective-permute-start.5
  104.6 131.9 %all-gather.12.cloned.1.call-start = ((), (), s32[]{:S(2)}) async-start(), calls=%async_computation.5 | async-start | bytes 2359296 | tf_op jit(solution)/shard_map/all_gather | solution.py:592
  137.4 151.9 %all-gather.14.cloned.1.call-start = ((), (), s32[]{:S(2)}) async-start(), calls=%async_computation.6 | async-start | bytes 2359296 | tf_op jit(solution)/shard_map/all_gather | solution.py:592
  156.6 79.9 %collective-permute-start.6 = (bf16[8,32,5248]{2,1,0:T(8,128)(2,1)}, bf16[8,32,5248]{2,1,0:T(8,128)(2,1)}, u32[]{:S(2)}, u32[]{:S(2)}) collective-permute-start(bf16[8,32,5248]{2,1,0:T(8,128)(2,1)} %bitcast.341), channel_id=1, source_target_pairs={{0,8},{8,0},{16,24},{24,16},{1,9},{9,1},{17,25},{25,17},{2,10},{10... | collective-permute-start | bytes 8060936 | tf_op jit(solution)/shard_map/ppermute | solution.py:543
  158.8 77.6 %collective-permute-start.7 = (bf16[8,32,5248]{2,1,0:T(8,128)(2,1)}, bf16[8,32,5248]{2,1,0:T(8,128)(2,1)}, u32[]{:S(2)}, u32[]{:S(2)}) collective-permute-start(bf16[8,32,5248]{2,1,0:T(8,128)(2,1)} %bitcast.342), channel_id=1, source_target_pairs={{0,16},{16,0},{8,24},{24,8},{1,17},{17,1},{9,25},{25,9},{2,18},{18... | collective-permute-start | bytes 8060936 | tf_op jit(solution)/shard_map/ppermute | solution.py:547
  236.5 8.9 collective-permute-start.8
  244.5 680.3 %reduce-scatter.5.cloned.1.call-start = ((), (), s32[]{:S(2)}) async-start(), calls=%async_computation.3 | async-start | bytes 4718592 | tf_op jit(solution)/shard_map/reduce_scatter | solution.py:686
  244.6 81.8 %collective-permute-start.10 = (bf16[8,32,4096]{2,1,0:T(8,128)(2,1)S(1)}, bf16[8,32,4096]{2,1,0:T(8,128)(2,1)}, u32[]{:S(2)}, u32[]{:S(2)}) collective-permute-start(bf16[8,32,4096]{2,1,0:T(8,128)(2,1)S(1)} %bitcast.345), channel_id=1, source_target_pairs={{0,16},{16,0},{8,24},{24,8},{1,17},{17,1},{9,25},{25,9},{2,18},{18... | collective-permute-start | bytes 6291464 | tf_op jit(solution)/shard_map/ppermute | solution.py:547
  244.7 81.7 %collective-permute-start.9 = (bf16[8,32,4096]{2,1,0:T(8,128)(2,1)S(1)}, bf16[8,32,4096]{2,1,0:T(8,128)(2,1)}, u32[]{:S(2)}, u32[]{:S(2)}) collective-permute-start(bf16[8,32,4096]{2,1,0:T(8,128)(2,1)S(1)} %bitcast.346), channel_id=1, source_target_pairs={{0,8},{8,0},{16,24},{24,16},{1,9},{9,1},{17,25},{25,17},{2,10},{10... | collective-permute-start | bytes 6291464 | tf_op jit(solution)/shard_map/ppermute | solution.py:543
  264.5 62.2 %copy-start.93 = (f32[1536]{0:T(1024)}, f32[1536]{0:T(1024)S(1)}, u32[]{:S(2)}) copy-start(f32[1536]{0:T(1024)S(1)} %broadcast_multiply_fusion.7) | copy-start | bytes 18436
  268.4 58.4 %copy-start.95 = (f32[1536]{0:T(1024)}, f32[1536]{0:T(1024)S(1)}, u32[]{:S(2)}) copy-start(f32[1536]{0:T(1024)S(1)} %add_rsqrt_fusion.2) | copy-start | bytes 18436
  269.0 57.7 %copy-start.97 = (f32[1,1024]{1,0:T(1,128)}, f32[1,1024]{1,0:T(1,128)S(1)}, u32[]{:S(2)}) copy-start(f32[1,1024]{1,0:T(1,128)S(1)} %get-tuple-element.467) | copy-start | bytes 12292
  289.3 82.3 %collective-permute-start.12 = (bf16[8,128,1024]{2,1,0:T(8,128)(2,1)}, bf16[8,128,1024]{2,1,0:T(8,128)(2,1)}, u32[]{:S(2)}, u32[]{:S(2)}) collective-permute-start(bf16[8,128,1024]{2,1,0:T(8,128)(2,1)} %bitcast.347), channel_id=1, source_target_pairs={{0,8},{8,0},{16,24},{24,16},{1,9},{9,1},{17,25},{25,17},{2,10},{10... | collective-permute-start | bytes 6291464 | tf_op jit(solution)/shard_map/ppermute | solution.py:543
  291.6 80.0 %collective-permute-start.13 = (bf16[8,128,1024]{2,1,0:T(8,128)(2,1)}, bf16[8,128,1024]{2,1,0:T(8,128)(2,1)}, u32[]{:S(2)}, u32[]{:S(2)}) collective-permute-start(bf16[8,128,1024]{2,1,0:T(8,128)(2,1)} %bitcast.348), channel_id=1, source_target_pairs={{0,16},{16,0},{8,24},{24,8},{1,17},{17,1},{9,25},{25,9},{2,18},{18... | collective-permute-start | bytes 6291464 | tf_op jit(solution)/shard_map/ppermute | solution.py:547
  326.4 14.2 %collective-permute-start.11 = (bf16[8,32,4096]{2,1,0:T(8,128)(2,1)}, bf16[8,32,4096]{2,1,0:T(8,128)(2,1)S(1)}, u32[]{:S(2)}, u32[]{:S(2)}) collective-permute-start(bf16[8,32,4096]{2,1,0:T(8,128)(2,1)} %collective-permute-done.10.third), channel_id=1, source_target_pairs={{0,8},{8,0},{16,24},{24,16},{1,9},{9,1},{17,25},{25,17},{2,10},{10... | collective-permute-start | bytes 6291464 | tf_op jit(solution)/shard_map/ppermute | solution.py:543
  348.9 25.0 %slice-start.14 = ((s8[7340032]{0:T(1024)(128)(4,1)}), s8[4194304]{0:T(1024)(128)(4,1)S(1)}, s32[]{:S(2)}) async-start(s8[7340032]{0:T(1024)(128)(4,1)} %bitcast.326), calls=%async_computation.22 | async-start | bytes 8388608
  348.9 22.9 %copy-start.101 = (s32[1055]{0:T(1024)S(1)}, s32[1055]{0:T(1024)}, u32[]{:S(2)}) copy-start(s32[1055]{0:T(1024)} %param.29) | copy-start | bytes 12664
  348.9 25.0 %slice-start.15 = ((s8[7340032]{0:T(1024)(128)(4,1)}), s8[3145728]{0:T(1024)(128)(4,1)S(1)}, s32[]{:S(2)}) async-start(s8[7340032]{0:T(1024)(128)(4,1)} %bitcast.326), calls=%async_computation.23 | async-start | bytes 6291456
  371.6 10.4 %collective-permute-start.14 = (bf16[8,128,1024]{2,1,0:T(8,128)(2,1)}, bf16[8,128,1024]{2,1,0:T(8,128)(2,1)}, u32[]{:S(2)}, u32[]{:S(2)}) collective-permute-start(bf16[8,128,1024]{2,1,0:T(8,128)(2,1)} %collective-permute-done.13.third), channel_id=1, source_target_pairs={{0,8},{8,0},{16,24},{24,16},{1,9},{9,1},{17,25},{25,17},{2,10},{10... | collective-permute-start | bytes 6291464 | tf_op jit(solution)/shard_map/ppermute | solution.py:543
  381.9 27.3 %slice-start = ((s8[6291456]{0:T(1024)(128)(4,1)}), s8[2097152]{0:T(1024)(128)(4,1)S(1)}, s32[]{:S(2)}) async-start(s8[6291456]{0:T(1024)(128)(4,1)} %bitcast.283), calls=%async_computation.8 | async-start | bytes 4194304
  439.1 50.9 %collective-permute-start.15 = (bf16[4096,256]{1,0:T(8,128)(2,1)}, bf16[4096,256]{1,0:T(8,128)(2,1)}, u32[]{:S(2)}, u32[]{:S(2)}) collective-permute-start(bf16[4096,256]{1,0:T(8,128)(2,1)} %convolution_convert_fusion.1), channel_id=1, source_target_pairs={{0,8},{8,0},{16,24},{24,16},{1,9},{9,1},{17,25},{25,17},{2,10},{10... | collective-permute-start | bytes 6291464 | tf_op jit(solution)/shard_map/ppermute | solution.py:543
  439.3 57.2 %collective-permute-start.16 = (bf16[4096,256]{1,0:T(8,128)(2,1)}, bf16[4096,256]{1,0:T(8,128)(2,1)}, u32[]{:S(2)}, u32[]{:S(2)}) collective-permute-start(bf16[4096,256]{1,0:T(8,128)(2,1)} %convolution_convert_fusion), channel_id=1, source_target_pairs={{0,8},{8,0},{16,24},{24,16},{1,9},{9,1},{17,25},{25,17},{2,10},{10... | collective-permute-start | bytes 6291464 | tf_op jit(solution)/shard_map/ppermute | solution.py:543
  442.6 25.7 %copy-start.28 = (bf16[1536,1024]{1,0:T(8,128)(2,1)S(1)}, bf16[1536,1024]{1,0:T(8,128)(2,1)}, u32[]{:S(2)}) copy-start(bf16[1536,1024]{1,0:T(8,128)(2,1)} %fusion.11) | copy-start | bytes 9437188
  496.5 28.8 %collective-permute-start.17 = (bf16[1024,1024]{1,0:T(8,128)(2,1)}, bf16[1024,1024]{1,0:T(8,128)(2,1)}, u32[]{:S(2)}, u32[]{:S(2)}) collective-permute-start(bf16[1024,1024]{1,0:T(8,128)(2,1)} %fusion.94), channel_id=1, source_target_pairs={{0,8},{8,0},{16,24},{24,16},{1,9},{9,1},{17,25},{25,17},{2,10},{10... | collective-permute-start | bytes 6291464 | tf_op jit(solution)/shard_map/ppermute | solution.py:543
  496.8 33.4 %collective-permute-start.18 = (bf16[1024,1024]{1,0:T(8,128)(2,1)}, bf16[1024,1024]{1,0:T(8,128)(2,1)}, u32[]{:S(2)}, u32[]{:S(2)}) collective-permute-start(bf16[1024,1024]{1,0:T(8,128)(2,1)} %fusion.97), channel_id=1, source_target_pairs={{0,8},{8,0},{16,24},{24,16},{1,9},{9,1},{17,25},{25,17},{2,10},{10... | collective-permute-start | bytes 6291464 | tf_op jit(solution)/shard_map/ppermute | solution.py:543
  497.0 93.0 %collective-permute-start.20 = (bf16[4096,256]{1,0:T(8,128)(2,1)}, bf16[4096,256]{1,0:T(8,128)(2,1)}, u32[]{:S(2)}, u32[]{:S(2)}) collective-permute-start(bf16[4096,256]{1,0:T(8,128)(2,1)} %fusion.12), channel_id=1, source_target_pairs={{0,16},{16,0},{8,24},{24,8},{1,17},{17,1},{9,25},{25,9},{2,18},{18... | collective-permute-start | bytes 6291464 | tf_op jit(solution)/shard_map/ppermute | solution.py:547
  536.7 53.3 %collective-permute-start.19 = (bf16[1024,1024]{1,0:T(8,128)(2,1)}, bf16[1024,1024]{1,0:T(8,128)(2,1)S(1)}, u32[]{:S(2)}, u32[]{:S(2)}) collective-permute-start(bf16[1024,1024]{1,0:T(8,128)(2,1)} %add_convert_fusion.6), channel_id=1, source_target_pairs={{0,16},{16,0},{8,24},{24,8},{1,17},{17,1},{9,25},{25,9},{2,18},{18... | collective-permute-start | bytes 6291464 | tf_op jit(solution)/shard_map/ppermute | solution.py:547
  630.9 339.4 %reduce-scatter.7.cloned.1.call-start = ((), (), s32[]{:S(2)}) async-start(), calls=%async_computation.7 | async-start | bytes 5013504
  646.1 34.0 %collective-permute-start.22 = (bf16[1024,1280]{0,1:T(8,128)(2,1)}, bf16[1024,1280]{0,1:T(8,128)(2,1)}, u32[]{:S(2)}, u32[]{:S(2)}) collective-permute-start(bf16[1024,1280]{0,1:T(8,128)(2,1)} %fusion.134), channel_id=1, source_target_pairs={{0,8},{8,0},{16,24},{24,16},{1,9},{9,1},{17,25},{25,17},{2,10},{10... | collective-permute-start | bytes 7864328 | tf_op jit(solution)/shard_map/ppermute | solution.py:543
  653.7 22.0 %collective-permute-start.21 = (bf16[1024,1280]{0,1:T(8,128)(2,1)}, bf16[1024,1280]{0,1:T(8,128)(2,1)}, u32[]{:S(2)}, u32[]{:S(2)}) collective-permute-start(bf16[1024,1280]{0,1:T(8,128)(2,1)} %fusion.137), channel_id=1, source_target_pairs={{0,8},{8,0},{16,24},{24,16},{1,9},{9,1},{17,25},{25,17},{2,10},{10... | collective-permute-start | bytes 7864328 | tf_op jit(solution)/shard_map/ppermute | solution.py:543
  680.1 75.0 %collective-permute-start.27 = (bf16[2,128,1024]{2,1,0:T(8,128)(2,1)}, bf16[2,128,1024]{2,1,0:T(8,128)(2,1)}, u32[]{:S(2)}, u32[]{:S(2)}) collective-permute-start(bf16[2,128,1024]{2,1,0:T(8,128)(2,1)} %get-tuple-element.260), channel_id=1, source_target_pairs={{0,8},{8,0},{16,24},{24,16},{1,9},{9,1},{17,25},{25,17},{2,10},{10... | collective-permute-start | bytes 1572872 | tf_op jit(solution)/shard_map/ppermute | solution.py:543
  716.1 24.1 %collective-permute-start.36 = (f32[6,1024]{1,0:T(8,128)S(1)}, f32[6,1024]{1,0:T(8,128)S(1)}, u32[]{:S(2)}, u32[]{:S(2)}) collective-permute-start(f32[6,1024]{1,0:T(8,128)S(1)} %stack.55), channel_id=1, source_target_pairs={{0,8},{8,0},{16,24},{24,16},{1,9},{9,1},{17,25},{25,17},{2,10},{10... | collective-permute-start | bytes 73736 | tf_op jit(solution)/shard_map/ppermute | solution.py:711
  740.1 4.2 collective-permute-start.37
  743.5 14.7 %collective-permute-start.23 = (bf16[1024,896]{0,1:T(8,128)(2,1)S(1)}, bf16[1024,896]{0,1:T(8,128)(2,1)S(1)}, u32[]{:S(2)}, u32[]{:S(2)}) collective-permute-start(bf16[1024,896]{0,1:T(8,128)(2,1)S(1)} %copy-done.45), channel_id=1, source_target_pairs={{0,8},{8,0},{16,24},{24,16},{1,9},{9,1},{17,25},{25,17},{2,10},{10... | collective-permute-start | bytes 5505032 | tf_op jit(solution)/shard_map/ppermute | solution.py:543
  744.4 2.8 collective-permute-start.38
  745.5 90.1 %collective-permute-start.26 = (bf16[1024,1280]{0,1:T(8,128)(2,1)S(1)}, bf16[1024,1280]{0,1:T(8,128)(2,1)}, u32[]{:S(2)}, u32[]{:S(2)}) collective-permute-start(bf16[1024,1280]{0,1:T(8,128)(2,1)S(1)} %add_convert_fusion.3), channel_id=1, source_target_pairs={{0,16},{16,0},{8,24},{24,8},{1,17},{17,1},{9,25},{25,9},{2,18},{18... | collective-permute-start | bytes 7864328 | tf_op jit(solution)/shard_map/ppermute | solution.py:547
  746.4 89.2 %collective-permute-start.29 = (bf16[2,128,1024]{2,1,0:T(8,128)(2,1)}, bf16[2,128,1024]{2,1,0:T(8,128)(2,1)}, u32[]{:S(2)}, u32[]{:S(2)}) collective-permute-start(bf16[2,128,1024]{2,1,0:T(8,128)(2,1)} %get-tuple-element.261), channel_id=1, source_target_pairs={{0,8},{8,0},{16,24},{24,16},{1,9},{9,1},{17,25},{25,17},{2,10},{10... | collective-permute-start | bytes 1572872 | tf_op jit(solution)/shard_map/ppermute | solution.py:543
  747.2 3.2 collective-permute-start.39
  750.4 4.2 collective-permute-start.40
  757.3 78.3 %collective-permute-start.28 = (bf16[2,128,1024]{2,1,0:T(8,128)(2,1)}, bf16[2,128,1024]{2,1,0:T(8,128)(2,1)}, u32[]{:S(2)}, u32[]{:S(2)}) collective-permute-start(bf16[2,128,1024]{2,1,0:T(8,128)(2,1)} %add_convert_fusion.9), channel_id=1, source_target_pairs={{0,16},{16,0},{8,24},{24,8},{1,17},{17,1},{9,25},{25,9},{2,18},{18... | collective-permute-start | bytes 1572872 | tf_op jit(solution)/shard_map/ppermute | solution.py:547
  819.2 16.5 %collective-permute-start.25 = (bf16[1024,896]{0,1:T(8,128)(2,1)}, bf16[1024,896]{0,1:T(8,128)(2,1)S(1)}, u32[]{:S(2)}, u32[]{:S(2)}) collective-permute-start(bf16[1024,896]{0,1:T(8,128)(2,1)} %pad_maximum_fusion.7), channel_id=1, source_target_pairs={{0,8},{8,0},{16,24},{24,16},{1,9},{9,1},{17,25},{25,17},{2,10},{10... | collective-permute-start | bytes 5505032 | tf_op jit(solution)/shard_map/ppermute | solution.py:543
  822.1 41.7 %collective-permute-start.24 = (bf16[1024,896]{0,1:T(8,128)(2,1)}, bf16[1024,896]{0,1:T(8,128)(2,1)S(1)}, u32[]{:S(2)}, u32[]{:S(2)}) collective-permute-start(bf16[1024,896]{0,1:T(8,128)(2,1)} %fusion.29), channel_id=1, source_target_pairs={{0,16},{16,0},{8,24},{24,8},{1,17},{17,1},{9,25},{25,9},{2,18},{18... | collective-permute-start | bytes 5505032 | tf_op jit(solution)/shard_map/ppermute | solution.py:547
  833.2 30.6 %copy-start.8 = (bf16[2,256,3,1024]{3,1,0,2:T(8,128)(2,1)S(1)}, bf16[2,256,3,1024]{3,1,0,2:T(8,128)(2,1)}, u32[]{:S(2)}) copy-start(bf16[2,256,3,1024]{3,1,0,2:T(8,128)(2,1)} %copy-done.3) | copy-start | bytes 9437188
  833.2 30.6 %copy-start.134 = (bf16[3,2,256,256]{3,2,1,0:T(8,128)(2,1)S(1)}, bf16[3,2,256,256]{3,2,1,0:T(8,128)(2,1)}, u32[]{:S(2)}) copy-start(bf16[3,2,256,256]{3,2,1,0:T(8,128)(2,1)} %get-tuple-element.252) | copy-start | bytes 2359300
  908.3 10.7 %collective-permute-start.31 = (bf16[2,256,1024]{1,2,0:T(8,128)(2,1)S(1)}, bf16[2,256,1024]{1,2,0:T(8,128)(2,1)S(1)}, u32[]{:S(2)}, u32[]{:S(2)}) collective-permute-start(bf16[2,256,1024]{1,2,0:T(8,128)(2,1)S(1)} %get-tuple-element.381), channel_id=1, source_target_pairs={{0,8},{8,0},{16,24},{24,16},{1,9},{9,1},{17,25},{25,17},{2,10},{10... | collective-permute-start | bytes 3145736 | tf_op jit(solution)/shard_map/ppermute | solution.py:543
  915.6 12.8 %collective-permute-start.30 = (bf16[2,256,1024]{1,2,0:T(8,128)(2,1)S(1)}, bf16[2,256,1024]{1,2,0:T(8,128)(2,1)S(1)}, u32[]{:S(2)}, u32[]{:S(2)}) collective-permute-start(bf16[2,256,1024]{1,2,0:T(8,128)(2,1)S(1)} %get-tuple-element.380), channel_id=1, source_target_pairs={{0,8},{8,0},{16,24},{24,16},{1,9},{9,1},{17,25},{25,17},{2,10},{10... | collective-permute-start | bytes 3145736 | tf_op jit(solution)/shard_map/ppermute | solution.py:543
  919.4 24.9 %collective-permute-start.32 = (bf16[2,256,1024]{1,2,0:T(8,128)(2,1)S(1)}, bf16[2,256,1024]{1,2,0:T(8,128)(2,1)}, u32[]{:S(2)}, u32[]{:S(2)}) collective-permute-start(bf16[2,256,1024]{1,2,0:T(8,128)(2,1)S(1)} %fusion.84), channel_id=1, source_target_pairs={{0,16},{16,0},{8,24},{24,8},{1,17},{17,1},{9,25},{25,9},{2,18},{18... | collective-permute-start | bytes 3145736 | tf_op jit(solution)/shard_map/ppermute | solution.py:547
  924.8 30.8 %collective-permute-start.41 = (bf16[128,2048]{1,0:T(8,128)(2,1)}, bf16[128,2048]{1,0:T(8,128)(2,1)}, u32[]{:S(2)}, u32[]{:S(2)}) collective-permute-start(bf16[128,2048]{1,0:T(8,128)(2,1)} %reduce-scatter.5.cloned.1.call-done), channel_id=1, source_target_pairs={{0,16},{16,0},{8,24},{24,8},{1,17},{17,1},{9,25},{25,9},{2,18},{18... | collective-permute-start | bytes 1572872 | tf_op jit(solution)/shard_map/ppermute | solution.py:547
  928.0 35.1 %collective-permute-start.42 = (bf16[128,2048]{1,0:T(8,128)(2,1)}, bf16[128,2048]{1,0:T(8,128)(2,1)}, u32[]{:S(2)}, u32[]{:S(2)}) collective-permute-start(bf16[128,2048]{1,0:T(8,128)(2,1)} %reduce-scatter.5.cloned.1.call-done), channel_id=1, source_target_pairs={{0,8},{8,0},{16,24},{24,16},{1,9},{9,1},{17,25},{25,17},{2,10},{10... | collective-permute-start | bytes 1572872 | tf_op jit(solution)/shard_map/ppermute | solution.py:543
  955.6 7.6 collective-permute-start.43
  972.5 13.4 %collective-permute-start.33 = (bf16[128,2176]{0,1:T(8,128)(2,1)}, bf16[128,2176]{0,1:T(8,128)(2,1)S(1)}, u32[]{:S(2)}, u32[]{:S(2)}) collective-permute-start(bf16[128,2176]{0,1:T(8,128)(2,1)} %copy.190), channel_id=1, source_target_pairs={{0,16},{16,0},{8,24},{24,8},{1,17},{17,1},{9,25},{25,9},{2,18},{18... | collective-permute-start | bytes 1671176 | tf_op jit(solution)/shard_map/ppermute | solution.py:547
  973.8 20.1 %collective-permute-start.34 = (bf16[128,2176]{0,1:T(8,128)(2,1)S(1)}, bf16[128,2176]{0,1:T(8,128)(2,1)S(1)}, u32[]{:S(2)}, u32[]{:S(2)}) collective-permute-start(bf16[128,2176]{0,1:T(8,128)(2,1)S(1)} %copy-done.32), channel_id=1, source_target_pairs={{0,8},{8,0},{16,24},{24,16},{1,9},{9,1},{17,25},{25,17},{2,10},{10... | collective-permute-start | bytes 1671176 | tf_op jit(solution)/shard_map/ppermute | solution.py:543
  985.9 8.1 collective-permute-start.35
  (154 other events, 819.9 us)
Sparse Core Ops, SparseCore 0:
  11.4 82.7 all-gather.7
  104.7 51.8 all-gather.9
  159.3 47.3 all-gather.11
  244.6 44.3 all-gather.13
  631.1 85.7 reduce-scatter.4
  880.1 90.2 reduce-scatter.6
